TPU v7x, 128 devices: a whole 4x4x4 slice. The times are simulated.
128 devices in a mesh: seq: 2 (over x_lo), fsdp: 64 (over y, z, x_hi, core).
Axes of the slice: x: 4 (x_hi: 2, x_lo: 2; x = x_hi * 2 + x_lo), y: 4, z: 4, core: 2. Of those that a mesh axis runs over, the one named last changes fastest.
Arguments:
- inputs: bfloat16 [64, 256, 1024], P('fsdp', 'seq'), may hold values from -8 to 8
- project_in: bfloat16 [1024, 2048], P('fsdp'), may hold values from -0.25 to 0.25
- project_out: bfloat16 [1024, 1024], P('fsdp'), may hold values from -0.75 to 0.75
- gain_attend: bfloat16 [1024], P('fsdp'), may hold values from 0.25 to 1.75
- gain_expert: bfloat16 [1024], P('fsdp'), may hold values from 0.25 to 1.75
- expert_gate: bfloat16 [16384, 1024], P('fsdp'), may hold values from -0.1875 to 0.1875
- expert_up: bfloat16 [16384, 1024], P('fsdp'), may hold values from -0.1875 to 0.1875
- expert_down: bfloat16 [16384, 1024], P('fsdp'), may hold values from -0.25 to 0.25
- routes: int32 [64, 256, 8], P('fsdp', 'seq'), may hold values from 0 to 31, all different within a row; in each aligned block of 128 rows (0 to 127, 128 to 255, ..., all dimensions but the last counted through in order) at most 36 rows name the same one
- route_weights: float32 [64, 256, 8], P('fsdp', 'seq'), may hold values from 0.03 to 0.4
- segments: int32 [64, 256], P('fsdp'), may hold values from 0 to 3, never falling along the last dimension, each value on 1 to 128 neighbouring positions
- cotangent: bfloat16 [64, 256, 1024], P('fsdp', 'seq'), may hold values from -6 to 6
Outputs:
- output: bfloat16 [64, 256, 1024], P('fsdp', 'seq')
- grad_inputs: bfloat16 [64, 256, 1024], P('fsdp', 'seq')
- grad_project_in: float32 [1024, 2048], P('fsdp')
- grad_project_out: float32 [1024, 1024], P('fsdp')
- grad_gain_attend: float32 [1024], P('fsdp')
- grad_gain_expert: float32 [1024], P('fsdp')
- grad_expert_gate: float32 [16384, 1024], P('fsdp')
- grad_expert_up: float32 [16384, 1024], P('fsdp')
- grad_expert_down: float32 [16384, 1024], P('fsdp')
Inputs may be any that keep to these rules, and one draw needn't show every extreme that they name: `routes`: each token names 8 different experts. In each aligned block of 128 tokens (the tokens of one device) no expert is named by more than 36 tokens, a bound that some block reaches. `segments`: never falling along a sequence; each document spans 1 to 128 positions, one exactly 128.
All inputs are finite; a program needn't handle non-finite values.
Results may differ from a plain program's by a relative error of at most 0.014.
The roundings to bfloat16 on the way count: a program that leaves them out, or rounds other values in their place, can miss the bound.
Values may be sent and summed in bfloat16 or wider, within the bound.
A program may use at most 128 MiB of HBM per device.

v0:
```python
import math

import jax
import jax.numpy as jnp
from jax import lax
from jax.sharding import PartitionSpec as P

HEADS = 16
KV_HEADS = 8
HEAD_DIM = 64
EXPERTS = 32
FF = 512
TOP = 8
CAP = 36


EPSILON = 1e-06
ROPE_BASE = 10000.0
block_limit = 512


def sent_together(arrays, axis, dim, along):
    widths = [math.prod(a.shape[along:]) for a in arrays]
    both = jnp.concatenate(
        [a.reshape(*a.shape[:along], w) for a, w in zip(arrays, widths)], axis=along
    )
    whole = lax.all_gather(both, axis, axis=dim, tiled=True)
    pieces = jnp.split(whole, [sum(widths[:k]) for k in range(1, len(widths))], axis=along)
    return tuple(
        (b.reshape(*whole.shape[:along], *a.shape[along:]) for a, b in zip(arrays, pieces))
    )


def cut_along(value, dim, devices):
    dims = value.shape
    pieces = value.reshape(*dims[:dim], devices, dims[dim] // devices, *dims[dim + 1 :])
    return jnp.moveaxis(pieces, dim, 0)


def edges_of(length, count):
    unit = 8 if length >= 8 * count else 1
    return [length // unit * k // count * unit for k in range(1, count)]


def joined_along(pieces, dim):
    pieces = jnp.moveaxis(pieces, 0, dim)
    dims = pieces.shape
    return pieces.reshape(*dims[:dim], dims[dim] * dims[dim + 1], *dims[dim + 2 :])


def several_exchanges(value, axis, pieces, split_dim, concat_dim):
    blocks = cut_along(value, split_dim, lax.axis_size(axis))
    cut = max(range(1, max(2, blocks.ndim - 1)), key=lambda d: blocks.shape[d])
    finished = []
    for share in jnp.split(blocks, edges_of(blocks.shape[cut], pieces), axis=cut):
        if share.size:
            finished.append(lax.all_to_all(share, axis, split_axis=0, concat_axis=0, tiled=True))
    return joined_along(jnp.concatenate(finished, axis=cut), concat_dim)


def side_by_side(arrays, axis, dim, along):
    columns = [a.reshape(*a.shape[:along], -1) for a in arrays]
    both = jnp.concatenate(columns, axis=along)
    whole, at, finished = (lax.psum_scatter(both, axis, scatter_dimension=dim, tiled=True), 0, [])
    for a, column in zip(arrays, columns):
        share = whole[..., at : at + column.shape[along]]
        finished.append(share.reshape(*share.shape[:along], *a.shape[along:]))
        at += column.shape[along]
    return tuple(finished)


def gathered_total(value, axis):
    pieces = lax.all_gather(value, axis)
    return pieces.sum(axis=0)


def rope_tables(positions):
    half_dim = HEAD_DIM // 2
    powers = jnp.arange(half_dim).astype(jnp.float32) * (2.0 / HEAD_DIM)
    inverse_freq = ROPE_BASE ** (-powers)
    angles = positions.astype(jnp.float32)[:, None] * inverse_freq[None, :]
    return (jnp.cos(angles), jnp.sin(angles))


def rotate(values, cosine_table, sine_table, turn_sign):
    half_dim = values.shape[-1] // 2
    leading = values[..., :half_dim]
    trailing = values[..., half_dim:]
    cosine_b = cosine_table[:, None, :]
    sine_b = sine_table[:, None, :] * turn_sign
    return jnp.concatenate(
        [leading * cosine_b - trailing * sine_b, trailing * cosine_b + leading * sine_b], axis=-1
    )


def norm_forward(values, gain_vector):
    inverse = lax.rsqrt(jnp.mean(values * values, axis=-1, keepdims=True) + EPSILON)
    return ((values * inverse * gain_vector.astype(jnp.float32)).astype(jnp.bfloat16), inverse)


def norm_backward(values, inverse, gain_vector, upstream):
    scaled = upstream * gain_vector.astype(jnp.float32)
    grad_gain = jnp.sum(upstream * values * inverse, axis=0)
    coupling = jnp.mean(scaled * values, axis=-1, keepdims=True)
    return (inverse * scaled - values * inverse * inverse * inverse * coupling, grad_gain)


def block_scores(query_block, key_all, segments, start_row):
    block_len = query_block.shape[0]
    length = key_all.shape[0]
    scores = jnp.einsum(
        "qkgd,skd->kgqs", query_block, key_all, preferred_element_type=jnp.float32
    ) * HEAD_DIM ** (-0.5)
    query_pos = start_row + jnp.arange(block_len)
    allowed = (jnp.arange(length)[None, :] <= query_pos[:, None]) & (
        segments[None, :] == segments[:, None]
    )
    return jnp.where(allowed[None, None], scores, -1e30)


def split_heads(query, keys, values):
    length = query.shape[0]
    block_len = min(block_limit, length)
    kv_count = keys.shape[1] // HEAD_DIM
    group_size = query.shape[1] // keys.shape[1]
    query_blocks = query.reshape(length // block_len, block_len, kv_count, group_size, HEAD_DIM)
    key_all = keys.reshape(length, kv_count, HEAD_DIM)
    value_all = values.reshape(length, kv_count, HEAD_DIM)
    starts = jnp.arange(length // block_len) * block_len
    return (query_blocks, key_all, value_all, starts, block_len)


def attend_forward(query, keys, values, segments):
    length = query.shape[0]
    query_blocks, key_all, value_all, starts, block_len = split_heads(query, keys, values)

    def one_block(packed):
        query_block, start_row = packed
        scores = block_scores(query_block, key_all, segments, start_row)
        highest = jnp.max(scores, axis=-1, keepdims=True)
        log_total = highest + jnp.log(jnp.sum(jnp.exp(scores - highest), axis=-1, keepdims=True))
        weights = jnp.exp(scores - log_total).astype(jnp.bfloat16)
        mixed = jnp.einsum("kgqs,skd->qkgd", weights, value_all, preferred_element_type=jnp.float32)
        return (mixed.astype(jnp.bfloat16).reshape(block_len, -1), log_total[..., 0])

    attended, log_totals = lax.map(one_block, (query_blocks, starts))
    return (attended.reshape(length, -1), log_totals)


def attend_backward(query, keys, values, segments, attended, log_totals, grad_attended):
    length = query.shape[0]
    query_blocks, key_all, value_all, starts, block_len = split_heads(query, keys, values)
    out_blocks = attended.reshape(query_blocks.shape)
    grad_blocks = grad_attended.reshape(query_blocks.shape)
    scale_factor = HEAD_DIM ** (-0.5)

    def one_block(sums_so_far, packed):
        grad_key_sum, grad_value_sum = sums_so_far
        query_block, out_block, grad_block, log_block, start_row = packed
        scores = block_scores(query_block, key_all, segments, start_row)
        weights = jnp.exp(scores - log_block[..., None])
        weights_low = weights.astype(jnp.bfloat16)
        grad_value_sum = grad_value_sum + jnp.einsum(
            "kgqs,qkgd->skd", weights_low, grad_block, preferred_element_type=jnp.float32
        )
        grad_weights = jnp.einsum(
            "qkgd,skd->kgqs", grad_block, value_all, preferred_element_type=jnp.float32
        )
        row_delta = jnp.transpose(
            jnp.sum(grad_block.astype(jnp.float32) * out_block.astype(jnp.float32), axis=-1),
            (1, 2, 0),
        )
        grad_scores = (weights * (grad_weights - row_delta[..., None])).astype(jnp.bfloat16)
        grad_query = (
            jnp.einsum("kgqs,skd->qkgd", grad_scores, key_all, preferred_element_type=jnp.float32)
            * scale_factor
        )
        grad_key_sum = (
            grad_key_sum
            + jnp.einsum(
                "kgqs,qkgd->skd", grad_scores, query_block, preferred_element_type=jnp.float32
            )
            * scale_factor
        )
        return ((grad_key_sum, grad_value_sum), grad_query.reshape(block_len, -1))

    zeros_kv = jnp.zeros(key_all.shape, jnp.float32)
    sums_end, grad_query = lax.scan(
        one_block, (zeros_kv, zeros_kv), (query_blocks, out_blocks, grad_blocks, log_totals, starts)
    )
    return (
        grad_query.reshape(length, -1),
        sums_end[0].reshape(length, -1),
        sums_end[1].reshape(length, -1),
    )


def spread_rows(row_block, slot_index, capacity, repeats, fsdp_size, per_dev):
    model_width = row_block.shape[1]
    packed_rows = (
        jnp.zeros((EXPERTS * capacity, model_width), jnp.bfloat16).at[slot_index].set(row_block)
    )
    grouped = jnp.repeat(packed_rows.reshape(EXPERTS, capacity, model_width), repeats, axis=0)
    return grouped.reshape(fsdp_size, per_dev, capacity, model_width)


def collect_rows(arrived, slot_index, repeats):
    capacity = arrived.shape[2]
    model_width = arrived.shape[3]
    summed_blocks = jnp.sum(
        arrived.reshape(EXPERTS, repeats, capacity, model_width).astype(jnp.float32), axis=1
    )
    return summed_blocks.reshape(EXPERTS * capacity, model_width)[slot_index]


def on_device(
    inputs,
    project_in,
    project_out,
    gain_attend,
    gain_expert,
    expert_gate,
    expert_up,
    expert_down,
    routes,
    route_weights,
    segments,
    cotangent,
):
    token_count = inputs.shape[1]
    model_width = inputs.shape[2]
    fsdp_size = lax.axis_size("fsdp")
    query_width = HEADS * HEAD_DIM
    kv_width = KV_HEADS * HEAD_DIM
    row_values = inputs[0].astype(jnp.float32)
    in_full, out_full, gain_one, gain_two = sent_together(
        (project_in, project_out, gain_attend, gain_expert), "fsdp", 0, 1
    )
    normed_one, inverse_one = norm_forward(row_values, gain_one)
    projected = jnp.dot(normed_one, in_full, preferred_element_type=jnp.float32)
    positions = lax.axis_index("seq") * token_count + jnp.arange(token_count)
    cosine_table, sine_table = rope_tables(positions)
    query = (
        rotate(
            projected[:, :query_width].reshape(token_count, HEADS, HEAD_DIM),
            cosine_table,
            sine_table,
            1.0,
        )
        .reshape(token_count, query_width)
        .astype(jnp.bfloat16)
    )
    keys = (
        rotate(
            projected[:, query_width : query_width + kv_width].reshape(
                token_count, KV_HEADS, HEAD_DIM
            ),
            cosine_table,
            sine_table,
            1.0,
        )
        .reshape(token_count, kv_width)
        .astype(jnp.bfloat16)
    )
    values = projected[:, query_width + kv_width :].astype(jnp.bfloat16)
    head_query, head_keys, head_values = (
        lax.all_to_all(query, "seq", split_axis=1, concat_axis=0, tiled=True),
        lax.all_to_all(keys, "seq", split_axis=1, concat_axis=0, tiled=True),
        lax.all_to_all(values, "seq", split_axis=1, concat_axis=0, tiled=True),
    )
    seq_ids = segments[0]
    attended, log_totals = attend_forward(head_query, head_keys, head_values, seq_ids)
    mixed = lax.all_to_all(attended, "seq", split_axis=0, concat_axis=1, tiled=True)
    residual = row_values + jnp.dot(mixed, out_full, preferred_element_type=jnp.float32)
    normed_two, inverse_two = norm_forward(residual, gain_two)
    route_ids = routes[0]
    mix_weights = route_weights[0]
    capacity = CAP
    picked = (route_ids[:, :, None] == jnp.arange(EXPERTS)[None, None, :]).astype(jnp.int32)
    per_token = jnp.sum(picked, axis=1)
    before = jnp.cumsum(per_token, axis=0) - per_token
    slot_rank = jnp.sum(before[:, None, :] * picked, axis=2)
    slot_index = (route_ids * capacity + slot_rank).reshape(-1)
    units_dev = expert_gate.shape[0]
    block_units = min(FF, units_dev)
    repeats = FF // block_units
    per_dev = units_dev // block_units
    gate_w = expert_gate.reshape(per_dev, block_units, model_width)
    up_w = expert_up.reshape(per_dev, block_units, model_width)
    down_w = expert_down.reshape(per_dev, block_units, model_width)
    copies = jnp.repeat(normed_two, TOP, axis=0)
    outgoing = spread_rows(copies, slot_index, capacity, repeats, fsdp_size, per_dev)
    arrived = lax.all_to_all(outgoing, "fsdp", split_axis=0, concat_axis=0, tiled=True)
    gate_pre = jnp.einsum("spcd,phd->spch", arrived, gate_w, preferred_element_type=jnp.float32)
    up_pre = jnp.einsum("spcd,phd->spch", arrived, up_w, preferred_element_type=jnp.float32)
    hidden = (jax.nn.silu(gate_pre) * up_pre).astype(jnp.bfloat16)
    pieces = jnp.einsum(
        "spch,phd->spcd", hidden, down_w, preferred_element_type=jnp.float32
    ).astype(jnp.bfloat16)
    returned = lax.all_to_all(pieces, "fsdp", split_axis=0, concat_axis=0, tiled=True)
    chosen = collect_rows(returned, slot_index, repeats).reshape(token_count, TOP, model_width)
    output = (residual + jnp.sum(chosen * mix_weights[:, :, None], axis=1)).astype(jnp.bfloat16)
    grad_out = cotangent[0].astype(jnp.float32)
    grad_mix = (
        (grad_out[:, None, :] * mix_weights[:, :, None])
        .astype(jnp.bfloat16)
        .reshape(token_count * TOP, model_width)
    )
    grad_outgoing = spread_rows(grad_mix, slot_index, capacity, repeats, fsdp_size, per_dev)
    grad_arrived = lax.all_to_all(grad_outgoing, "fsdp", split_axis=0, concat_axis=0, tiled=True)
    grad_hidden = jnp.einsum(
        "spcd,phd->spch", grad_arrived, down_w, preferred_element_type=jnp.float32
    )
    sigmoid_gate = jax.nn.sigmoid(gate_pre)
    grad_gate_pre = (
        grad_hidden * up_pre * sigmoid_gate * (1.0 + gate_pre * (1.0 - sigmoid_gate))
    ).astype(jnp.bfloat16)
    grad_up_pre = (grad_hidden * gate_pre * sigmoid_gate).astype(jnp.bfloat16)
    grad_down_w = jnp.einsum(
        "spch,spcd->phd", hidden, grad_arrived, preferred_element_type=jnp.float32
    ).reshape(units_dev, model_width)
    grad_gate_w = jnp.einsum(
        "spch,spcd->phd", grad_gate_pre, arrived, preferred_element_type=jnp.float32
    ).reshape(units_dev, model_width)
    grad_up_w = jnp.einsum(
        "spch,spcd->phd", grad_up_pre, arrived, preferred_element_type=jnp.float32
    ).reshape(units_dev, model_width)
    back_pieces = jnp.einsum(
        "spch,phd->spcd", grad_gate_pre, gate_w, preferred_element_type=jnp.float32
    )
    back_pieces = (
        back_pieces
        + jnp.einsum("spch,phd->spcd", grad_up_pre, up_w, preferred_element_type=jnp.float32)
    ).astype(jnp.bfloat16)
    grad_back = several_exchanges(back_pieces, "fsdp", 2, 0, 0)
    grad_normed_two = jnp.sum(
        collect_rows(grad_back, slot_index, repeats).reshape(token_count, TOP, model_width), axis=1
    )
    grad_norm_two, second_gain_gradient = norm_backward(
        residual, inverse_two, gain_two, grad_normed_two
    )
    grad_residual = grad_out + grad_norm_two
    grad_res_low = grad_residual.astype(jnp.bfloat16)
    in_again, out_again = (in_full, out_full)
    grad_out_w = jnp.dot(mixed.T, grad_res_low, preferred_element_type=jnp.float32)
    grad_mixed = jnp.dot(grad_res_low, out_again.T, preferred_element_type=jnp.float32).astype(
        jnp.bfloat16
    )
    grad_heads = lax.all_to_all(grad_mixed, "seq", split_axis=1, concat_axis=0, tiled=True)
    grad_query, grad_keys, grad_values = attend_backward(
        head_query, head_keys, head_values, seq_ids, attended, log_totals, grad_heads
    )
    head_len = head_query.shape[0]
    head_cosine, head_sine = rope_tables(jnp.arange(head_len))
    grad_query = (
        rotate(grad_query.reshape(head_len, -1, HEAD_DIM), head_cosine, head_sine, -1.0)
        .reshape(head_len, -1)
        .astype(jnp.bfloat16)
    )
    grad_keys = (
        rotate(grad_keys.reshape(head_len, -1, HEAD_DIM), head_cosine, head_sine, -1.0)
        .reshape(head_len, -1)
        .astype(jnp.bfloat16)
    )
    grad_values = grad_values.astype(jnp.bfloat16)
    back_query, back_keys, back_values = (
        lax.all_to_all(grad_query, "seq", split_axis=0, concat_axis=1, tiled=True),
        lax.all_to_all(grad_keys, "seq", split_axis=0, concat_axis=1, tiled=True),
        lax.all_to_all(grad_values, "seq", split_axis=0, concat_axis=1, tiled=True),
    )
    grad_projected = jnp.concatenate([back_query, back_keys, back_values], axis=1)
    grad_in_w = jnp.dot(normed_one.T, grad_projected, preferred_element_type=jnp.float32)
    grad_normed_one = jnp.dot(grad_projected, in_again.T, preferred_element_type=jnp.float32)
    grad_norm_one, first_gain_gradient = norm_backward(
        row_values, inverse_one, gain_one, grad_normed_one
    )
    grad_inputs = (grad_residual + grad_norm_one).astype(jnp.bfloat16)
    shard_parts = side_by_side(
        (grad_in_w, grad_out_w, first_gain_gradient, second_gain_gradient), "fsdp", 0, 1
    )
    pair_total = (
        gathered_total(shard_parts[0], "seq"),
        gathered_total(shard_parts[1], "seq"),
        gathered_total(shard_parts[2], "seq"),
        gathered_total(shard_parts[3], "seq"),
        gathered_total(grad_gate_w, "seq"),
        gathered_total(grad_up_w, "seq"),
        gathered_total(grad_down_w, "seq"),
    )
    owned_parts = (pair_total[0], pair_total[1], pair_total[2], pair_total[3])
    return (
        output.reshape(1, token_count, model_width),
        grad_inputs.reshape(1, token_count, model_width),
        owned_parts[0],
        owned_parts[1],
        owned_parts[2],
        owned_parts[3],
        pair_total[4],
        pair_total[5],
        pair_total[6],
    )


def solution(mesh):
    in_specs = (
        P("fsdp", "seq", None),
        P("fsdp", None),
        P("fsdp", None),
        P("fsdp"),
        P("fsdp"),
        P("fsdp", None),
        P("fsdp", None),
        P("fsdp", None),
        P("fsdp", "seq", None),
        P("fsdp", "seq", None),
        P("fsdp", None),
        P("fsdp", "seq", None),
    )
    out_specs = (
        P("fsdp", "seq", None),
        P("fsdp", "seq", None),
        P("fsdp", None),
        P("fsdp", None),
        P("fsdp"),
        P("fsdp"),
        P("fsdp", None),
        P("fsdp", None),
        P("fsdp", None),
    )
    return jax.shard_map(
        on_device, mesh=mesh, in_specs=in_specs, out_specs=out_specs, check_vma=False
    )
```

profile of v0, /device:TPU:0, one launch (start us, length us, event | category | flops | bytes accessed | tf_op | source)
XLA Modules:
  0.0 1006.1 jit_solution(11629497013597124336)
XLA Ops:
  15.7 75.5 %all-gather.12.cloned.1.call-done = bf16[1024,3074]{1,0:T(8,128)(2,1)} async-done(((bf16[16,3074]{1,0:T(8,128)(2,1)}), bf16[1024,3074]{1,0:T(8,128)(2,1)}) %all-gather.12.cloned.1.call-update) | async-done | bytes 6295568 | tf_op jit(solution)/shard_map/all_gather | solution.py:27
  137.3 7.3 scatter_custom_fusion
  153.5 20.1 %all-to-all-start.4 = ((bf16[64,1,36,1024]{3,2,1,0:T(8,128)(2,1)}), bf16[64,1,36,1024]{3,2,1,0:T(8,128)(2,1)}, u32[]{:S(2)}, u32[]{:S(2)}) async-start(bf16[64,1,36,1024]{3,2,1,0:T(8,128)(2,1)} %bitcast.282), calls=%async_computation.4 | async-start | bytes 10485760 | tf_op jit(solution)/shard_map/all_to_all | solution.py:293
  178.4 8.1 scatter_custom_fusion.1
  190.6 48.8 %all-to-all-done.4 = bf16[64,1,36,1024]{3,2,1,0:T(8,128)(2,1)} async-done(((bf16[64,1,36,1024]{3,2,1,0:T(8,128)(2,1)}), bf16[64,1,36,1024]{3,2,1,0:T(8,128)(2,1)}, u32[]{:S(2)}, u32[]{:S(2)}) %all-to-all-start.4) | async-done | bytes 4718624 | tf_op jit(solution)/shard_map/all_to_all | solution.py:293
  244.2 11.6 %all-to-all-start.6 = ((bf16[64,1,36,1024]{3,2,1,0:T(8,128)(2,1)}), bf16[64,1,36,1024]{3,2,1,0:T(8,128)(2,1)}, u32[]{:S(2)}, u32[]{:S(2)}) async-start(bf16[64,1,36,1024]{3,2,1,0:T(8,128)(2,1)} %bitcast.283), calls=%async_computation.6 | async-start | bytes 10485760 | tf_op jit(solution)/shard_map/all_to_all | solution.py:310
  255.8 9.5 fusion.9
  265.4 9.3 fusion.11
  274.7 47.2 %all-to-all-done.6 = bf16[64,1,36,1024]{3,2,1,0:T(8,128)(2,1)} async-done(((bf16[64,1,36,1024]{3,2,1,0:T(8,128)(2,1)}), bf16[64,1,36,1024]{3,2,1,0:T(8,128)(2,1)}, u32[]{:S(2)}, u32[]{:S(2)}) %all-to-all-start.6) | async-done | bytes 4718624 | tf_op jit(solution)/shard_map/all_to_all | solution.py:310
  321.9 11.3 %fusion.25 = (bf16[64,1,36,256]{3,0,2,1:T(8,128)(2,1)S(1)}, bf16[64,1,36,256]{3,0,2,1:T(8,128)(2,1)S(1)}, bf16[64,1,36,256]{3,0,2,1:T(8,128)(2,1)}) fusion(f32[64,36,256]{2,0,1:T(8,128)} %fusion.11, f32[64,36,256]{2,0,1:T(8,128)} %fusion.9, bf16[256,1024]{1,0:T(8,128)(2,1)S(1)} %copy-done, bf16[64,1,36,1024]{3,2,1,0:T(8,128)(2,1)} %all-to-all-done.6), kind=kOutput, calls=%fused_computation.39 | convolution fusion | flops 1217396736 | bytes 13500416 | tf_op jit(solution)/shard_map/spcd,phd->spch/dot_general | solution.py:311
  340.9 11.8 %all-to-all-start.7 = ((bf16[64,1,1,16,1024]{4,3,2,1,0:T(8,128)(2,1)}), bf16[64,1,1,16,1024]{4,3,2,1,0:T(8,128)(2,1)}, u32[]{:S(2)}, u32[]{:S(2)}) async-start(bf16[64,1,1,16,1024]{4,3,2,1,0:T(8,128)(2,1)} %copy.139), calls=%async_computation.7 | async-start | bytes 4194304 | tf_op jit(solution)/shard_map/all_to_all | solution.py:57
  357.5 25.9 %all-to-all-done.7 = bf16[64,1,1,16,1024]{4,3,2,1,0:T(8,128)(2,1)} async-done(((bf16[64,1,1,16,1024]{4,3,2,1,0:T(8,128)(2,1)}), bf16[64,1,1,16,1024]{4,3,2,1,0:T(8,128)(2,1)}, u32[]{:S(2)}, u32[]{:S(2)}) %all-to-all-start.7) | async-done | bytes 2097184 | tf_op jit(solution)/shard_map/all_to_all | solution.py:57
  396.7 34.3 %all-to-all-done.8 = bf16[64,1,1,20,1024]{4,3,2,1,0:T(8,128)(2,1)} async-done(((bf16[64,1,1,20,1024]{4,3,2,1,0:T(8,128)(2,1)}), bf16[64,1,1,20,1024]{4,3,2,1,0:T(8,128)(2,1)}, u32[]{:S(2)}, u32[]{:S(2)}) %all-to-all-start.8) | async-done | bytes 2621472 | tf_op jit(solution)/shard_map/all_to_all | solution.py:57
  431.0 6.6 all-to-all-start.5
  437.7 9.3 fusion.54
  448.9 9.3 fusion.48
  471.4 8.8 gather_fusion.1
  480.2 43.4 %all-to-all-done.5 = bf16[64,1,36,1024]{3,2,1,0:T(8,128)(2,1)} async-done(((bf16[64,1,36,1024]{3,2,1,0:T(8,128)(2,1)}), bf16[64,1,36,1024]{3,2,1,0:T(8,128)(2,1)}, u32[]{:S(2)}, u32[]{:S(2)}) %all-to-all-start.5) | async-done | bytes 4718624 | tf_op jit(solution)/shard_map/all_to_all | solution.py:300
  523.6 6.8 convert_reduce_fusion.1
  535.6 8.8 gather_fusion
  544.4 6.0 bitcast_reduce_fusion
  559.8 9.3 fusion.51
  612.8 14.1 %concatenate.35 = f32[1024,3074]{1,0:T(8,128)} concatenate(f32[1024,2048]{1,0:T(8,128)} %fusion.101, f32[1024,1024]{1,0:T(8,128)} %fusion.106, f32[1024,1]{1,0:T(8,128)S(1)} %copy.152, f32[1024,1]{1,0:T(8,128)S(1)} %copy.153), dimensions={1} | concatenate | bytes 25182208 | tf_op jit(solution)/shard_map/concatenate | solution.py:63
  638.3 339.8 %reduce-scatter.2.cloned.1.call-done = f32[16,3074]{1,0:T(8,128)} async-done(((f32[1024,3074]{1,0:T(8,128)}), f32[16,3074]{1,0:T(8,128)}) %reduce-scatter.2.cloned.1.call-update) | async-done | bytes 196752 | tf_op jit(solution)/shard_map/reduce_scatter | solution.py:64
  (219 shorter events, 207.6 us)
Async XLA Ops:
  7.2 314.7 %copy-start = (bf16[256,1024]{1,0:T(8,128)(2,1)S(1)}, bf16[256,1024]{1,0:T(8,128)(2,1)}, u32[]{:S(2)}) copy-start(bf16[256,1024]{1,0:T(8,128)(2,1)} %param.19) | copy-start | bytes 1572868
  7.2 84.0 %all-gather.12.cloned.1.call-start = ((), (), s32[]{:S(2)}) async-start(), calls=%async_computation.14 | async-start | bytes 6656000 | tf_op jit(solution)/shard_map/all_gather | solution.py:27
  14.4 81.2 %copy-start.31 = (f32[32]{0:T(128)}, f32[32]{0:T(128)S(1)}, u32[]{:S(2)}) copy-start(f32[32]{0:T(128)S(1)} %negate_power_fusion) | copy-start | bytes 388
  15.6 80.1 %copy-start.28 = (f32[128]{0:T(128)}, f32[128]{0:T(128)S(1)}, u32[]{:S(2)}) copy-start(f32[128]{0:T(128)S(1)} %add_rsqrt_fusion.1) | copy-start | bytes 1540
  96.4 19.3 %copy-start.30 = (s32[1,256]{1,0:T(1,128)S(1)}, s32[1,256]{1,0:T(1,128)}, u32[]{:S(2)}) copy-start(s32[1,256]{1,0:T(1,128)} %param.22) | copy-start | bytes 3076
  96.4 8.0 all-to-all-start
  104.4 7.8 all-to-all-start.1
  112.2 8.6 all-to-all-start.2
  124.4 8.6 all-to-all-start.3
  153.5 85.8 %all-to-all-start.4 = ((bf16[64,1,36,1024]{3,2,1,0:T(8,128)(2,1)}), bf16[64,1,36,1024]{3,2,1,0:T(8,128)(2,1)}, u32[]{:S(2)}, u32[]{:S(2)}) async-start(bf16[64,1,36,1024]{3,2,1,0:T(8,128)(2,1)} %bitcast.282), calls=%async_computation.4 | async-start | bytes 10485760 | tf_op jit(solution)/shard_map/all_to_all | solution.py:293
  244.2 77.7 %all-to-all-start.6 = ((bf16[64,1,36,1024]{3,2,1,0:T(8,128)(2,1)}), bf16[64,1,36,1024]{3,2,1,0:T(8,128)(2,1)}, u32[]{:S(2)}, u32[]{:S(2)}) async-start(bf16[64,1,36,1024]{3,2,1,0:T(8,128)(2,1)} %bitcast.283), calls=%async_computation.6 | async-start | bytes 10485760 | tf_op jit(solution)/shard_map/all_to_all | solution.py:310
  340.9 42.5 %all-to-all-start.7 = ((bf16[64,1,1,16,1024]{4,3,2,1,0:T(8,128)(2,1)}), bf16[64,1,1,16,1024]{4,3,2,1,0:T(8,128)(2,1)}, u32[]{:S(2)}, u32[]{:S(2)}) async-start(bf16[64,1,1,16,1024]{4,3,2,1,0:T(8,128)(2,1)} %copy.139), calls=%async_computation.7 | async-start | bytes 4194304 | tf_op jit(solution)/shard_map/all_to_all | solution.py:57
  383.4 47.5 %all-to-all-start.8 = ((bf16[64,1,1,20,1024]{4,3,2,1,0:T(8,128)(2,1)}), bf16[64,1,1,20,1024]{4,3,2,1,0:T(8,128)(2,1)}, u32[]{:S(2)}, u32[]{:S(2)}) async-start(bf16[64,1,1,20,1024]{4,3,2,1,0:T(8,128)(2,1)} %copy.140), calls=%async_computation.8 | async-start | bytes 6291456 | tf_op jit(solution)/shard_map/all_to_all | solution.py:57
  431.0 92.6 %all-to-all-start.5 = ((bf16[64,1,36,1024]{3,2,1,0:T(8,128)(2,1)}), bf16[64,1,36,1024]{3,2,1,0:T(8,128)(2,1)}, u32[]{:S(2)}, u32[]{:S(2)}) async-start(bf16[64,1,36,1024]{3,2,1,0:T(8,128)(2,1)} %copy.133), calls=%async_computation.5 | async-start | bytes 10485760 | tf_op jit(solution)/shard_map/all_to_all | solution.py:300
  437.6 191.2 %all-gather.18.cloned.1.call-start = ((), (), s32[]{:S(2)}) async-start(), calls=%async_computation.18 | async-start | bytes 3145728 | tf_op jit(solution)/shard_map/all_gather | solution.py:73
  447.0 184.7 %all-gather.14.cloned.1.call-start = ((), (), s32[]{:S(2)}) async-start(), calls=%async_computation.16 | async-start | bytes 3145728 | tf_op jit(solution)/shard_map/all_gather | solution.py:73
  556.1 13.0 %all-to-all-start.9 = ((bf16[128,2,512]{0,2,1:T(8,128)(2,1)}), bf16[128,2,512]{0,2,1:T(8,128)(2,1)S(1)}, u32[]{:S(2)}, u32[]{:S(2)}) async-start(bf16[128,2,512]{0,2,1:T(8,128)(2,1)} %bitcast.65), calls=%async_computation.9 | async-start | bytes 524288 | tf_op jit(solution)/shard_map/all_to_all | solution.py:349
  559.6 75.0 %all-gather.16.cloned.1.call-start = ((), (), s32[]{:S(2)}) async-start(), calls=%async_computation.17 | async-start | bytes 3145728 | tf_op jit(solution)/shard_map/all_gather | solution.py:73
  572.9 9.2 all-to-all-start.12
  578.0 17.6 %copy-start.6 = (f32[128,1024]{1,0:T(8,128)S(1)}, f32[128,1024]{1,0:T(8,128)}, u32[]{:S(2)}) copy-start(f32[128,1024]{1,0:T(8,128)} %copy-done.5) | copy-start | bytes 1572868
  582.1 9.7 all-to-all-start.11
  591.8 12.4 %all-to-all-start.10 = ((bf16[2,128,512]{1,2,0:T(8,128)(2,1)}), bf16[2,128,512]{1,2,0:T(8,128)(2,1)S(1)}, u32[]{:S(2)}, u32[]{:S(2)}) async-start(bf16[2,128,512]{1,2,0:T(8,128)(2,1)} %copy.146), calls=%async_computation.10 | async-start | bytes 524288 | tf_op jit(solution)/shard_map/all_to_all | solution.py:367
  595.3 382.9 %reduce-scatter.2.cloned.1.call-start = ((), (), s32[]{:S(2)}) async-start(), calls=%async_computation.15 | async-start | bytes 13312000 | tf_op jit(solution)/shard_map/reduce_scatter | solution.py:64
  634.5 364.8 %copy-start.1 = (bf16[256,1024]{1,0:T(8,128)(2,1)S(1)}, bf16[256,1024]{1,0:T(8,128)(2,1)}, u32[]{:S(2)}) copy-start(bf16[256,1024]{1,0:T(8,128)(2,1)} %param.19) | copy-start | bytes 1572868
  (29 other events, 163.4 us)
Sparse Core Ops, SparseCore 0:
  11.8 79.3 all-gather.11
  447.2 59.4 all-gather.17
  508.9 36.6 all-gather.13
  569.2 39.0 all-gather.15
  627.1 351.0 reduce-scatter.1
where the time goes:
time: 1010 us
  waiting for transfers between devices  644 us (64%)
  local copies, waits for them, and re-layouts  105 us (10%)
  matrix products  87.3 us (9%)
  starting transfers between devices  84 us (8%)
  other arithmetic  54.4 us (5%)
  blocking collectives  15.5 us (2%)
  between operations  15.4 us (2%)
    reduce_scatter x1, waiting for transfers between devices, side_by_side(): lax.psum_scatter(both, axis, scatter_dimension=dim, tiled=True)  340 us
    all_gather x1, waiting for transfers between devices, sent_together(): whole = lax.all_gather(both, axis, axis=dim, tiled=True)  75.5 us
    all_to_all x2, waiting for transfers between devices, several_exchanges(): lax.all_to_all(share, axis, split_axis=0, concat_axis=0, tiled=True)  60.2 us
    all_to_all x1, waiting for transfers between devices, on_device(): lax.all_to_all(outgoing, 'fsdp', split_axis=0, concat_axis=0, tiled=True)  48.8 us
    all_to_all x1, waiting for transfers between devices, on_device(): lax.all_to_all(grad_outgoing, 'fsdp', split_axis=0, concat_axis=0, tiled=...  47.2 us
    all_to_all x1, waiting for transfers between devices, on_device(): lax.all_to_all(pieces, 'fsdp', split_axis=0, concat_axis=0, tiled=True)  43.4 us
  transfers between devices with their start and end apart: 18, of which 14 were waited for; matrix products, arithmetic and copies ran while one was open for 18% of the time, Pallas kernels for 0%

commit v1 on v0

v1 whole, which is shorter than its diff:
```python
import jax
import jax.numpy as jnp
from jax import lax
from jax.experimental import pallas as pl
from jax.experimental.pallas import tpu as pltpu
from jax.sharding import Mesh, PartitionSpec as P

HEADS = 16
KV_HEADS = 8
HEAD_DIM = 64
EXPERTS = 32
FF = 512
TOP = 8
CAP = 36
SLOTS = 40
BLOCK = 256
ROW_BLOCK = 256

EPSILON = 1e-06
ROPE_BASE = 10000.0

f32 = jnp.float32
bf16 = jnp.bfloat16

RING = 4
MESH_ID = pl.DeviceIdType.MESH
SWAP = [(0, 1), (1, 0)]
NT = (((1,), (1,)), ((), ()))
TN = (((0,), (0,)), ((), ()))


def dot(a, b, dims=(((1,), (0,)), ((), ()))):
    return lax.dot_general(a, b, dims, preferred_element_type=f32)


def rope_tables(positions):
    half_dim = HEAD_DIM // 2
    powers = jnp.arange(half_dim).astype(f32) * (2.0 / HEAD_DIM)
    inverse_freq = ROPE_BASE ** (-powers)
    angles = positions.astype(f32)[:, None] * inverse_freq[None, :]
    return (jnp.cos(angles), jnp.sin(angles))


def rotate(values, cosine_table, sine_table, turn_sign):
    half_dim = values.shape[-1] // 2
    leading = values[..., :half_dim]
    trailing = values[..., half_dim:]
    cosine_b = cosine_table[:, None, :]
    sine_b = sine_table[:, None, :] * turn_sign
    return jnp.concatenate(
        [leading * cosine_b - trailing * sine_b, trailing * cosine_b + leading * sine_b], axis=-1
    )


def rotate_wide(values, cosine_table, sine_table, turn_sign):
    rows, width = values.shape
    heads = values.reshape(rows, width // HEAD_DIM, HEAD_DIM)
    return rotate(heads, cosine_table, sine_table, turn_sign).reshape(rows, width)


def norm_forward(values, gain_vector):
    inverse = lax.rsqrt(jnp.mean(values * values, axis=-1, keepdims=True) + EPSILON)
    return ((values * inverse * gain_vector.astype(f32)).astype(bf16), inverse)


def norm_backward(values, inverse, gain_vector, upstream):
    scaled = upstream * gain_vector.astype(f32)
    grad_gain = jnp.sum(upstream * values * inverse, axis=0)
    coupling = jnp.mean(scaled * values, axis=-1, keepdims=True)
    return (inverse * scaled - values * inverse * inverse * inverse * coupling, grad_gain)


def rounded(values):
    return lax.reduce_precision(values, exponent_bits=8, mantissa_bits=7)


def three_parts(values):
    first = rounded(values)
    second = rounded(values - first)
    third = values - first - second
    return (first.astype(bf16), second.astype(bf16), third.astype(bf16))


def masked_scores(query, keys, allowed):
    scores = jnp.einsum("qkgd,skd->kgqs", query, keys, preferred_element_type=f32)
    return jnp.where(allowed[None, None], scores * HEAD_DIM ** (-0.5), -1e30)


def attend_forward(query, keys, values, allowed):
    scores = masked_scores(query, keys, allowed)
    highest = jnp.max(scores, axis=-1, keepdims=True)
    log_total = highest + jnp.log(jnp.sum(jnp.exp(scores - highest), axis=-1, keepdims=True))
    weights = jnp.exp(scores - log_total).astype(bf16)
    mixed = jnp.einsum("kgqs,skd->qkgd", weights, values, preferred_element_type=f32)
    return (mixed.astype(bf16), log_total)


def attend_backward(query, keys, values, allowed, attended, log_total, grad_attended):
    scale_factor = HEAD_DIM ** (-0.5)
    weights = jnp.exp(masked_scores(query, keys, allowed) - log_total)
    grad_values = jnp.einsum(
        "kgqs,qkgd->skd", weights.astype(bf16), grad_attended, preferred_element_type=f32
    )
    grad_weights = jnp.einsum("qkgd,skd->kgqs", grad_attended, values, preferred_element_type=f32)
    row_delta = jnp.sum(grad_attended.astype(f32) * attended.astype(f32), axis=-1)
    row_delta = jnp.transpose(row_delta, (1, 2, 0))
    grad_scores = (weights * (grad_weights - row_delta[..., None])).astype(bf16)
    grad_query = jnp.einsum("kgqs,skd->qkgd", grad_scores, keys, preferred_element_type=f32)
    grad_keys = jnp.einsum("kgqs,qkgd->skd", grad_scores, query, preferred_element_type=f32)
    return (grad_query * scale_factor, grad_keys * scale_factor, grad_values)


def experts_first_body(x_ref, g_ref, pre_w_ref, down_w_ref, hidden_ref, grads_ref, back_ref):
    pre = dot(x_ref[...], pre_w_ref[...], NT)
    grad_hidden = dot(g_ref[...], down_w_ref[...], NT)
    back = None
    for b in range(FF // BLOCK):
        gate = pre[:, 2 * b * BLOCK : (2 * b + 1) * BLOCK]
        up = pre[:, (2 * b + 1) * BLOCK : (2 * b + 2) * BLOCK]
        grad_h = grad_hidden[:, b * BLOCK : (b + 1) * BLOCK]
        sigmoid_gate = 1.0 / (1.0 + jnp.exp(-gate))
        silu = gate * sigmoid_gate
        hidden_ref[:, b * BLOCK : (b + 1) * BLOCK] = (silu * up).astype(bf16)
        grad_gate = (grad_h * up * sigmoid_gate * (1.0 + gate * (1.0 - sigmoid_gate))).astype(bf16)
        grad_up = (grad_h * gate * sigmoid_gate).astype(bf16)
        both = jnp.concatenate([grad_gate, grad_up], axis=1)
        grads_ref[:, 2 * b * BLOCK : (2 * b + 2) * BLOCK] = both
        part = dot(both, pre_w_ref[2 * b * BLOCK : (2 * b + 2) * BLOCK, :]).astype(bf16).astype(f32)
        back = part if back is None else back + part
    back_ref[...] = back.astype(bf16)


def experts_first(arrived, grad_arrived, pre_w, down_w):
    rows, width = arrived.shape
    whole = lambda i: (0, 0)
    by_row = lambda i: (i, 0)
    return pl.pallas_call(
        experts_first_body,
        grid=(rows // ROW_BLOCK,),
        in_specs=[
            pl.BlockSpec((ROW_BLOCK, width), by_row),
            pl.BlockSpec((ROW_BLOCK, width), by_row),
            pl.BlockSpec((2 * FF, width), whole),
            pl.BlockSpec((FF, width), whole),
        ],
        out_specs=[
            pl.BlockSpec((ROW_BLOCK, FF), by_row),
            pl.BlockSpec((ROW_BLOCK, 2 * FF), by_row),
            pl.BlockSpec((ROW_BLOCK, width), by_row),
        ],
        out_shape=[
            jax.ShapeDtypeStruct((rows, FF), bf16),
            jax.ShapeDtypeStruct((rows, 2 * FF), bf16),
            jax.ShapeDtypeStruct((rows, width), bf16),
        ],
        cost_estimate=pl.CostEstimate(
            flops=2 * rows * width * FF * 5,
            bytes_accessed=rows * width * 2 * 5,
            transcendentals=rows * FF,
        ),
        name="experts_first",
    )(arrived, grad_arrived, pre_w, down_w)


def experts_second_body(x_ref, g_ref, hidden_ref, grads_ref, down_w_ref, out_ref, mine_ref, theirs_ref):
    @pl.when(pl.program_id(0) == 0)
    def _():
        mine_ref[...] = jnp.zeros_like(mine_ref)
        theirs_ref[...] = jnp.zeros_like(theirs_ref)

    out = None
    for b, total_ref in enumerate((mine_ref, theirs_ref)):
        hidden = hidden_ref[:, b * BLOCK : (b + 1) * BLOCK]
        part = dot(hidden, down_w_ref[b * BLOCK : (b + 1) * BLOCK, :]).astype(bf16).astype(f32)
        out = part if out is None else out + part
        total_ref[: 2 * BLOCK, :] += dot(
            grads_ref[:, 2 * b * BLOCK : (2 * b + 2) * BLOCK], x_ref[...], TN
        )
        total_ref[2 * BLOCK :, :] += dot(hidden, g_ref[...], TN)
    out_ref[...] = out.astype(bf16)


def experts_second(arrived, grad_arrived, hidden, grads, down_w):
    rows, width = arrived.shape
    whole = lambda i: (0, 0)
    by_row = lambda i: (i, 0)
    return pl.pallas_call(
        experts_second_body,
        grid=(rows // ROW_BLOCK,),
        in_specs=[
            pl.BlockSpec((ROW_BLOCK, width), by_row),
            pl.BlockSpec((ROW_BLOCK, width), by_row),
            pl.BlockSpec((ROW_BLOCK, FF), by_row),
            pl.BlockSpec((ROW_BLOCK, 2 * FF), by_row),
            pl.BlockSpec((FF, width), whole),
        ],
        out_specs=[
            pl.BlockSpec((ROW_BLOCK, width), by_row),
            pl.BlockSpec((3 * BLOCK, width), whole),
            pl.BlockSpec((3 * BLOCK, width), whole),
        ],
        out_shape=[
            jax.ShapeDtypeStruct((rows, width), bf16),
            jax.ShapeDtypeStruct((3 * BLOCK, width), f32),
            jax.ShapeDtypeStruct((3 * BLOCK, width), f32),
        ],
        cost_estimate=pl.CostEstimate(
            flops=2 * rows * width * FF * 4,
            bytes_accessed=rows * width * 2 * 5 + 6 * BLOCK * width * 4,
            transcendentals=0,
        ),
        name="experts_second",
    )(arrived, grad_arrived, hidden, grads, down_w)


def gather_body(shard_ref, out_ref, send_sem, recv_sem, local_sem):
    seq, chip, core = (lax.axis_index(name) for name in ("seq", "chip", "core"))
    y, z, half = (chip // (2 * RING), (chip // 2) % RING, chip % 2)

    def device(to_y, to_z, to_half, to_core):
        return (seq, (to_y * RING + to_z) * 2 + to_half, to_core)

    def first(step):
        return device((y + core * step) % RING, (z + (1 - core) * step) % RING, half, core)

    def last(step):
        return device((y + (1 - core) * step) % RING, (z + core * step) % RING, half, core)

    partner = device(y, z, half, 1 - core)
    across = device(y, z, 1 - half, core)
    ahead, behind = (1, RING - 1)
    barrier = pltpu.get_barrier_semaphore()
    for other in (partner, across, first(ahead), first(behind), last(ahead), last(behind)):
        pl.semaphore_signal(barrier, inc=1, device_id=other, device_id_type=MESH_ID)
    pl.semaphore_wait(barrier, 6)

    def send(i, src, dst, to):
        return pltpu.make_async_remote_copy(
            src_ref=src,
            dst_ref=dst,
            send_sem=send_sem.at[i],
            recv_sem=recv_sem.at[i],
            device_id=to,
            device_id_type=MESH_ID,
        )

    def line(c, step, part=None):
        cut = slice(None) if part is None else pl.ds(part * (RING // 2), RING // 2)
        if c == 0:
            return out_ref.at[(y + step) % RING, cut, :, 0]
        return out_ref.at[cut, (z + step) % RING, :, 1]

    def pair(c, step, part=None):
        cut = slice(None) if part is None else part
        if c == 0:
            return out_ref.at[y, (z + step) % RING, cut, 0]
        return out_ref.at[(y + step) % RING, z, cut, 1]

    def run(c):
        sent = []

        def go(i, region, to):
            copy = send(i, region, region, to)
            copy.start()
            sent.append(copy)

        def arrive(i, region):
            send(i, region, region, partner).wait_recv()

        own = out_ref.at[y, z, half, c]
        copy = send(0, shard_ref, own, across)
        copy.start()
        sent.append(copy)
        local = pltpu.make_async_copy(shard_ref, own, local_sem)
        local.start()
        local.wait()
        arrive(0, out_ref.at[y, z, 1 - half, c])
        go(1, pair(c, 0), first(ahead))
        go(2, pair(c, 0), first(behind))
        arrive(1, pair(c, behind))
        go(3, pair(c, behind, 0), first(ahead))
        arrive(2, pair(c, ahead))
        go(4, pair(c, ahead, 1), first(behind))
        arrive(3, pair(c, 2, 0))
        arrive(4, pair(c, 2, 1))
        go(5, line(c, 0), last(ahead))
        go(6, line(c, 0), last(behind))
        go(9, line(c, 0), partner)
        arrive(5, line(c, behind))
        go(7, line(c, behind, 0), last(ahead))
        go(10, line(c, behind), partner)
        arrive(6, line(c, ahead))
        go(8, line(c, ahead, 1), last(behind))
        go(11, line(c, ahead), partner)
        arrive(7, line(c, 2, 0))
        go(12, line(c, 2, 0), partner)
        arrive(8, line(c, 2, 1))
        go(13, line(c, 2, 1), partner)
        arrive(9, line(1 - c, 0))
        arrive(10, line(1 - c, behind))
        arrive(11, line(1 - c, ahead))
        arrive(12, line(1 - c, 2, 0))
        arrive(13, line(1 - c, 2, 1))
        for copy in sent:
            copy.wait_send()

    for c in (0, 1):
        pl.when(core == c)(lambda c=c: run(c))


def gather_weights(shard):
    rows, width = shard.shape
    out = pl.pallas_call(
        gather_body,
        out_shape=jax.ShapeDtypeStruct((RING, RING, 2, 2, rows, width), shard.dtype),
        in_specs=[pl.BlockSpec(memory_space=pltpu.VMEM)],
        out_specs=pl.BlockSpec(memory_space=pl.ANY),
        scratch_shapes=[
            pltpu.SemaphoreType.DMA((14,)),
            pltpu.SemaphoreType.DMA((14,)),
            pltpu.SemaphoreType.DMA,
        ],
        compiler_params=pltpu.CompilerParams(collective_id=0, has_side_effects=True),
        cost_estimate=pl.CostEstimate(
            flops=0, bytes_accessed=rows * width * 2 * 4 * RING * RING * 8, transcendentals=0
        ),
        name="gather_weights",
    )(shard)
    return out.reshape(4 * RING * RING * rows, width)


def projection_grads_body(mine_ref, sent_ref, gp_ref, gr_ref, gains_ref, total_ref, away_ref):
    width = gp_ref.shape[1]
    wide = width + gr_ref.shape[1]
    spread = lax.broadcasted_iota(jnp.int32, (8, 128), 0)
    lane = lax.broadcasted_iota(jnp.int32, (8, 128), 1)
    apart = ((spread == lane) & (spread < 6)).astype(bf16)
    tokens = gp_ref.shape[0]
    for ref, out_ref, which in ((mine_ref, total_ref, 0), (sent_ref, away_ref, 1)):
        out_ref[:, :width] = dot(ref[:tokens, :], gp_ref[...], TN).astype(out_ref.dtype)
        out_ref[:, width:wide] = dot(ref[tokens:, :], gr_ref[...], TN).astype(out_ref.dtype)
        out_ref[:, wide:] = dot(gains_ref[which], apart, TN).astype(out_ref.dtype)


def projection_grads(rows_mine, rows_sent, grad_projected, grad_res_low, gains):
    count = rows_mine.shape[1]
    width = grad_projected.shape[1] + grad_res_low.shape[1] + 128
    tile = 128
    whole = lambda i: (0, 0)
    by_column = lambda i: (0, i)
    by_row = lambda i: (i, 0)
    return pl.pallas_call(
        projection_grads_body,
        grid=(count // tile,),
        in_specs=[
            pl.BlockSpec((rows_mine.shape[0], tile), by_column),
            pl.BlockSpec((rows_sent.shape[0], tile), by_column),
            pl.BlockSpec(grad_projected.shape, whole),
            pl.BlockSpec(grad_res_low.shape, whole),
            pl.BlockSpec((2, 8, tile), lambda i: (0, 0, i)),
        ],
        out_specs=[pl.BlockSpec((tile, width), by_row), pl.BlockSpec((tile, width), by_row)],
        out_shape=[
            jax.ShapeDtypeStruct((count, width), f32),
            jax.ShapeDtypeStruct((count, width), bf16),
        ],
        name="projection_grads",
    )(rows_mine, rows_sent, grad_projected, grad_res_low, gains)


def merge_halves_body(mine_ref, came_ref, out_ref):
    wide = out_ref.shape[1] - 128
    out_ref[:, :wide] = (mine_ref[:, :wide] + came_ref[:, :wide].astype(f32)).astype(bf16)
    parts = mine_ref[:, wide:] + came_ref[:, wide:].astype(f32)
    lane = lax.broadcasted_iota(jnp.int32, parts.shape, 1)
    total = parts + pltpu.roll(parts, 126, 1) + pltpu.roll(parts, 124, 1)
    total = jnp.where(lane < 2, total, 0.0)
    one = total.astype(bf16).astype(f32)
    two = (total - one).astype(bf16).astype(f32)
    three = total - one - two
    out_ref[:, wide:] = (one + pltpu.roll(two, 2, 1) + pltpu.roll(three, 4, 1)).astype(bf16)


def merge_halves(mine, came):
    rows, width = mine.shape
    tile = 128
    by_row = lambda i: (i, 0)
    return pl.pallas_call(
        merge_halves_body,
        grid=(rows // tile,),
        in_specs=[pl.BlockSpec((tile, width), by_row), pl.BlockSpec((tile, width), by_row)],
        out_specs=pl.BlockSpec((tile, width), by_row),
        out_shape=jax.ShapeDtypeStruct((rows, width), bf16),
        name="merge_halves",
    )(mine, came)


def spread_plan(route_ids, mix_weights):
    token_count = route_ids.shape[0]
    expert_ids = jnp.arange(EXPERTS)[None, None, :]
    named = route_ids[:, :, None] == expert_ids
    picked = jnp.any(named, axis=1)
    token_weight = jnp.sum(jnp.where(named, mix_weights[:, :, None], 0.0), axis=1)
    earlier = jnp.arange(token_count)[None, :] < jnp.arange(token_count)[:, None]
    rank = dot(earlier.astype(bf16), picked.astype(bf16)).astype(jnp.int32)
    at_slot = jnp.where(picked, rank, -1).T[:, None, :] == jnp.arange(SLOTS)[None, :, None]
    placed = at_slot.astype(bf16).reshape(EXPERTS * SLOTS, token_count)
    weighted = jnp.where(at_slot, token_weight.T[:, None, :], 0.0)
    slot_weight = jnp.sum(weighted, axis=2).reshape(EXPERTS * SLOTS, 1)
    mixers = [part.reshape(EXPERTS * SLOTS, token_count) for part in three_parts(weighted)]
    return (placed, slot_weight, mixers)


def exchange(rows):
    width = rows.shape[-1]
    blocks = rows.reshape(EXPERTS, -1, width)
    return lax.all_to_all(blocks, "chip", split_axis=0, concat_axis=0, tiled=True).reshape(-1, width)


def on_device(
    inputs,
    project_in,
    project_out,
    gain_attend,
    gain_expert,
    expert_gate,
    expert_up,
    expert_down,
    routes,
    route_weights,
    segments,
    cotangent,
):
    token_count = inputs.shape[1]
    model_width = inputs.shape[2]
    query_width = HEADS * HEAD_DIM
    kv_width = KV_HEADS * HEAD_DIM
    group = HEADS // KV_HEADS
    seq = lax.axis_index("seq")
    core = lax.axis_index("core")
    own_low = inputs[0]
    other_low = lax.ppermute(own_low, "seq", SWAP)

    placed, slot_weight, mixers = spread_plan(routes[0], route_weights[0])
    grad_rows = (dot(placed, cotangent[0]) * slot_weight).astype(bf16)
    grad_arrived = exchange(grad_rows)

    own_units = jnp.concatenate([expert_gate, expert_up, expert_down], axis=0)
    other_units = lax.ppermute(own_units, "core", SWAP)
    pre_w = jnp.concatenate([own_units[: 2 * BLOCK], other_units[: 2 * BLOCK]], axis=0)
    down_w = jnp.concatenate([expert_down, other_units[2 * BLOCK :]], axis=0)

    share = gain_attend.shape[0]
    wide = query_width + 2 * kv_width + query_width
    filler = jnp.zeros((share, 126), bf16)
    gathered = gather_weights(
        jnp.concatenate(
            [project_in, project_out, gain_attend[:, None], gain_expert[:, None], filler], axis=1
        )
    )
    in_full = gathered[:, : query_width + 2 * kv_width]
    out_full = gathered[:, query_width + 2 * kv_width : wide]
    gain_one, gain_two = (gathered[:, wide], gathered[:, wide + 1])

    row_values = own_low.astype(f32)
    normed_one, inverse_one = norm_forward(row_values, gain_one)
    normed_other, _ = norm_forward(other_low.astype(f32), gain_one)
    kv_w = in_full[:, query_width:]
    projected = dot(normed_one, in_full)
    projected_other = dot(normed_other, kv_w)
    own_at = seq * token_count + jnp.arange(token_count)
    other_at = (1 - seq) * token_count + jnp.arange(token_count)
    own_cos, own_sin = rope_tables(own_at)
    other_cos, other_sin = rope_tables(other_at)
    query = rotate_wide(projected[:, :query_width], own_cos, own_sin, 1.0).astype(bf16)
    key_cut = query_width + kv_width
    own_keys = rotate_wide(projected[:, query_width:key_cut], own_cos, own_sin, 1.0)
    other_keys = rotate_wide(projected_other[:, :kv_width], other_cos, other_sin, 1.0)
    keys = jnp.concatenate([own_keys, other_keys], axis=0).astype(bf16)
    values = jnp.concatenate([projected[:, key_cut:], projected_other[:, kv_width:]], axis=0)
    query = query.reshape(token_count, KV_HEADS, group, HEAD_DIM)
    keys = keys.reshape(2 * token_count, KV_HEADS, HEAD_DIM)
    values = values.astype(bf16).reshape(2 * token_count, KV_HEADS, HEAD_DIM)
    seq_ids = segments[0]
    own_ids = lax.dynamic_slice(seq_ids, (seq * token_count,), (token_count,))
    other_ids = lax.dynamic_slice(seq_ids, ((1 - seq) * token_count,), (token_count,))
    key_at = jnp.concatenate([own_at, other_at])
    key_ids = jnp.concatenate([own_ids, other_ids])
    allowed = (key_at[None, :] <= own_at[:, None]) & (key_ids[None, :] == own_ids[:, None])
    attended, log_total = attend_forward(query, keys, values, allowed)
    mixed = attended.reshape(token_count, query_width)
    residual = row_values + dot(mixed, out_full)
    normed_two, inverse_two = norm_forward(residual, gain_two)

    arrived = exchange(dot(placed, normed_two).astype(bf16))
    hidden, grads, back = experts_first(arrived, grad_arrived, pre_w, down_w)
    grad_back = exchange(back)
    out_rows, mine, theirs = experts_second(arrived, grad_arrived, hidden, grads, down_w)
    grad_back, out_rows = lax.optimization_barrier((grad_back, out_rows))
    returned = exchange(out_rows)
    chip_total = mine + lax.ppermute(theirs, "core", SWAP)
    total_low = rounded(chip_total)
    total_other = lax.ppermute(total_low.astype(bf16), "seq", SWAP)

    grad_out = cotangent[0].astype(f32)
    grad_normed_two = dot(placed, grad_back, TN)
    grad_norm_two, gain_two_grad = norm_backward(residual, inverse_two, gain_two, grad_normed_two)
    grad_residual = grad_out + grad_norm_two
    grad_res_low = grad_residual.astype(bf16)
    grad_mixed = dot(grad_res_low, out_full, NT).astype(bf16)
    grad_query, grad_keys, grad_values = attend_backward(
        query, keys, values, allowed, attended, log_total, grad_mixed.reshape(attended.shape)
    )
    grad_query = grad_query.reshape(token_count, query_width)
    grad_keys = grad_keys.reshape(2 * token_count, kv_width)
    grad_values = grad_values.reshape(2 * token_count, kv_width)
    away_keys = rotate_wide(grad_keys[token_count:], other_cos, other_sin, -1.0)
    away = jnp.concatenate([away_keys, grad_values[token_count:]], axis=1).astype(bf16)
    came = lax.ppermute(away, "seq", SWAP).astype(f32)
    grad_query = rotate_wide(grad_query, own_cos, own_sin, -1.0)
    grad_keys = rotate_wide(grad_keys[:token_count], own_cos, own_sin, -1.0) + came[:, :kv_width]
    grad_values = grad_values[:token_count] + came[:, kv_width:]
    grad_projected = jnp.concatenate([grad_query, grad_keys, grad_values], axis=1).astype(bf16)
    grad_projected, total_other = lax.optimization_barrier((grad_projected, total_other))
    grad_units = total_low + total_other.astype(f32)
    grad_normed_one = dot(grad_projected, in_full, NT)
    grad_norm_one, gain_one_grad = norm_backward(row_values, inverse_one, gain_one, grad_normed_one)
    grad_inputs = (grad_residual + grad_norm_one).astype(bf16)

    owners = EXPERTS
    feature = jnp.arange(model_width)[:, None]
    slot = jnp.arange(model_width)[None, :]
    half_width = model_width // 2
    of_core = jnp.where(slot < half_width, core, 1 - core)
    at = slot % half_width
    chosen_half = feature == (2 * (at // share) + of_core) * share + at % share
    chosen_half = chosen_half.astype(bf16)
    features = dot(jnp.concatenate([normed_one, mixed], axis=0), chosen_half).astype(bf16)
    gain_pair = jnp.stack([gain_one_grad, gain_two_grad], axis=0)
    gain_parts = jnp.concatenate(three_parts(gain_pair) + (jnp.zeros_like(gain_pair, bf16),), axis=0)
    gain_parts = dot(gain_parts, chosen_half).astype(bf16)
    gain_parts = jnp.stack([gain_parts[:, :half_width], gain_parts[:, half_width:]], axis=0)
    grads_mine, grads_sent = projection_grads(
        features[:, :half_width], features[:, half_width:], grad_projected, grad_res_low, gain_parts
    )
    chip_rows = merge_halves(grads_mine, lax.ppermute(grads_sent, "core", SWAP))
    landed = lax.all_to_all(
        chip_rows.reshape(owners, share, wide + 128),
        "chip",
        split_axis=0,
        concat_axis=0,
        tiled=True,
    )
    totals = jnp.sum(landed.astype(f32), axis=0)
    totals = totals + lax.ppermute(totals, "seq", SWAP)
    gain_totals = totals[:, wide : wide + 2] + totals[:, wide + 2 : wide + 4]
    gain_totals = gain_totals + totals[:, wide + 4 : wide + 6]

    mix = jnp.concatenate(mixers, axis=1)
    chosen = dot(mix, returned, TN).reshape(3, token_count, model_width)
    output = (residual + (chosen[2] + chosen[1] + chosen[0])).astype(bf16)
    in_width = query_width + 2 * kv_width
    return (
        output.reshape(1, token_count, model_width),
        grad_inputs.reshape(1, token_count, model_width),
        totals[:, :in_width],
        totals[:, in_width:wide],
        gain_totals[:, 0],
        gain_totals[:, 1],
        grad_units[:BLOCK],
        grad_units[BLOCK : 2 * BLOCK],
        grad_units[2 * BLOCK :],
    )


def solution(mesh):
    devices = mesh.devices
    cores = Mesh(devices.reshape(devices.shape[0], -1, 2), ("seq", "chip", "core"))
    every = ("chip", "core")
    by_token = P(every, "seq", None)
    by_row = P(every, None)
    in_specs = (
        by_token,
        by_row,
        by_row,
        P(every),
        P(every),
        by_row,
        by_row,
        by_row,
        by_token,
        by_token,
        by_row,
        by_token,
    )
    out_specs = (by_token, by_token, by_row, by_row, P(every), P(every), by_row, by_row, by_row)
    return jax.shard_map(
        on_device, mesh=cores, in_specs=in_specs, out_specs=out_specs, check_vma=False
    )
```

time: 1010 us -> 400 us (0.40)
  waiting for transfers between devices: 644 us -> 162 us
  Pallas kernels: 0 us -> 104 us
  local copies, waits for them, and re-layouts: 105 us -> 15.8 us
  matrix products: 87.3 us -> 36.3 us
  starting transfers between devices: 84 us -> 51.2 us
  other arithmetic: 54.4 us -> 26.5 us
  blocking collectives: 15.5 us -> 0 us
  between operations: 15.4 us -> 1.83 us
    reduce_scatter x1 -> x0, waiting for transfers between devices: 340 us -> none  [side_by_side(): lax.psum_scatter(both, axis, scatter_dimension=dim, tiled=True)]
    all_to_all x13 -> x5, waiting for transfers between devices: 229 us -> 121 us  [the longest x4 87.4 us: exchange(): lax.all_to_all(blocks, 'chip', split_axis=0, concat_axis=0, tiled=True)]
    pallas_call x0 -> x5, Pallas kernels: none -> 104 us  [the longest x1 68.2 us: gather_weights(): pl.pallas_call(gather_body, out_shape=jax.ShapeDtypeStruct((RING, RING, 2...]
    all_gather x4 -> x0, waiting for transfers between devices: 75.5 us -> none  [the longest x1 75.5 us: sent_together(): whole = lax.all_gather(both, axis, axis=dim, tiled=True)]
    dot_general x21 -> x18, matrix products: 87.3 us -> 36.3 us  [the longest x12 30.8 us: dot(): return lax.dot_general(a, b, dims, preferred_element_type=f32)]
    all_to_all x13 -> x5, starting transfers between devices: 83.2 us -> 33.3 us  [the longest x4 26.7 us: exchange(): lax.all_to_all(blocks, 'chip', split_axis=0, concat_axis=0, tiled=True)]
    ppermute x0 -> x7, waiting for transfers between devices: none -> 41.2 us  [the longest x1 34.1 us: on_device(): came = lax.ppermute(away, 'seq', SWAP).astype(f32)]
    reduce_sum x15 -> x5, other arithmetic: 30.1 us -> 1.87 us  [the longest x1 0.73 us: spread_plan(): jnp.sum(jnp.where(named, mix_weights[:, :, None], 0.0), axis=1)]
  transfers between devices with their start and end apart: 18 -> 12, of which waited for: 14 -> 8; matrix products, arithmetic and copies ran while one was open for 18% -> 16% of each run, Pallas kernels for 0% -> 22%
where the time goes in v1:
time: 400 us; the launch traced here: 398 us
  waiting for transfers between devices  162 us (40%)
  Pallas kernels  104 us (26%)
  starting transfers between devices  51.2 us (13%)
  matrix products  36.3 us (9%)
  other arithmetic  26.5 us (7%)
  local copies, waits for them, and re-layouts  15.8 us (4%)
    all_to_all x4, waiting for transfers between devices, exchange(): lax.all_to_all(blocks, 'chip', split_axis=0, concat_axis=0, tiled=True)  87.4 us
    pallas_call x1, Pallas kernels, gather_weights(): pl.pallas_call(gather_body, out_shape=jax.ShapeDtypeStruct((RING, RING, 2...  68.2 us
    ppermute x1, waiting for transfers between devices, on_device(): came = lax.ppermute(away, 'seq', SWAP).astype(f32)  34.1 us
    all_to_all x1, waiting for transfers between devices, on_device(): lax.all_to_all(chip_rows.reshape(owners, share, wide + 128), 'chip', spli...  33.9 us
    dot_general x12, matrix products, dot(): return lax.dot_general(a, b, dims, preferred_element_type=f32)  30.8 us
    all_to_all x4, starting transfers between devices, exchange(): lax.all_to_all(blocks, 'chip', split_axis=0, concat_axis=0, tiled=True)  26.7 us
    pallas_call x1, Pallas kernels, experts_first(): pl.pallas_call(experts_first_body, grid=(rows // ROW_BLOCK,), in_specs=[p...  12 us
    pallas_call x1, Pallas kernels, experts_second(): pl.pallas_call(experts_second_body, grid=(rows // ROW_BLOCK,), in_specs=[...  11.4 us
  transfers between devices with their start and end apart: 12, of which 8 were waited for; matrix products, arithmetic and copies ran while one was open for 16% of the time, Pallas kernels for 22%

profile of v1, /device:TPU:0, one launch (start us, length us, event | category | flops | bytes accessed | tf_op | source)
XLA Modules:
  0.0 398.4 jit_solution(5584842469752682899)
XLA Ops:
  4.4 3.3 multiply_convert_fusion
  7.7 10.8 %all-to-all-start.1 = ((bf16[32,40,1024]{2,1,0:T(8,128)(2,1)}), bf16[32,40,1024]{2,1,0:T(8,128)(2,1)}, u32[]{:S(2)}, u32[]{:S(2)}) async-start(bf16[32,40,1024]{2,1,0:T(8,128)(2,1)} %bitcast.31), calls=%async_computation.1 | async-start | bytes 5242880 | tf_op jit(solution)/shard_map/all_to_all | solution.py:417
  19.6 68.2 %gather_weights.1 = bf16[4,4,2,2,16,3200]{5,4,3,2,1,0:T(8,128)(2,1)} custom-call(bf16[16,3200]{1,0:T(8,128)(2,1)} %concatenate.74.shard_ref), custom_call_target="tpu_custom_call" | custom-call | bytes 52428800 | tf_op jit(solution)/shard_map/gather_weights/pallas_call | solution.py:313
  109.5 6.2 %all-to-all-start = ((bf16[32,40,1024]{2,1,0:T(8,128)(2,1)}), bf16[32,40,1024]{2,1,0:T(8,128)(2,1)}, u32[]{:S(2)}, u32[]{:S(2)}) async-start(bf16[32,40,1024]{2,1,0:T(8,128)(2,1)} %bitcast.150), calls=%async_computation | async-start | bytes 5242880 | tf_op jit(solution)/shard_map/all_to_all | solution.py:417
  117.2 3.3 collective-permute-done.1
  123.3 32.4 %all-to-all-done = bf16[32,40,1024]{2,1,0:T(8,128)(2,1)} async-done(((bf16[32,40,1024]{2,1,0:T(8,128)(2,1)}), bf16[32,40,1024]{2,1,0:T(8,128)(2,1)}, u32[]{:S(2)}, u32[]{:S(2)}) %all-to-all-start) | async-done | bytes 2621472 | tf_op jit(solution)/shard_map/all_to_all | solution.py:417
  155.7 12.0 %experts_first.1 = (bf16[1280,512]{1,0:T(8,128)(2,1)}, bf16[1280,1024]{1,0:T(8,128)(2,1)}, bf16[1280,1024]{1,0:T(8,128)(2,1)}) custom-call(bf16[1280,1024]{1,0:T(8,128)(2,1)} %bitcast.28.x_ref, bf16[1280,1024]{1,0:T(8,128)(2,1)} %bitcast.32.g_ref, bf16[1024,1024]{1,0:T(8,128)(2,1)} %pad_maximum_fusion.pre_w_ref, bf16[512,1024]{1,0:T(8,128)(2,1)} %pad_maximum_fusion.2.down_w_ref), custom_call_target="tpu_custom_call" | custom-call | flops 6710886400 | bytes 13107200 | tf_op jit(solution)/shard_map/experts_first/pallas_call | solution.py:137
  167.6 5.0 %all-to-all-start.2 = ((bf16[32,40,1024]{2,1,0:T(8,128)(2,1)}), bf16[32,40,1024]{2,1,0:T(8,128)(2,1)}, u32[]{:S(2)}, u32[]{:S(2)}) async-start(bf16[32,40,1024]{2,1,0:T(8,128)(2,1)} %bitcast.157), calls=%async_computation.2 | async-start | bytes 5242880 | tf_op jit(solution)/shard_map/all_to_all | solution.py:417
  172.6 11.4 %experts_second.1 = (bf16[1280,1024]{1,0:T(8,128)(2,1)}, f32[768,1024]{1,0:T(8,128)}, f32[768,1024]{1,0:T(8,128)}) custom-call(bf16[1280,1024]{1,0:T(8,128)(2,1)} %bitcast.28.x_ref, bf16[1280,1024]{1,0:T(8,128)(2,1)} %bitcast.32.g_ref, bf16[1280,512]{1,0:T(8,128)(2,1)} %get-tuple-element.22.hidden_ref, bf16[1280,1024]{1,0:T(8,128)(2,1)} %get-tuple-element.23.grads_ref, ...), custom_call_target="tpu_custom_call" | custom-call | flops 5368709120 | bytes 19398656 | tf_op jit(solution)/shard_map/experts_second/pallas_call | solution.py:187
  188.4 22.3 %all-to-all-done.2 = bf16[32,40,1024]{2,1,0:T(8,128)(2,1)} async-done(((bf16[32,40,1024]{2,1,0:T(8,128)(2,1)}), bf16[32,40,1024]{2,1,0:T(8,128)(2,1)}, u32[]{:S(2)}, u32[]{:S(2)}) %all-to-all-start.2) | async-done | bytes 2621472 | tf_op jit(solution)/shard_map/all_to_all | solution.py:417
  210.7 3.0 multiply_reduce_fusion
  221.9 3.6 fusion.26
  225.4 6.5 %collective-permute-start.4 = (bf16[768,1024]{1,0:T(8,128)(2,1)}, bf16[768,1024]{1,0:T(8,128)(2,1)}, u32[]{:S(2)}, u32[]{:S(2)}) collective-permute-start(bf16[768,1024]{1,0:T(8,128)(2,1)} %fusion.26), channel_id=1, source_target_pairs={{0,64},{64,0},{1,65},{65,1},{2,66},{66,2},{3,67},{67,3},{4,68},{68... | collective-permute-start | bytes 4718600 | tf_op jit(solution)/shard_map/ppermute | solution.py:503
  235.5 34.1 %collective-permute-done.2 = bf16[128,1024]{1,0:T(8,128)(2,1)S(1)} collective-permute-done((bf16[128,1024]{1,0:T(8,128)(2,1)S(1)}, bf16[128,1024]{1,0:T(8,128)(2,1)S(1)}, u32[]{:S(2)}, u32[]{:S(2)}) %collective-permute-start.2) | collective-permute-done | bytes 262176 | tf_op jit(solution)/shard_map/ppermute | solution.py:519
  270.0 5.2 %fusion.50 = (f32[1024]{0:T(1024)S(1)}, f32[128]{0:T(128)}, f32[128,1024]{1,0:T(8,128)}) fusion(f32[128]{0:T(128)S(1)} %copy-done.57, bf16[1,128,1024]{2,1,0:T(8,128)(2,1)S(1)} %copy-done.6, f32[1024]{0:T(1024)S(1)} %bitcast.185, bf16[128,2048]{1,0:T(8,128)(2,1)S(1)} %pad_maximum_fusion.3.gp_ref, bf16[1024,3200]{1,0:T(8,128)(2,1)} %bitcast.149), kind=kOutput, calls=%fused_computation.78 | convolution fusion | flops 537787264 | bytes 5514240 | tf_op jit(solution)/shard_map/dot_general | solution.py:33
  276.6 6.0 %projection_grads.1 = (f32[512,3200]{1,0:T(8,128)}, bf16[512,3200]{1,0:T(8,128)(2,1)}) custom-call(bf16[256,512]{1,0:T(8,128)(2,1)} %get-tuple-element.53.mine_ref, bf16[256,512]{1,0:T(8,128)(2,1)} %get-tuple-element.52.sent_ref, bf16[128,2048]{1,0:T(8,128)(2,1)} %copy-done.10, bf16[128,1024]{1,0:T(8,128)(2,1)} %copy-done.20, ...), custom_call_target="tpu_custom_call" | custom-call | tf_op jit(solution)/shard_map/projection_grads/pallas_call | solution.py:352
  282.6 4.8 %all-to-all-start.3 = ((bf16[32,40,1024]{2,1,0:T(8,128)(2,1)}), bf16[32,40,1024]{2,1,0:T(8,128)(2,1)}, u32[]{:S(2)}, u32[]{:S(2)}) async-start(bf16[32,40,1024]{2,1,0:T(8,128)(2,1)} %bitcast.156), calls=%async_computation.3 | async-start | bytes 5242880 | tf_op jit(solution)/shard_map/all_to_all | solution.py:417
  290.5 6.6 %merge_halves.1 = bf16[512,3200]{1,0:T(8,128)(2,1)} custom-call(f32[512,3200]{1,0:T(8,128)} %get-tuple-element.30.mine_ref, bf16[512,3200]{1,0:T(8,128)(2,1)} %copy-done.7), custom_call_target="tpu_custom_call" | custom-call | tf_op jit(solution)/shard_map/merge_halves/pallas_call | solution.py:388
  297.1 32.6 %all-to-all-done.3 = bf16[32,40,1024]{2,1,0:T(8,128)(2,1)} async-done(((bf16[32,40,1024]{2,1,0:T(8,128)(2,1)}), bf16[32,40,1024]{2,1,0:T(8,128)(2,1)}, u32[]{:S(2)}, u32[]{:S(2)}) %all-to-all-start.3) | async-done | bytes 2621472 | tf_op jit(solution)/shard_map/all_to_all | solution.py:417
  329.7 6.6 %all-to-all-start.4 = ((bf16[32,16,3200]{2,1,0:T(8,128)(2,1)}), bf16[32,16,3200]{2,1,0:T(8,128)(2,1)S(1)}, u32[]{:S(2)}, u32[]{:S(2)}) async-start(bf16[32,16,3200]{2,1,0:T(8,128)(2,1)} %bitcast.143), calls=%async_computation.4 | async-start | bytes 6553600 | tf_op jit(solution)/shard_map/all_to_all | solution.py:547
  338.5 4.2 %convert_add_fusion = f32[768,1024]{1,0:T(8,128)S(1)} fusion(bf16[768,1024]{1,0:T(8,128)(2,1)} %collective-permute-done.4, f32[768,1024]{1,0:T(8,128)} %get-tuple-element.27, f32[768,1024]{1,0:T(8,128)} %collective-permute-done.3), kind=kLoop, calls=%fused_computation.10 | loop fusion | flops 3145728 | bytes 11010048 | tf_op jit(solution)/shard_map/add | solution.py:525
  344.5 4.1 %fusion.29 = f32[384,1024]{1,0:T(8,128)} fusion(bf16[1280,1024]{1,0:T(8,128)(2,1)} %bitcast.36, bf16[1280,128]{1,0:T(8,128)(2,1)S(1)} %get-tuple-element.66, bf16[1280,128]{1,0:T(8,128)(2,1)S(1)} %get-tuple-element.65, bf16[1280,128]{1,0:T(8,128)(2,1)S(1)} %get-tuple-element.64), kind=kOutput, calls=%fused_computation.47 | convolution fusion | flops 1009582080 | bytes 5177344 | tf_op jit(solution)/shard_map/dot_general | solution.py:33
  348.7 33.9 %all-to-all-done.4 = bf16[32,16,3200]{2,1,0:T(8,128)(2,1)S(1)} async-done(((bf16[32,16,3200]{2,1,0:T(8,128)(2,1)}), bf16[32,16,3200]{2,1,0:T(8,128)(2,1)S(1)}, u32[]{:S(2)}, u32[]{:S(2)}) %all-to-all-start.4) | async-done | bytes 3276832 | tf_op jit(solution)/shard_map/all_to_all | solution.py:547
  383.1 9.4 %collective-permute-start.6 = (f32[16,3200]{1,0:T(8,128)S(1)}, f32[16,3200]{1,0:T(8,128)S(1)}, u32[]{:S(2)}, u32[]{:S(2)}) collective-permute-start(f32[16,3200]{1,0:T(8,128)S(1)} %convert_reduce_fusion), channel_id=1, source_target_pairs={{0,64},{64,0},{1,65},{65,1},{2,66},{66,2},{3,67},{67,3},{4,68},{68... | collective-permute-start | bytes 614408 | tf_op jit(solution)/shard_map/ppermute | solution.py:555
  (245 shorter events, 60.9 us)
Async XLA Ops:
  0.6 98.2 %collective-permute-start = (bf16[128,1024]{1,0:T(8,128)(2,1)}, bf16[128,1024]{1,0:T(8,128)(2,1)}, u32[]{:S(2)}, u32[]{:S(2)}) collective-permute-start(bf16[128,1024]{1,0:T(8,128)(2,1)} %bitcast.155), channel_id=1, source_target_pairs={{0,64},{64,0},{1,65},{65,1},{2,66},{66,2},{3,67},{67,3},{4,68},{68... | collective-permute-start | bytes 786440 | tf_op jit(solution)/shard_map/ppermute | solution.py:442
  3.1 94.4 %copy-start.23 = (s32[32,128]{1,0:T(8,128)}, s32[32,128]{1,0:T(8,128)S(1)}, u32[]{:S(2)}) copy-start(s32[32,128]{1,0:T(8,128)S(1)} %fusion.28) | copy-start | bytes 49156
  7.7 101.8 %all-to-all-start.1 = ((bf16[32,40,1024]{2,1,0:T(8,128)(2,1)}), bf16[32,40,1024]{2,1,0:T(8,128)(2,1)}, u32[]{:S(2)}, u32[]{:S(2)}) async-start(bf16[32,40,1024]{2,1,0:T(8,128)(2,1)} %bitcast.31), calls=%async_computation.1 | async-start | bytes 5242880 | tf_op jit(solution)/shard_map/all_to_all | solution.py:417
  18.7 70.5 %copy-start.56 = (f32[128]{0:T(128)}, f32[128]{0:T(128)S(1)}, u32[]{:S(2)}) copy-start(f32[128]{0:T(128)S(1)} %add_rsqrt_fusion.2) | copy-start | bytes 1540
  107.0 106.8 %copy-start = (f32[128,1024]{1,0:T(8,128)}, f32[128,1024]{1,0:T(8,128)S(1)}, u32[]{:S(2)}) copy-start(f32[128,1024]{1,0:T(8,128)S(1)} %get-tuple-element.86) | copy-start | bytes 1572868
  109.5 46.2 %all-to-all-start = ((bf16[32,40,1024]{2,1,0:T(8,128)(2,1)}), bf16[32,40,1024]{2,1,0:T(8,128)(2,1)}, u32[]{:S(2)}, u32[]{:S(2)}) async-start(bf16[32,40,1024]{2,1,0:T(8,128)(2,1)} %bitcast.150), calls=%async_computation | async-start | bytes 5242880 | tf_op jit(solution)/shard_map/all_to_all | solution.py:417
  117.0 3.5 collective-permute-start.1
  167.6 43.1 %all-to-all-start.2 = ((bf16[32,40,1024]{2,1,0:T(8,128)(2,1)}), bf16[32,40,1024]{2,1,0:T(8,128)(2,1)}, u32[]{:S(2)}, u32[]{:S(2)}) async-start(bf16[32,40,1024]{2,1,0:T(8,128)(2,1)} %bitcast.157), calls=%async_computation.2 | async-start | bytes 5242880 | tf_op jit(solution)/shard_map/all_to_all | solution.py:417
  184.1 37.8 %collective-permute-start.3 = (f32[768,1024]{1,0:T(8,128)}, f32[768,1024]{1,0:T(8,128)}, u32[]{:S(2)}, u32[]{:S(2)}) collective-permute-start(f32[768,1024]{1,0:T(8,128)} %get-tuple-element.28), channel_id=1, source_target_pairs={{0,1},{1,0},{2,3},{3,2},{4,5},{5,4},{6,7},{7,6},{8,9},{9,8},{10,11... | collective-permute-start | bytes 9437192 | tf_op jit(solution)/shard_map/ppermute | solution.py:501
  184.7 26.0 %copy-start.16 = (pred[1280,128]{1,0:T(32,128)(4,1)S(1)}, pred[1280,128]{1,0:T(32,128)(4,1)}, u32[]{:S(2)}) copy-start(pred[1280,128]{1,0:T(32,128)(4,1)} %copy-done.15) | copy-start | bytes 491524
  187.6 27.0 %copy-start.8 = (bf16[1,128,1024]{2,1,0:T(8,128)(2,1)S(1)}, bf16[1,128,1024]{2,1,0:T(8,128)(2,1)}, u32[]{:S(2)}) copy-start(bf16[1,128,1024]{2,1,0:T(8,128)(2,1)} %param.23) | copy-start | bytes 786436
  225.4 44.5 %collective-permute-start.4 = (bf16[768,1024]{1,0:T(8,128)(2,1)}, bf16[768,1024]{1,0:T(8,128)(2,1)}, u32[]{:S(2)}, u32[]{:S(2)}) collective-permute-start(bf16[768,1024]{1,0:T(8,128)(2,1)} %fusion.26), channel_id=1, source_target_pairs={{0,64},{64,0},{1,65},{65,1},{2,66},{66,2},{3,67},{67,3},{4,68},{68... | collective-permute-start | bytes 4718600 | tf_op jit(solution)/shard_map/ppermute | solution.py:503
  233.8 35.9 %collective-permute-start.2 = (bf16[128,1024]{1,0:T(8,128)(2,1)S(1)}, bf16[128,1024]{1,0:T(8,128)(2,1)S(1)}, u32[]{:S(2)}, u32[]{:S(2)}) collective-permute-start(bf16[128,1024]{1,0:T(8,128)(2,1)S(1)} %pad_maximum_fusion.7), channel_id=1, source_target_pairs={{0,64},{64,0},{1,65},{65,1},{2,66},{66,2},{3,67},{67,3},{4,68},{68... | collective-permute-start | bytes 786440 | tf_op jit(solution)/shard_map/ppermute | solution.py:519
  235.2 34.7 %copy-start.6 = (bf16[1,128,1024]{2,1,0:T(8,128)(2,1)S(1)}, bf16[1,128,1024]{2,1,0:T(8,128)(2,1)}, u32[]{:S(2)}) copy-start(bf16[1,128,1024]{2,1,0:T(8,128)(2,1)} %param.12) | copy-start | bytes 786436
  235.3 34.7 %copy-start.47 = (f32[1024,1]{0,1:T(1,128)S(1)}, f32[1024,1]{0,1:T(1,128)}, u32[]{:S(2)}) copy-start(f32[1024,1]{0,1:T(1,128)} %copy-done.45) | copy-start | bytes 12292
  235.3 34.7 %copy-start.57 = (f32[128]{0:T(128)S(1)}, f32[128]{0:T(128)}, u32[]{:S(2)}) copy-start(f32[128]{0:T(128)} %copy-done.56) | copy-start | bytes 1540
  282.6 6.1 %collective-permute-start.5 = (bf16[512,3200]{1,0:T(8,128)(2,1)}, bf16[512,3200]{1,0:T(8,128)(2,1)S(1)}, u32[]{:S(2)}, u32[]{:S(2)}) collective-permute-start(bf16[512,3200]{1,0:T(8,128)(2,1)} %get-tuple-element.31), channel_id=1, source_target_pairs={{0,1},{1,0},{2,3},{3,2},{4,5},{5,4},{6,7},{7,6},{8,9},{9,8},{10,11... | collective-permute-start | bytes 9830408 | tf_op jit(solution)/shard_map/ppermute | solution.py:546
  282.6 47.1 %all-to-all-start.3 = ((bf16[32,40,1024]{2,1,0:T(8,128)(2,1)}), bf16[32,40,1024]{2,1,0:T(8,128)(2,1)}, u32[]{:S(2)}, u32[]{:S(2)}) async-start(bf16[32,40,1024]{2,1,0:T(8,128)(2,1)} %bitcast.156), calls=%async_computation.3 | async-start | bytes 5242880 | tf_op jit(solution)/shard_map/all_to_all | solution.py:417
  329.7 52.9 %all-to-all-start.4 = ((bf16[32,16,3200]{2,1,0:T(8,128)(2,1)}), bf16[32,16,3200]{2,1,0:T(8,128)(2,1)S(1)}, u32[]{:S(2)}, u32[]{:S(2)}) async-start(bf16[32,16,3200]{2,1,0:T(8,128)(2,1)} %bitcast.143), calls=%async_computation.4 | async-start | bytes 6553600 | tf_op jit(solution)/shard_map/all_to_all | solution.py:547
  348.6 43.9 %copy-start.41 = (f32[1024,1]{0,1:T(1,128)S(1)}, f32[1024,1]{0,1:T(1,128)}, u32[]{:S(2)}) copy-start(f32[1024,1]{0,1:T(1,128)} %copy.100) | copy-start | bytes 12292
  348.6 43.9 %copy-start.48 = (f32[1024,1]{0,1:T(1,128)S(1)}, f32[1024,1]{0,1:T(1,128)}, u32[]{:S(2)}) copy-start(f32[1024,1]{0,1:T(1,128)} %copy-done.45) | copy-start | bytes 12292
  348.6 43.9 %copy-start.53 = (f32[128]{0:T(128)S(1)}, f32[128]{0:T(128)}, u32[]{:S(2)}) copy-start(f32[128]{0:T(128)} %copy-done.51) | copy-start | bytes 1540
  348.6 43.9 %copy-start.58 = (f32[128]{0:T(128)S(1)}, f32[128]{0:T(128)}, u32[]{:S(2)}) copy-start(f32[128]{0:T(128)} %copy-done.56) | copy-start | bytes 1540
  383.1 13.2 %collective-permute-start.6 = (f32[16,3200]{1,0:T(8,128)S(1)}, f32[16,3200]{1,0:T(8,128)S(1)}, u32[]{:S(2)}, u32[]{:S(2)}) collective-permute-start(f32[16,3200]{1,0:T(8,128)S(1)} %convert_reduce_fusion), channel_id=1, source_target_pairs={{0,64},{64,0},{1,65},{65,1},{2,66},{66,2},{3,67},{67,3},{4,68},{68... | collective-permute-start | bytes 614408 | tf_op jit(solution)/shard_map/ppermute | solution.py:555
  (54 other events, 348.0 us)

commit v2 on v1

--- a/solution.py
+++ b/solution.py
@@ -162,51 +162,124 @@
     )(arrived, grad_arrived, pre_w, down_w)
 
 
-def experts_second_body(x_ref, g_ref, hidden_ref, grads_ref, down_w_ref, out_ref, mine_ref, theirs_ref):
-    @pl.when(pl.program_id(0) == 0)
-    def _():
-        mine_ref[...] = jnp.zeros_like(mine_ref)
-        theirs_ref[...] = jnp.zeros_like(theirs_ref)
-
-    out = None
-    for b, total_ref in enumerate((mine_ref, theirs_ref)):
-        hidden = hidden_ref[:, b * BLOCK : (b + 1) * BLOCK]
-        part = dot(hidden, down_w_ref[b * BLOCK : (b + 1) * BLOCK, :]).astype(bf16).astype(f32)
-        out = part if out is None else out + part
-        total_ref[: 2 * BLOCK, :] += dot(
-            grads_ref[:, 2 * b * BLOCK : (2 * b + 2) * BLOCK], x_ref[...], TN
+def experts_second_body(
+    x_ref,
+    g_ref,
+    hidden_ref,
+    grads_ref,
+    down_w_ref,
+    out_ref,
+    total_ref,
+    theirs,
+    came,
+    low,
+    low_came,
+    send_sem,
+    recv_sem,
+):
+    seq, chip, core = (lax.axis_index(name) for name in ("seq", "chip", "core"))
+    partner = (seq, chip, 1 - core)
+    mirror = (1 - seq, chip, core)
+    barrier = pltpu.get_barrier_semaphore()
+    for other in (partner, mirror):
+        pl.semaphore_signal(barrier, inc=1, device_id=other, device_id_type=MESH_ID)
+    pl.semaphore_wait(barrier, 2)
+    width = x_ref.shape[1]
+
+    def send(i, src, dst, to):
+        return pltpu.make_async_remote_copy(
+            src_ref=src,
+            dst_ref=dst,
+            send_sem=send_sem.at[i],
+            recv_sem=recv_sem.at[i],
+            device_id=to,
+            device_id_type=MESH_ID,
         )
-        total_ref[2 * BLOCK :, :] += dot(hidden, g_ref[...], TN)
-    out_ref[...] = out.astype(bf16)
+
+    def unit_grads(block, kind, store):
+        if kind < 2:
+            at = (2 * block + kind) * BLOCK
+            left, right = (grads_ref, x_ref)
+        else:
+            at = block * BLOCK
+            left, right = (hidden_ref, g_ref)
+
+        @pl.loop(0, width // BLOCK)
+        def _(n):
+            columns = pl.ds(pl.multiple_of(n * BLOCK, BLOCK), BLOCK)
+            store[kind, :, columns] = dot(left[:, at : at + BLOCK], right[:, columns], TN)
+
+    away = [send(k, theirs.at[k], came.at[k], partner) for k in range(3)]
+    across = [send(3 + k, low.at[k], low_came.at[k], mirror) for k in range(3)]
+    for k in range(3):
+        unit_grads(1, k, theirs)
+        if k:
+            away[k - 1].start()
+    unit_grads(0, 0, total_ref)
+    away[2].start()
+
+    def join(k):
+        away[k].wait_recv()
+
+        @pl.loop(0, BLOCK // 32)
+        def _(r):
+            rows = pl.ds(pl.multiple_of(r * 32, 32), 32)
+            low[k, rows, :] = (total_ref[k, rows, :] + came[k, rows, :]).astype(bf16)
+
+    for k in range(3):
+        join(k)
+        if k < 2:
+            unit_grads(0, k + 1, total_ref)
+            across[k].start()
+
+    @pl.loop(0, x_ref.shape[0] // ROW_BLOCK)
+    def _(r):
+        rows = pl.ds(pl.multiple_of(r * ROW_BLOCK, ROW_BLOCK), ROW_BLOCK)
+        out = None
+        for b in range(FF // BLOCK):
+            units = slice(b * BLOCK, (b + 1) * BLOCK)
+            part = dot(hidden_ref[rows, units], down_w_ref[units, :]).astype(bf16).astype(f32)
+            out = part if out is None else out + part
+        out_ref[rows, :] = out.astype(bf16)
+
+        @pl.when(r == 0)
+        def _():
+            across[2].start()
+
+    for k in range(3):
+        across[k].wait_recv()
+
+        @pl.loop(0, BLOCK // 32)
+        def _(r):
+            rows = pl.ds(pl.multiple_of(r * 32, 32), 32)
+            total_ref[k, rows, :] = low[k, rows, :].astype(f32) + low_came[k, rows, :].astype(f32)
+
+    for copy in away + across:
+        copy.wait_send()
 
 
 def experts_second(arrived, grad_arrived, hidden, grads, down_w):
     rows, width = arrived.shape
-    whole = lambda i: (0, 0)
-    by_row = lambda i: (i, 0)
     return pl.pallas_call(
         experts_second_body,
-        grid=(rows // ROW_BLOCK,),
-        in_specs=[
-            pl.BlockSpec((ROW_BLOCK, width), by_row),
-            pl.BlockSpec((ROW_BLOCK, width), by_row),
-            pl.BlockSpec((ROW_BLOCK, FF), by_row),
-            pl.BlockSpec((ROW_BLOCK, 2 * FF), by_row),
-            pl.BlockSpec((FF, width), whole),
-        ],
-        out_specs=[
-            pl.BlockSpec((ROW_BLOCK, width), by_row),
-            pl.BlockSpec((3 * BLOCK, width), whole),
-            pl.BlockSpec((3 * BLOCK, width), whole),
-        ],
+        in_specs=[pl.BlockSpec(memory_space=pltpu.VMEM)] * 5,
+        out_specs=[pl.BlockSpec(memory_space=pltpu.VMEM)] * 2,
         out_shape=[
             jax.ShapeDtypeStruct((rows, width), bf16),
-            jax.ShapeDtypeStruct((3 * BLOCK, width), f32),
-            jax.ShapeDtypeStruct((3 * BLOCK, width), f32),
-        ],
+            jax.ShapeDtypeStruct((3, BLOCK, width), f32),
+        ],
+        scratch_shapes=[
+            pltpu.VMEM((3, BLOCK, width), f32),
+            pltpu.VMEM((3, BLOCK, width), f32),
+            pltpu.VMEM((3, BLOCK, width), bf16),
+            pltpu.VMEM((3, BLOCK, width), bf16),
+            pltpu.SemaphoreType.DMA((6,)),
+            pltpu.SemaphoreType.DMA((6,)),
+        ],
+        compiler_params=pltpu.CompilerParams(collective_id=1, has_side_effects=True),
         cost_estimate=pl.CostEstimate(
             flops=2 * rows * width * FF * 4,
-            bytes_accessed=rows * width * 2 * 5 + 6 * BLOCK * width * 4,
+            bytes_accessed=rows * width * 2 * 20,
             transcendentals=0,
         ),
         name="experts_second",
@@ -443,7 +516,6 @@
 
     placed, slot_weight, mixers = spread_plan(routes[0], route_weights[0])
     grad_rows = (dot(placed, cotangent[0]) * slot_weight).astype(bf16)
-    grad_arrived = exchange(grad_rows)
 
     own_units = jnp.concatenate([expert_gate, expert_up, expert_down], axis=0)
     other_units = lax.ppermute(own_units, "core", SWAP)
@@ -458,6 +530,8 @@
             [project_in, project_out, gain_attend[:, None], gain_expert[:, None], filler], axis=1
         )
     )
+    gathered, grad_rows = lax.optimization_barrier((gathered, grad_rows))
+    grad_arrived = exchange(grad_rows)
     in_full = gathered[:, : query_width + 2 * kv_width]
     out_full = gathered[:, query_width + 2 * kv_width : wide]
     gain_one, gain_two = (gathered[:, wide], gathered[:, wide + 1])
@@ -495,12 +569,9 @@
     arrived = exchange(dot(placed, normed_two).astype(bf16))
     hidden, grads, back = experts_first(arrived, grad_arrived, pre_w, down_w)
     grad_back = exchange(back)
-    out_rows, mine, theirs = experts_second(arrived, grad_arrived, hidden, grads, down_w)
+    out_rows, grad_units = experts_second(arrived, grad_arrived, hidden, grads, down_w)
     grad_back, out_rows = lax.optimization_barrier((grad_back, out_rows))
     returned = exchange(out_rows)
-    chip_total = mine + lax.ppermute(theirs, "core", SWAP)
-    total_low = rounded(chip_total)
-    total_other = lax.ppermute(total_low.astype(bf16), "seq", SWAP)
 
     grad_out = cotangent[0].astype(f32)
     grad_normed_two = dot(placed, grad_back, TN)
@@ -521,8 +592,7 @@
     grad_keys = rotate_wide(grad_keys[:token_count], own_cos, own_sin, -1.0) + came[:, :kv_width]
     grad_values = grad_values[:token_count] + came[:, kv_width:]
     grad_projected = jnp.concatenate([grad_query, grad_keys, grad_values], axis=1).astype(bf16)
-    grad_projected, total_other = lax.optimization_barrier((grad_projected, total_other))
-    grad_units = total_low + total_other.astype(f32)
+    grad_projected, returned = lax.optimization_barrier((grad_projected, returned))
     grad_normed_one = dot(grad_projected, in_full, NT)
     grad_norm_one, gain_one_grad = norm_backward(row_values, inverse_one, gain_one, grad_normed_one)
     grad_inputs = (grad_residual + grad_norm_one).astype(bf16)
@@ -567,9 +637,9 @@
         totals[:, in_width:wide],
         gain_totals[:, 0],
         gain_totals[:, 1],
-        grad_units[:BLOCK],
-        grad_units[BLOCK : 2 * BLOCK],
-        grad_units[2 * BLOCK :],
+        grad_units[0],
+        grad_units[1],
+        grad_units[2],
     )
 
 

time: 400 us -> 381 us (0.953)
  waiting for transfers between devices: 162 us -> 125 us
  Pallas kernels: 104 us -> 132 us
  other arithmetic: 26.5 us -> 16.1 us
  local copies, waits for them, and re-layouts: 15.8 us -> 26.2 us
  starting transfers between devices: 51.2 us -> 43 us
    pallas_call x1, Pallas kernels: 11.4 us -> 64.1 us  [experts_second(): pl.pallas_call(experts_second_body, in_specs=[pl.BlockSpec(memory_space=p...]
    all_to_all x4, waiting for transfers between devices: 87.4 us -> 47.4 us  [exchange(): lax.all_to_all(blocks, 'chip', split_axis=0, concat_axis=0, tiled=True)]
    pallas_call x1, Pallas kernels: 68.2 us -> 43.7 us  [gather_weights(): pl.pallas_call(gather_body, out_shape=jax.ShapeDtypeStruct((RING, RING, 2...]
    optimization_barrier x0 -> x1, local copies, waits for them, and re-layouts: none -> 9.58 us  [on_device(): gathered, grad_rows = lax.optimization_barrier((gathered, grad_rows))]
    ppermute x1, waiting for transfers between devices: 34.1 us -> 26.7 us  [on_device(): came = lax.ppermute(away, 'seq', SWAP).astype(f32)]
    ppermute x1, starting transfers between devices: 9.44 us -> 2.87 us  [on_device(): totals = totals + lax.ppermute(totals, 'seq', SWAP)]
    ppermute x2 -> x0, starting transfers between devices: 6.53 us -> none  [the longest x1 6.53 us: on_device(): total_other = lax.ppermute(total_low.astype(bf16), 'seq', SWAP)]
    all_to_all x1, waiting for transfers between devices: 33.9 us -> 39.1 us  [on_device(): lax.all_to_all(chip_rows.reshape(owners, share, wide + 128), 'chip', spli...]
  transfers between devices with their start and end apart: 12 -> 10, of which waited for: 8 -> 8; matrix products, arithmetic and copies ran while one was open for 16% -> 15% of each run, Pallas kernels for 22% -> 28%
where the time goes in v2:
time: 381 us; the launch traced here: 379 us
  Pallas kernels  132 us (35%)
  waiting for transfers between devices  125 us (33%)
  starting transfers between devices  43 us (11%)
  matrix products  34.2 us (9%)
  local copies, waits for them, and re-layouts  26.2 us (7%)
  other arithmetic  16.1 us (4%)
    pallas_call x1, Pallas kernels, experts_second(): pl.pallas_call(experts_second_body, in_specs=[pl.BlockSpec(memory_space=p...  64.1 us
    all_to_all x4, waiting for transfers between devices, exchange(): lax.all_to_all(blocks, 'chip', split_axis=0, concat_axis=0, tiled=True)  47.4 us
    pallas_call x1, Pallas kernels, gather_weights(): pl.pallas_call(gather_body, out_shape=jax.ShapeDtypeStruct((RING, RING, 2...  43.7 us
    all_to_all x1, waiting for transfers between devices, on_device(): lax.all_to_all(chip_rows.reshape(owners, share, wide + 128), 'chip', spli...  39.1 us
    all_to_all x4, starting transfers between devices, exchange(): lax.all_to_all(blocks, 'chip', split_axis=0, concat_axis=0, tiled=True)  31.1 us
    dot_general x12, matrix products, dot(): return lax.dot_general(a, b, dims, preferred_element_type=f32)  29.7 us
    ppermute x1, waiting for transfers between devices, on_device(): came = lax.ppermute(away, 'seq', SWAP).astype(f32)  26.7 us
    pallas_call x1, Pallas kernels, experts_first(): pl.pallas_call(experts_first_body, grid=(rows // ROW_BLOCK,), in_specs=[p...  12 us
  transfers between devices with their start and end apart: 10, of which 8 were waited for; matrix products, arithmetic and copies ran while one was open for 15% of the time, Pallas kernels for 28%

profile of v2, /device:TPU:0, one launch (start us, length us, event | category | flops | bytes accessed | tf_op | source)
XLA Modules:
  0.0 379.0 jit_solution(1279346467691758651)
XLA Ops:
  5.4 43.7 %gather_weights.1 = bf16[4,4,2,2,16,3200]{5,4,3,2,1,0:T(8,128)(2,1)} custom-call(bf16[16,3200]{1,0:T(8,128)(2,1)} %concatenate.74.shard_ref), custom_call_target="tpu_custom_call" | custom-call | bytes 52428800 | tf_op jit(solution)/shard_map/gather_weights/pallas_call | solution.py:386
  52.1 7.5 %all-to-all-start.1 = ((bf16[32,40,1024]{2,1,0:T(8,128)(2,1)}), bf16[32,40,1024]{2,1,0:T(8,128)(2,1)}, u32[]{:S(2)}, u32[]{:S(2)}) async-start(bf16[32,40,1024]{2,1,0:T(8,128)(2,1)} %bitcast.33), calls=%async_computation.1 | async-start | bytes 5242880 | tf_op jit(solution)/shard_map/all_to_all | solution.py:490
  59.8 9.6 %copy.71 = bf16[1024,3200]{0,1:T(8,128)(2,1)} copy(bf16[1024,3200]{1,0:T(8,128)(2,1)} %bitcast.149) | data formatting | bytes 13107200 | tf_op jit(solution)/shard_map/optimization_barrier | solution.py:533
  70.9 3.0 fusion.4
  88.7 10.9 %all-to-all-done.1 = bf16[32,40,1024]{2,1,0:T(8,128)(2,1)} async-done(((bf16[32,40,1024]{2,1,0:T(8,128)(2,1)}), bf16[32,40,1024]{2,1,0:T(8,128)(2,1)}, u32[]{:S(2)}, u32[]{:S(2)}) %all-to-all-start.1) | async-done | bytes 2621472 | tf_op jit(solution)/shard_map/all_to_all | solution.py:490
  99.6 4.8 %all-to-all-start = ((bf16[32,40,1024]{2,1,0:T(8,128)(2,1)}), bf16[32,40,1024]{2,1,0:T(8,128)(2,1)}, u32[]{:S(2)}, u32[]{:S(2)}) async-start(bf16[32,40,1024]{2,1,0:T(8,128)(2,1)} %bitcast.156), calls=%async_computation | async-start | bytes 5242880 | tf_op jit(solution)/shard_map/all_to_all | solution.py:490
  106.1 3.4 collective-permute-done.1
  112.2 30.4 %all-to-all-done = bf16[32,40,1024]{2,1,0:T(8,128)(2,1)} async-done(((bf16[32,40,1024]{2,1,0:T(8,128)(2,1)}), bf16[32,40,1024]{2,1,0:T(8,128)(2,1)}, u32[]{:S(2)}, u32[]{:S(2)}) %all-to-all-start) | async-done | bytes 2621472 | tf_op jit(solution)/shard_map/all_to_all | solution.py:490
  142.6 12.0 %experts_first.1 = (bf16[1280,512]{1,0:T(8,128)(2,1)}, bf16[1280,1024]{1,0:T(8,128)(2,1)}, bf16[1280,1024]{1,0:T(8,128)(2,1)}) custom-call(bf16[1280,1024]{1,0:T(8,128)(2,1)} %bitcast.32.x_ref, bf16[1280,1024]{1,0:T(8,128)(2,1)} %bitcast.34.g_ref, bf16[1024,1024]{1,0:T(8,128)(2,1)} %pad_maximum_fusion.pre_w_ref, bf16[512,1024]{1,0:T(8,128)(2,1)} %pad_maximum_fusion.2.down_w_ref), custom_call_target="tpu_custom_call" | custom-call | flops 6710886400 | bytes 13107200 | tf_op jit(solution)/shard_map/experts_first/pallas_call | solution.py:137
  154.6 5.1 %all-to-all-start.2 = ((bf16[32,40,1024]{2,1,0:T(8,128)(2,1)}), bf16[32,40,1024]{2,1,0:T(8,128)(2,1)}, u32[]{:S(2)}, u32[]{:S(2)}) async-start(bf16[32,40,1024]{2,1,0:T(8,128)(2,1)} %bitcast.163), calls=%async_computation.2 | async-start | bytes 5242880 | tf_op jit(solution)/shard_map/all_to_all | solution.py:490
  164.5 64.1 %experts_second.1 = (bf16[1280,1024]{1,0:T(8,128)(2,1)}, f32[3,256,1024]{2,1,0:T(8,128)}) custom-call(bf16[1280,1024]{1,0:T(8,128)(2,1)} %bitcast.32.x_ref, bf16[1280,1024]{1,0:T(8,128)(2,1)} %bitcast.34.g_ref, bf16[1280,512]{1,0:T(8,128)(2,1)} %get-tuple-element.25.hidden_ref, bf16[1280,1024]{1,0:T(8,128)(2,1)} %get-tuple-element.26.grads_ref, ...), custom_call_target="tpu_custom_call" | custom-call | flops 5368709120 | bytes 52428800 | tf_op jit(solution)/shard_map/experts_second/pallas_call | solution.py:263
  228.7 3.0 multiply_reduce_fusion
  235.4 13.7 %all-to-all-start.3 = ((bf16[32,40,1024]{2,1,0:T(8,128)(2,1)}), bf16[32,40,1024]{2,1,0:T(8,128)(2,1)}, u32[]{:S(2)}, u32[]{:S(2)}) async-start(bf16[32,40,1024]{2,1,0:T(8,128)(2,1)} %bitcast.162), calls=%async_computation.3 | async-start | bytes 5242880 | tf_op jit(solution)/shard_map/all_to_all | solution.py:490
  254.0 26.7 %collective-permute-done.2 = bf16[128,1024]{1,0:T(8,128)(2,1)S(1)} collective-permute-done((bf16[128,1024]{1,0:T(8,128)(2,1)S(1)}, bf16[128,1024]{1,0:T(8,128)(2,1)S(1)}, u32[]{:S(2)}, u32[]{:S(2)}) %collective-permute-start.2) | collective-permute-done | bytes 262176 | tf_op jit(solution)/shard_map/ppermute | solution.py:590
  280.9 6.0 %all-to-all-done.3 = bf16[32,40,1024]{2,1,0:T(8,128)(2,1)} async-done(((bf16[32,40,1024]{2,1,0:T(8,128)(2,1)}), bf16[32,40,1024]{2,1,0:T(8,128)(2,1)}, u32[]{:S(2)}, u32[]{:S(2)}) %all-to-all-start.3) | async-done | bytes 2621472 | tf_op jit(solution)/shard_map/all_to_all | solution.py:490
  286.9 5.1 %fusion.49 = (f32[1024]{0:T(1024)S(1)}, f32[128]{0:T(128)}, f32[128,1024]{1,0:T(8,128)}) fusion(f32[128]{0:T(128)S(1)} %copy-done.59, bf16[1,128,1024]{2,1,0:T(8,128)(2,1)S(1)} %copy-done.5, f32[1024]{0:T(1024)S(1)} %bitcast.191, bf16[128,2048]{1,0:T(8,128)(2,1)S(1)} %pad_maximum_fusion.3.gp_ref, bf16[1024,3200]{1,0:T(8,128)(2,1)} %bitcast.154), kind=kOutput, calls=%fused_computation.78 | convolution fusion | flops 537787264 | bytes 5514240 | tf_op jit(solution)/shard_map/dot_general | solution.py:33
  293.4 6.0 %projection_grads.1 = (f32[512,3200]{1,0:T(8,128)}, bf16[512,3200]{1,0:T(8,128)(2,1)}) custom-call(bf16[256,512]{1,0:T(8,128)(2,1)} %get-tuple-element.55.mine_ref, bf16[256,512]{1,0:T(8,128)(2,1)} %get-tuple-element.54.sent_ref, bf16[128,2048]{1,0:T(8,128)(2,1)} %copy-done.9, bf16[128,1024]{1,0:T(8,128)(2,1)} %copy-done.21, ...), custom_call_target="tpu_custom_call" | custom-call | tf_op jit(solution)/shard_map/projection_grads/pallas_call | solution.py:425
  299.5 6.1 %collective-permute-done.3.came_ref = bf16[512,3200]{1,0:T(8,128)(2,1)S(1)} collective-permute-done((bf16[512,3200]{1,0:T(8,128)(2,1)}, bf16[512,3200]{1,0:T(8,128)(2,1)S(1)}, u32[]{:S(2)}, u32[]{:S(2)}) %collective-permute-start.3) | collective-permute-done | bytes 3276832 | tf_op jit(solution)/shard_map/ppermute | solution.py:616
  307.3 6.6 %merge_halves.1 = bf16[512,3200]{1,0:T(8,128)(2,1)} custom-call(f32[512,3200]{1,0:T(8,128)} %get-tuple-element.32.mine_ref, bf16[512,3200]{1,0:T(8,128)(2,1)} %copy-done.6), custom_call_target="tpu_custom_call" | custom-call | tf_op jit(solution)/shard_map/merge_halves/pallas_call | solution.py:461
  313.9 7.2 %all-to-all-start.4 = ((bf16[32,16,3200]{2,1,0:T(8,128)(2,1)}), bf16[32,16,3200]{2,1,0:T(8,128)(2,1)S(1)}, u32[]{:S(2)}, u32[]{:S(2)}) async-start(bf16[32,16,3200]{2,1,0:T(8,128)(2,1)} %bitcast.155), calls=%async_computation.4 | async-start | bytes 6553600 | tf_op jit(solution)/shard_map/all_to_all | solution.py:617
  322.2 3.6 slice_bitcast_fusion
  326.3 4.1 %fusion.28 = f32[384,1024]{1,0:T(8,128)} fusion(bf16[1280,1024]{1,0:T(8,128)(2,1)} %bitcast.56, bf16[1280,128]{1,0:T(8,128)(2,1)S(1)} %get-tuple-element.67, bf16[1280,128]{1,0:T(8,128)(2,1)S(1)} %get-tuple-element.68, bf16[1280,128]{1,0:T(8,128)(2,1)S(1)} %get-tuple-element.66), kind=kOutput, calls=%fused_computation.47 | convolution fusion | flops 1009582080 | bytes 5177344 | tf_op jit(solution)/shard_map/dot_general | solution.py:33
  330.4 39.1 %all-to-all-done.4 = bf16[32,16,3200]{2,1,0:T(8,128)(2,1)S(1)} async-done(((bf16[32,16,3200]{2,1,0:T(8,128)(2,1)}), bf16[32,16,3200]{2,1,0:T(8,128)(2,1)S(1)}, u32[]{:S(2)}, u32[]{:S(2)}) %all-to-all-start.4) | async-done | bytes 3276832 | tf_op jit(solution)/shard_map/all_to_all | solution.py:617
  370.0 2.9 collective-permute-start.4
  (241 shorter events, 52.6 us)
Async XLA Ops:
  0.6 77.3 %collective-permute-start = (bf16[128,1024]{1,0:T(8,128)(2,1)}, bf16[128,1024]{1,0:T(8,128)(2,1)}, u32[]{:S(2)}, u32[]{:S(2)}) collective-permute-start(bf16[128,1024]{1,0:T(8,128)(2,1)} %bitcast.161), channel_id=1, source_target_pairs={{0,64},{64,0},{1,65},{65,1},{2,66},{66,2},{3,67},{67,3},{4,68},{68... | collective-permute-start | bytes 786440 | tf_op jit(solution)/shard_map/ppermute | solution.py:515
  5.4 43.7 %copy-start.50 = (s32[1,128,8]{1,2,0:T(8,128)S(1)}, s32[1,128,8]{1,2,0:T(8,128)}, u32[]{:S(2)}) copy-start(s32[1,128,8]{1,2,0:T(8,128)} %param.20) | copy-start | bytes 12292
  5.4 44.0 %copy-start.57 = (f32[1,128,8]{1,2,0:T(8,128)S(1)}, f32[1,128,8]{1,2,0:T(8,128)}, u32[]{:S(2)}) copy-start(f32[1,128,8]{1,2,0:T(8,128)} %param.21) | copy-start | bytes 12292
  5.4 44.4 %copy-start.7 = (bf16[1,128,1024]{2,1,0:T(8,128)(2,1)S(1)}, bf16[1,128,1024]{2,1,0:T(8,128)(2,1)}, u32[]{:S(2)}) copy-start(bf16[1,128,1024]{2,1,0:T(8,128)(2,1)} %param.23) | copy-start | bytes 786436
  52.1 47.5 %all-to-all-start.1 = ((bf16[32,40,1024]{2,1,0:T(8,128)(2,1)}), bf16[32,40,1024]{2,1,0:T(8,128)(2,1)}, u32[]{:S(2)}, u32[]{:S(2)}) async-start(bf16[32,40,1024]{2,1,0:T(8,128)(2,1)} %bitcast.33), calls=%async_computation.1 | async-start | bytes 5242880 | tf_op jit(solution)/shard_map/all_to_all | solution.py:490
  86.2 145.5 %copy-start = (f32[128,1024]{1,0:T(8,128)}, f32[128,1024]{1,0:T(8,128)S(1)}, u32[]{:S(2)}) copy-start(f32[128,1024]{1,0:T(8,128)S(1)} %get-tuple-element.88) | copy-start | bytes 1572868
  99.6 43.0 %all-to-all-start = ((bf16[32,40,1024]{2,1,0:T(8,128)(2,1)}), bf16[32,40,1024]{2,1,0:T(8,128)(2,1)}, u32[]{:S(2)}, u32[]{:S(2)}) async-start(bf16[32,40,1024]{2,1,0:T(8,128)(2,1)} %bitcast.156), calls=%async_computation | async-start | bytes 5242880 | tf_op jit(solution)/shard_map/all_to_all | solution.py:490
  106.0 3.5 collective-permute-start.1
  154.6 74.0 %all-to-all-start.2 = ((bf16[32,40,1024]{2,1,0:T(8,128)(2,1)}), bf16[32,40,1024]{2,1,0:T(8,128)(2,1)}, u32[]{:S(2)}, u32[]{:S(2)}) async-start(bf16[32,40,1024]{2,1,0:T(8,128)(2,1)} %bitcast.163), calls=%async_computation.2 | async-start | bytes 5242880 | tf_op jit(solution)/shard_map/all_to_all | solution.py:490
  164.5 64.1 %copy-start.16 = (pred[1280,128]{1,0:T(32,128)(4,1)S(1)}, pred[1280,128]{1,0:T(32,128)(4,1)}, u32[]{:S(2)}) copy-start(pred[1280,128]{1,0:T(32,128)(4,1)} %bitcast_compare_fusion) | copy-start | bytes 491524
  164.5 64.1 %copy-start.42 = (f32[1024,1]{0,1:T(1,128)S(1)}, f32[1024,1]{0,1:T(1,128)}, u32[]{:S(2)}) copy-start(f32[1024,1]{0,1:T(1,128)} %get-tuple-element.41) | copy-start | bytes 12292
  164.5 64.1 %copy-start.53 = (f32[128]{0:T(128)S(1)}, f32[128]{0:T(128)}, u32[]{:S(2)}) copy-start(f32[128]{0:T(128)} %copy-done.52) | copy-start | bytes 1540
  235.4 51.4 %all-to-all-start.3 = ((bf16[32,40,1024]{2,1,0:T(8,128)(2,1)}), bf16[32,40,1024]{2,1,0:T(8,128)(2,1)}, u32[]{:S(2)}, u32[]{:S(2)}) async-start(bf16[32,40,1024]{2,1,0:T(8,128)(2,1)} %bitcast.162), calls=%async_computation.3 | async-start | bytes 5242880 | tf_op jit(solution)/shard_map/all_to_all | solution.py:490
  253.1 27.6 %collective-permute-start.2 = (bf16[128,1024]{1,0:T(8,128)(2,1)S(1)}, bf16[128,1024]{1,0:T(8,128)(2,1)S(1)}, u32[]{:S(2)}, u32[]{:S(2)}) collective-permute-start(bf16[128,1024]{1,0:T(8,128)(2,1)S(1)} %pad_maximum_fusion.7), channel_id=1, source_target_pairs={{0,64},{64,0},{1,65},{65,1},{2,66},{66,2},{3,67},{67,3},{4,68},{68... | collective-permute-start | bytes 786440 | tf_op jit(solution)/shard_map/ppermute | solution.py:590
  253.7 33.2 %copy-start.5 = (bf16[1,128,1024]{2,1,0:T(8,128)(2,1)S(1)}, bf16[1,128,1024]{2,1,0:T(8,128)(2,1)}, u32[]{:S(2)}) copy-start(bf16[1,128,1024]{2,1,0:T(8,128)(2,1)} %param.12) | copy-start | bytes 786436
  253.7 33.2 %copy-start.48 = (f32[1024,1]{0,1:T(1,128)S(1)}, f32[1024,1]{0,1:T(1,128)}, u32[]{:S(2)}) copy-start(f32[1024,1]{0,1:T(1,128)} %copy-done.47) | copy-start | bytes 12292
  253.7 33.2 %copy-start.59 = (f32[128]{0:T(128)S(1)}, f32[128]{0:T(128)}, u32[]{:S(2)}) copy-start(f32[128]{0:T(128)} %copy-done.58) | copy-start | bytes 1540
  299.5 6.1 %collective-permute-start.3 = (bf16[512,3200]{1,0:T(8,128)(2,1)}, bf16[512,3200]{1,0:T(8,128)(2,1)S(1)}, u32[]{:S(2)}, u32[]{:S(2)}) collective-permute-start(bf16[512,3200]{1,0:T(8,128)(2,1)} %get-tuple-element.33), channel_id=1, source_target_pairs={{0,1},{1,0},{2,3},{3,2},{4,5},{5,4},{6,7},{7,6},{8,9},{9,8},{10,11... | collective-permute-start | bytes 9830408 | tf_op jit(solution)/shard_map/ppermute | solution.py:616
  313.9 55.7 %all-to-all-start.4 = ((bf16[32,16,3200]{2,1,0:T(8,128)(2,1)}), bf16[32,16,3200]{2,1,0:T(8,128)(2,1)S(1)}, u32[]{:S(2)}, u32[]{:S(2)}) async-start(bf16[32,16,3200]{2,1,0:T(8,128)(2,1)} %bitcast.155), calls=%async_computation.4 | async-start | bytes 6553600 | tf_op jit(solution)/shard_map/all_to_all | solution.py:617
  330.4 42.5 %copy-start.44 = (f32[1024,1]{0,1:T(1,128)S(1)}, f32[1024,1]{0,1:T(1,128)}, u32[]{:S(2)}) copy-start(f32[1024,1]{0,1:T(1,128)} %get-tuple-element.41) | copy-start | bytes 12292
  330.4 42.5 %copy-start.49 = (f32[1024,1]{0,1:T(1,128)S(1)}, f32[1024,1]{0,1:T(1,128)}, u32[]{:S(2)}) copy-start(f32[1024,1]{0,1:T(1,128)} %copy-done.47) | copy-start | bytes 12292
  330.4 42.5 %copy-start.55 = (f32[128]{0:T(128)S(1)}, f32[128]{0:T(128)}, u32[]{:S(2)}) copy-start(f32[128]{0:T(128)} %copy-done.52) | copy-start | bytes 1540
  330.4 42.5 %copy-start.60 = (f32[128]{0:T(128)S(1)}, f32[128]{0:T(128)}, u32[]{:S(2)}) copy-start(f32[128]{0:T(128)} %copy-done.58) | copy-start | bytes 1540
  370.0 6.8 %collective-permute-start.4 = (f32[16,3200]{1,0:T(8,128)S(1)}, f32[16,3200]{1,0:T(8,128)S(1)}, u32[]{:S(2)}, u32[]{:S(2)}) collective-permute-start(f32[16,3200]{1,0:T(8,128)S(1)} %convert_reduce_fusion), channel_id=1, source_target_pairs={{0,64},{64,0},{1,65},{65,1},{2,66},{66,2},{3,67},{67,3},{4,68},{68... | collective-permute-start | bytes 614408 | tf_op jit(solution)/shard_map/ppermute | solution.py:625
  (54 other events, 220.1 us)

commit v3 on v2

--- a/solution.py
+++ b/solution.py
@@ -170,8 +170,10 @@
     down_w_ref,
     out_ref,
     total_ref,
+    third_ref,
     theirs,
     came,
+    last,
     low,
     low_came,
     send_sem,
@@ -196,7 +198,7 @@
             device_id_type=MESH_ID,
         )
 
-    def unit_grads(block, kind, store):
+    def unit_grads(block, kind, target):
         if kind < 2:
             at = (2 * block + kind) * BLOCK
             left, right = (grads_ref, x_ref)
@@ -207,15 +209,17 @@
         @pl.loop(0, width // BLOCK)
         def _(n):
             columns = pl.ds(pl.multiple_of(n * BLOCK, BLOCK), BLOCK)
-            store[kind, :, columns] = dot(left[:, at : at + BLOCK], right[:, columns], TN)
+            target[:, columns] = dot(left[:, at : at + BLOCK], right[:, columns], TN)
 
     away = [send(k, theirs.at[k], came.at[k], partner) for k in range(3)]
-    across = [send(3 + k, low.at[k], low_came.at[k], mirror) for k in range(3)]
+    across = [send(3 + k, low.at[k], low_came.at[k], mirror) for k in range(2)]
+    mine = [total_ref.at[0], total_ref.at[1], last]
+    lows = [low.at[0], low.at[1], third_ref]
     for k in range(3):
-        unit_grads(1, k, theirs)
+        unit_grads(1, k, theirs.at[k])
         if k:
             away[k - 1].start()
-    unit_grads(0, 0, total_ref)
+    unit_grads(0, 0, mine[0])
     away[2].start()
 
     def join(k):
@@ -224,12 +228,12 @@
         @pl.loop(0, BLOCK // 32)
         def _(r):
             rows = pl.ds(pl.multiple_of(r * 32, 32), 32)
-            low[k, rows, :] = (total_ref[k, rows, :] + came[k, rows, :]).astype(bf16)
+            lows[k][rows, :] = (mine[k][rows, :] + came[k, rows, :]).astype(bf16)
 
     for k in range(3):
         join(k)
         if k < 2:
-            unit_grads(0, k + 1, total_ref)
+            unit_grads(0, k + 1, mine[k + 1])
             across[k].start()
 
     @pl.loop(0, x_ref.shape[0] // ROW_BLOCK)
@@ -242,11 +246,7 @@
             out = part if out is None else out + part
         out_ref[rows, :] = out.astype(bf16)
 
-        @pl.when(r == 0)
-        def _():
-            across[2].start()
-
-    for k in range(3):
+    for k in range(2):
         across[k].wait_recv()
 
         @pl.loop(0, BLOCK // 32)
@@ -263,18 +263,20 @@
     return pl.pallas_call(
         experts_second_body,
         in_specs=[pl.BlockSpec(memory_space=pltpu.VMEM)] * 5,
-        out_specs=[pl.BlockSpec(memory_space=pltpu.VMEM)] * 2,
+        out_specs=[pl.BlockSpec(memory_space=pltpu.VMEM)] * 3,
         out_shape=[
             jax.ShapeDtypeStruct((rows, width), bf16),
-            jax.ShapeDtypeStruct((3, BLOCK, width), f32),
+            jax.ShapeDtypeStruct((2, BLOCK, width), f32),
+            jax.ShapeDtypeStruct((BLOCK, width), bf16),
         ],
         scratch_shapes=[
             pltpu.VMEM((3, BLOCK, width), f32),
             pltpu.VMEM((3, BLOCK, width), f32),
-            pltpu.VMEM((3, BLOCK, width), bf16),
-            pltpu.VMEM((3, BLOCK, width), bf16),
-            pltpu.SemaphoreType.DMA((6,)),
-            pltpu.SemaphoreType.DMA((6,)),
+            pltpu.VMEM((BLOCK, width), f32),
+            pltpu.VMEM((2, BLOCK, width), bf16),
+            pltpu.VMEM((2, BLOCK, width), bf16),
+            pltpu.SemaphoreType.DMA((5,)),
+            pltpu.SemaphoreType.DMA((5,)),
         ],
         compiler_params=pltpu.CompilerParams(collective_id=1, has_side_effects=True),
         cost_estimate=pl.CostEstimate(
@@ -402,22 +404,24 @@
     return out.reshape(4 * RING * RING * rows, width)
 
 
-def projection_grads_body(mine_ref, sent_ref, gp_ref, gr_ref, gains_ref, total_ref, away_ref):
-    width = gp_ref.shape[1]
+def projection_grads_body(mine_ref, sent_ref, gq_ref, gkv_ref, gr_ref, gains_ref, total_ref, away_ref):
+    query = gq_ref.shape[1]
+    width = query + gkv_ref.shape[1]
     wide = width + gr_ref.shape[1]
     spread = lax.broadcasted_iota(jnp.int32, (8, 128), 0)
     lane = lax.broadcasted_iota(jnp.int32, (8, 128), 1)
     apart = ((spread == lane) & (spread < 6)).astype(bf16)
-    tokens = gp_ref.shape[0]
+    tokens = gq_ref.shape[0]
     for ref, out_ref, which in ((mine_ref, total_ref, 0), (sent_ref, away_ref, 1)):
-        out_ref[:, :width] = dot(ref[:tokens, :], gp_ref[...], TN).astype(out_ref.dtype)
-        out_ref[:, width:wide] = dot(ref[tokens:, :], gr_ref[...], TN).astype(out_ref.dtype)
+        out_ref[:, :query] = dot(ref[:tokens, :], gq_ref[...], TN).astype(out_ref.dtype)
+        out_ref[:, query:width] = dot(ref[: 2 * tokens, :], gkv_ref[...], TN).astype(out_ref.dtype)
+        out_ref[:, width:wide] = dot(ref[2 * tokens :, :], gr_ref[...], TN).astype(out_ref.dtype)
         out_ref[:, wide:] = dot(gains_ref[which], apart, TN).astype(out_ref.dtype)
 
 
-def projection_grads(rows_mine, rows_sent, grad_projected, grad_res_low, gains):
+def projection_grads(rows_mine, rows_sent, grad_query, grad_kv, grad_res_low, gains):
     count = rows_mine.shape[1]
-    width = grad_projected.shape[1] + grad_res_low.shape[1] + 128
+    width = grad_query.shape[1] + grad_kv.shape[1] + grad_res_low.shape[1] + 128
     tile = 128
     whole = lambda i: (0, 0)
     by_column = lambda i: (0, i)
@@ -428,7 +432,8 @@
         in_specs=[
             pl.BlockSpec((rows_mine.shape[0], tile), by_column),
             pl.BlockSpec((rows_sent.shape[0], tile), by_column),
-            pl.BlockSpec(grad_projected.shape, whole),
+            pl.BlockSpec(grad_query.shape, whole),
+            pl.BlockSpec(grad_kv.shape, whole),
             pl.BlockSpec(grad_res_low.shape, whole),
             pl.BlockSpec((2, 8, tile), lambda i: (0, 0, i)),
         ],
@@ -438,34 +443,246 @@
             jax.ShapeDtypeStruct((count, width), bf16),
         ],
         name="projection_grads",
-    )(rows_mine, rows_sent, grad_projected, grad_res_low, gains)
-
-
-def merge_halves_body(mine_ref, came_ref, out_ref):
-    wide = out_ref.shape[1] - 128
-    out_ref[:, :wide] = (mine_ref[:, :wide] + came_ref[:, :wide].astype(f32)).astype(bf16)
-    parts = mine_ref[:, wide:] + came_ref[:, wide:].astype(f32)
-    lane = lax.broadcasted_iota(jnp.int32, parts.shape, 1)
+    )(rows_mine, rows_sent, grad_query, grad_kv, grad_res_low, gains)
+
+
+def packed(values):
+    lane = lax.broadcasted_iota(jnp.int32, (values.shape[0], 128), 1)
+    wide = values.shape[1] - 128
+    parts = values[:, wide:]
     total = parts + pltpu.roll(parts, 126, 1) + pltpu.roll(parts, 124, 1)
     total = jnp.where(lane < 2, total, 0.0)
     one = total.astype(bf16).astype(f32)
     two = (total - one).astype(bf16).astype(f32)
     three = total - one - two
-    out_ref[:, wide:] = (one + pltpu.roll(two, 2, 1) + pltpu.roll(three, 4, 1)).astype(bf16)
-
-
-def merge_halves(mine, came):
-    rows, width = mine.shape
-    tile = 128
-    by_row = lambda i: (i, 0)
+    tail = one + pltpu.roll(two, 2, 1) + pltpu.roll(three, 4, 1)
+    return jnp.concatenate([values[:, :wide].astype(bf16), tail.astype(bf16)], axis=1)
+
+
+def reduce_body(
+    mine,
+    sent,
+    low,
+    total_ref,
+    unit_ref,
+    came,
+    acc,
+    stage,
+    in1,
+    in2,
+    stage_a,
+    in_a1,
+    in_a2,
+    stage_x,
+    in_x,
+    own,
+    in_own,
+    low_came,
+    chip_send,
+    chip_recv,
+    ring_send,
+    ring_recv,
+):
+    seq, chip, core = (lax.axis_index(name) for name in ("seq", "chip", "core"))
+    y, z, half = (chip // (2 * RING), (chip // 2) % RING, chip % 2)
+    flip = 1 - core
+    at_last = flip * y + core * z
+    at_first = flip * z + core * y
+
+    def device(to_y, to_z, to_half, to_core):
+        return (seq, (to_y * RING + to_z) * 2 + to_half, to_core)
+
+    def first(step):
+        return device((y + core * step) % RING, (z + flip * step) % RING, half, core)
+
+    def last(step):
+        return device((y + flip * step) % RING, (z + core * step) % RING, half, core)
+
+    partner = device(y, z, half, flip)
+    across = device(y, z, 1 - half, core)
+    mirror = (1 - seq, chip, core)
+    ahead, behind = (1, RING - 1)
+    barrier = pltpu.get_barrier_semaphore()
+    others = (partner, across, mirror, first(ahead), first(behind), last(ahead), last(behind))
+    for other in others:
+        pl.semaphore_signal(barrier, inc=1, device_id=other, device_id_type=MESH_ID)
+    pl.semaphore_wait(barrier, len(others))
+
+    def send(i, src, dst, to):
+        return pltpu.make_async_remote_copy(
+            src_ref=src,
+            dst_ref=dst,
+            send_sem=ring_send.at[i],
+            recv_sem=ring_recv.at[i],
+            device_id=to,
+            device_id_type=MESH_ID,
+        )
+
+    def on_chip(s, j, of_core):
+        line = ((1 - of_core) * y + of_core * z + s) % RING
+        a = (1 - of_core) * line + of_core * j
+        b = (1 - of_core) * j + of_core * line
+        return (
+            a,
+            b,
+            pltpu.make_async_remote_copy(
+                src_ref=sent.at[a, b],
+                dst_ref=came.at[a, b],
+                send_sem=chip_send.at[s, j],
+                recv_sem=chip_recv.at[s, j],
+                device_id=partner,
+                device_id_type=MESH_ID,
+            ),
+        )
+
+    order = (2, ahead, behind, 0)
+    two = RING // 2
+    units = send(12, low, low_came, mirror)
+    units.start()
+    for s in order:
+
+        @pl.loop(0, RING)
+        def _(j):
+            on_chip(s, j, flip)[2].start()
+
+    ring = [
+        send(0, stage.at[2, :two], in1.at[0], last(ahead)),
+        send(1, stage.at[2, two:], in1.at[1], last(behind)),
+        send(2, stage.at[1, two:], in2.at[0, two:], last(ahead)),
+        send(3, stage.at[1, :two], in2.at[0, :two], last(ahead)),
+        send(4, stage.at[3, :two], in2.at[1, :two], last(behind)),
+        send(5, stage.at[3, two:], in2.at[1, two:], last(behind)),
+        send(6, stage_a.at[2, 0], in_a1.at[0], first(ahead)),
+        send(7, stage_a.at[2, 1], in_a1.at[1], first(behind)),
+        send(8, stage_a.at[1], in_a2.at[0], first(ahead)),
+        send(9, stage_a.at[3], in_a2.at[1], first(behind)),
+        send(10, stage_x, in_x, across),
+        send(11, own, in_own, mirror),
+    ]
+
+    def merge(s, low_j, high_j, to_stage):
+        @pl.loop(low_j, high_j)
+        def _(j):
+            a, b, copy = on_chip(s, j, core)
+            copy.wait_recv()
+            for h in range(2):
+                value = mine[a, b, h] + came[a, b, h].astype(f32)
+                if to_stage:
+                    stage[s, j, h] = packed(value)
+                if not to_stage or s != 2:
+                    acc[s, j, h] = value
+
+    merge(2, 0, RING, True)
+    ring[0].start()
+    ring[1].start()
+    merge(ahead, 0, RING, True)
+    ring[2].start()
+    merge(behind, 0, RING, True)
+    ring[4].start()
+    merge(0, 0, RING, False)
+    for i, s, source, first_j in ((0, ahead, 0, 0), (1, behind, 1, two)):
+        ring[i].wait_recv()
+
+        @pl.loop(0, two)
+        def _(k):
+            for h in range(2):
+                value = acc[s, first_j + k, h] + in1[source, k, h].astype(f32)
+                stage[s, first_j + k, h] = packed(value)
+
+        ring[3 if i == 0 else 5].start()
+
+    for i, source, first_j in ((2, 0, two), (4, 1, 0), (3, 0, 0), (5, 1, two)):
+        ring[i].wait_recv()
+
+        @pl.loop(first_j, first_j + two)
+        def _(j):
+            for h in range(2):
+                acc[0, j, h] = acc[0, j, h] + in2[source, j, h].astype(f32)
+
+    def at(step):
+        return (at_first + step) % RING
+
+    for h in range(2):
+        stage_a[2, h] = packed(acc[0, at(2), h])
+    ring[6].start()
+    ring[7].start()
+    stage_a[1, 1] = packed(acc[0, at(ahead), 1])
+    stage_a[3, 0] = packed(acc[0, at(behind), 0])
+    ring[6].wait_recv()
+    stage_a[1, 0] = packed(acc[0, at(ahead), 0] + in_a1[0].astype(f32))
+    ring[8].start()
+    ring[7].wait_recv()
+    stage_a[3, 1] = packed(acc[0, at(behind), 1] + in_a1[1].astype(f32))
+    ring[9].start()
+    ring[8].wait_recv()
+    ring[9].wait_recv()
+    away = 1 - half
+    stage_x[...] = packed(
+        acc[0, at_first, away] + in_a2[0, away].astype(f32) + in_a2[1, away].astype(f32)
+    )
+    ring[10].start()
+    own[...] = acc[0, at_first, half] + in_a2[0, half].astype(f32) + in_a2[1, half].astype(f32)
+    ring[10].wait_recv()
+    own[...] = own[...] + in_x[...].astype(f32)
+    ring[11].start()
+    units.wait_recv()
+
+    @pl.loop(0, low.shape[0] // 32)
+    def _(r):
+        rows = pl.ds(pl.multiple_of(r * 32, 32), 32)
+        unit_ref[rows, :] = low[rows, :].astype(f32) + low_came[rows, :].astype(f32)
+
+    ring[11].wait_recv()
+    total_ref[...] = own[...] + in_own[...]
+    units.wait_send()
+    for copy in ring:
+        copy.wait_send()
+    for s in order:
+
+        @pl.loop(0, RING)
+        def _(j):
+            on_chip(s, j, flip)[2].wait_send()
+
+
+def reduce_grads(mine, sent, low):
+    width = mine.shape[1]
+    share = mine.shape[0] // (2 * RING * RING)
+    shape = (RING, RING, 2, share, width)
+    two = RING // 2
+    pair = (2, share, width)
     return pl.pallas_call(
-        merge_halves_body,
-        grid=(rows // tile,),
-        in_specs=[pl.BlockSpec((tile, width), by_row), pl.BlockSpec((tile, width), by_row)],
-        out_specs=pl.BlockSpec((tile, width), by_row),
-        out_shape=jax.ShapeDtypeStruct((rows, width), bf16),
-        name="merge_halves",
-    )(mine, came)
+        reduce_body,
+        in_specs=[pl.BlockSpec(memory_space=pltpu.VMEM)] * 3,
+        out_specs=[pl.BlockSpec(memory_space=pltpu.VMEM)] * 2,
+        out_shape=[
+            jax.ShapeDtypeStruct((share, width), f32),
+            jax.ShapeDtypeStruct(low.shape, f32),
+        ],
+        scratch_shapes=[
+            pltpu.VMEM(shape, bf16),
+            pltpu.VMEM(shape, f32),
+            pltpu.VMEM(shape, bf16),
+            pltpu.VMEM((2, two) + pair, bf16),
+            pltpu.VMEM((2, RING) + pair, bf16),
+            pltpu.VMEM((RING,) + pair, bf16),
+            pltpu.VMEM(pair, bf16),
+            pltpu.VMEM((2,) + pair, bf16),
+            pltpu.VMEM((share, width), bf16),
+            pltpu.VMEM((share, width), bf16),
+            pltpu.VMEM((share, width), f32),
+            pltpu.VMEM((share, width), f32),
+            pltpu.VMEM(low.shape, bf16),
+            pltpu.SemaphoreType.DMA((RING, RING)),
+            pltpu.SemaphoreType.DMA((RING, RING)),
+            pltpu.SemaphoreType.DMA((13,)),
+            pltpu.SemaphoreType.DMA((13,)),
+        ],
+        compiler_params=pltpu.CompilerParams(collective_id=2, has_side_effects=True),
+        cost_estimate=pl.CostEstimate(
+            flops=mine.size * 8, bytes_accessed=mine.size * 60, transcendentals=0
+        ),
+        name="reduce_grads",
+    )(mine.reshape(shape), sent.reshape(shape), low)
 
 
 def spread_plan(route_ids, mix_weights):
@@ -538,7 +755,7 @@
 
     row_values = own_low.astype(f32)
     normed_one, inverse_one = norm_forward(row_values, gain_one)
-    normed_other, _ = norm_forward(other_low.astype(f32), gain_one)
+    normed_other, inverse_other = norm_forward(other_low.astype(f32), gain_one)
     kv_w = in_full[:, query_width:]
     projected = dot(normed_one, in_full)
     projected_other = dot(normed_other, kv_w)
@@ -569,7 +786,7 @@
     arrived = exchange(dot(placed, normed_two).astype(bf16))
     hidden, grads, back = experts_first(arrived, grad_arrived, pre_w, down_w)
     grad_back = exchange(back)
-    out_rows, grad_units = experts_second(arrived, grad_arrived, hidden, grads, down_w)
+    out_rows, grad_units, third_low = experts_second(arrived, grad_arrived, hidden, grads, down_w)
     grad_back, out_rows = lax.optimization_barrier((grad_back, out_rows))
     returned = exchange(out_rows)
 
@@ -587,17 +804,17 @@
     grad_values = grad_values.reshape(2 * token_count, kv_width)
     away_keys = rotate_wide(grad_keys[token_count:], other_cos, other_sin, -1.0)
     away = jnp.concatenate([away_keys, grad_values[token_count:]], axis=1).astype(bf16)
-    came = lax.ppermute(away, "seq", SWAP).astype(f32)
-    grad_query = rotate_wide(grad_query, own_cos, own_sin, -1.0)
-    grad_keys = rotate_wide(grad_keys[:token_count], own_cos, own_sin, -1.0) + came[:, :kv_width]
-    grad_values = grad_values[:token_count] + came[:, kv_width:]
-    grad_projected = jnp.concatenate([grad_query, grad_keys, grad_values], axis=1).astype(bf16)
-    grad_projected, returned = lax.optimization_barrier((grad_projected, returned))
-    grad_normed_one = dot(grad_projected, in_full, NT)
-    grad_norm_one, gain_one_grad = norm_backward(row_values, inverse_one, gain_one, grad_normed_one)
-    grad_inputs = (grad_residual + grad_norm_one).astype(bf16)
-
-    owners = EXPERTS
+    came = lax.ppermute(away, "seq", SWAP)
+    grad_query = rotate_wide(grad_query, own_cos, own_sin, -1.0).astype(bf16)
+    grad_keys = rotate_wide(grad_keys[:token_count], own_cos, own_sin, -1.0)
+    grad_kv = jnp.concatenate([grad_keys, grad_values[:token_count]], axis=1).astype(bf16)
+    from_query = dot(grad_query, in_full[:, :query_width], NT)
+    from_kv = dot(jnp.concatenate([grad_kv, away], axis=0), kv_w, NT)
+    from_own = from_query + from_kv[:token_count]
+    other_values = other_low.astype(f32)
+    gain_one_grad = jnp.sum(from_own * row_values * inverse_one, axis=0)
+    gain_one_grad += jnp.sum(from_kv[token_count:] * other_values * inverse_other, axis=0)
+
     feature = jnp.arange(model_width)[:, None]
     slot = jnp.arange(model_width)[None, :]
     half_width = model_width // 2
@@ -605,26 +822,27 @@
     at = slot % half_width
     chosen_half = feature == (2 * (at // share) + of_core) * share + at % share
     chosen_half = chosen_half.astype(bf16)
-    features = dot(jnp.concatenate([normed_one, mixed], axis=0), chosen_half).astype(bf16)
+    features = jnp.concatenate([normed_one, normed_other, mixed], axis=0)
+    features = dot(features, chosen_half).astype(bf16)
     gain_pair = jnp.stack([gain_one_grad, gain_two_grad], axis=0)
     gain_parts = jnp.concatenate(three_parts(gain_pair) + (jnp.zeros_like(gain_pair, bf16),), axis=0)
     gain_parts = dot(gain_parts, chosen_half).astype(bf16)
     gain_parts = jnp.stack([gain_parts[:, :half_width], gain_parts[:, half_width:]], axis=0)
     grads_mine, grads_sent = projection_grads(
-        features[:, :half_width], features[:, half_width:], grad_projected, grad_res_low, gain_parts
+        features[:, :half_width],
+        features[:, half_width:],
+        grad_query,
+        jnp.concatenate([grad_kv, away], axis=0),
+        grad_res_low,
+        gain_parts,
     )
-    chip_rows = merge_halves(grads_mine, lax.ppermute(grads_sent, "core", SWAP))
-    landed = lax.all_to_all(
-        chip_rows.reshape(owners, share, wide + 128),
-        "chip",
-        split_axis=0,
-        concat_axis=0,
-        tiled=True,
-    )
-    totals = jnp.sum(landed.astype(f32), axis=0)
-    totals = totals + lax.ppermute(totals, "seq", SWAP)
+    totals, third_total = reduce_grads(grads_mine, grads_sent, third_low)
     gain_totals = totals[:, wide : wide + 2] + totals[:, wide + 2 : wide + 4]
     gain_totals = gain_totals + totals[:, wide + 4 : wide + 6]
+
+    grad_normed_one = from_own + dot(came, kv_w, NT)
+    grad_norm_one, _ = norm_backward(row_values, inverse_one, gain_one, grad_normed_one)
+    grad_inputs = (grad_residual + grad_norm_one).astype(bf16)
 
     mix = jnp.concatenate(mixers, axis=1)
     chosen = dot(mix, returned, TN).reshape(3, token_count, model_width)
@@ -639,7 +857,7 @@
         gain_totals[:, 1],
         grad_units[0],
         grad_units[1],
-        grad_units[2],
+        third_total,
     )
 
 

time: 381 us -> 325 us (0.85)
  waiting for transfers between devices: 125 us -> 44.2 us
  Pallas kernels: 132 us -> 161 us
  starting transfers between devices: 43 us -> 33.8 us
    pallas_call x1, Pallas kernels: 6.56 us -> 48.1 us  [reduce_grads(): pl.pallas_call(reduce_body, in_specs=[pl.BlockSpec(memory_space=pltpu.VME...]
    all_to_all x1 -> x0, waiting for transfers between devices: 39.1 us -> none  [on_device(): lax.all_to_all(chip_rows.reshape(owners, share, wide + 128), 'chip', spli...]
    ppermute x3 -> x1, waiting for transfers between devices: 35.4 us -> 0.01 us  [on_device(): came = lax.ppermute(away, 'seq', SWAP)]
    pallas_call x1, Pallas kernels: 64.1 us -> 50.5 us  [experts_second(): pl.pallas_call(experts_second_body, in_specs=[pl.BlockSpec(memory_space=p...]
    all_to_all x1 -> x0, starting transfers between devices: 7.24 us -> none  [on_device(): lax.all_to_all(chip_rows.reshape(owners, share, wide + 128), 'chip', spli...]
    all_to_all x4, waiting for transfers between devices: 47.4 us -> 40.8 us  [exchange(): lax.all_to_all(blocks, 'chip', split_axis=0, concat_axis=0, tiled=True)]
    dot_general x12 -> x14, matrix products: 29.7 us -> 31.7 us  [dot(): return lax.dot_general(a, b, dims, preferred_element_type=f32)]
  transfers between devices with their start and end apart: 10 -> 7, of which waited for: 8 -> 3; matrix products, arithmetic and copies ran while one was open for 15% -> 19% of each run, Pallas kernels for 28% -> 46%
where the time goes in v3:
time: 325 us; the launch traced here: 323 us
  Pallas kernels  161 us (50%)
  waiting for transfers between devices  44.2 us (14%)
  matrix products  36 us (11%)
  starting transfers between devices  33.8 us (10%)
  local copies, waits for them, and re-layouts  29.2 us (9%)
  other arithmetic  17.1 us (5%)
    pallas_call x1, Pallas kernels, experts_second(): pl.pallas_call(experts_second_body, in_specs=[pl.BlockSpec(memory_space=p...  50.5 us
    pallas_call x1, Pallas kernels, reduce_grads(): pl.pallas_call(reduce_body, in_specs=[pl.BlockSpec(memory_space=pltpu.VME...  48.1 us
    pallas_call x1, Pallas kernels, gather_weights(): pl.pallas_call(gather_body, out_shape=jax.ShapeDtypeStruct((RING, RING, 2...  43.7 us
    all_to_all x4, waiting for transfers between devices, exchange(): lax.all_to_all(blocks, 'chip', split_axis=0, concat_axis=0, tiled=True)  40.8 us
    all_to_all x4, starting transfers between devices, exchange(): lax.all_to_all(blocks, 'chip', split_axis=0, concat_axis=0, tiled=True)  31.9 us
    dot_general x14, matrix products, dot(): return lax.dot_general(a, b, dims, preferred_element_type=f32)  31.7 us
    pallas_call x1, Pallas kernels, experts_first(): pl.pallas_call(experts_first_body, grid=(rows // ROW_BLOCK,), in_specs=[p...  11.9 us
    optimization_barrier x1, local copies, waits for them, and re-layouts, on_device(): gathered, grad_rows = lax.optimization_barrier((gathered, grad_rows))  9.57 us
  transfers between devices with their start and end apart: 7, of which 3 were waited for; matrix products, arithmetic and copies ran while one was open for 19% of the time, Pallas kernels for 46%

profile of v3, /device:TPU:0, one launch (start us, length us, event | category | flops | bytes accessed | tf_op | source)
XLA Modules:
  0.0 322.7 jit_solution(1575733509780445632)
XLA Ops:
  5.4 43.7 %gather_weights.1 = bf16[4,4,2,2,16,3200]{5,4,3,2,1,0:T(8,128)(2,1)} custom-call(bf16[16,3200]{1,0:T(8,128)(2,1)} %concatenate.79.shard_ref), custom_call_target="tpu_custom_call" | custom-call | bytes 52428800 | tf_op jit(solution)/shard_map/gather_weights/pallas_call | solution.py:388
  49.8 2.4 multiply_convert_fusion
  52.2 7.4 %all-to-all-start.1 = ((bf16[32,40,1024]{2,1,0:T(8,128)(2,1)}), bf16[32,40,1024]{2,1,0:T(8,128)(2,1)}, u32[]{:S(2)}, u32[]{:S(2)}) async-start(bf16[32,40,1024]{2,1,0:T(8,128)(2,1)} %bitcast.31), calls=%async_computation.1 | async-start | bytes 5242880 | tf_op jit(solution)/shard_map/all_to_all | solution.py:707
  59.8 9.6 %copy.71 = bf16[1024,3200]{0,1:T(8,128)(2,1)} copy(bf16[1024,3200]{1,0:T(8,128)(2,1)} %bitcast.154) | data formatting | bytes 13107200 | tf_op jit(solution)/shard_map/optimization_barrier | solution.py:750
  73.9 3.1 fusion.2
  84.4 2.3 multiply_reduce_fusion.3
  86.7 2.4 convolution_convert_fusion
  89.1 10.9 %all-to-all-done.1 = bf16[32,40,1024]{2,1,0:T(8,128)(2,1)} async-done(((bf16[32,40,1024]{2,1,0:T(8,128)(2,1)}), bf16[32,40,1024]{2,1,0:T(8,128)(2,1)}, u32[]{:S(2)}, u32[]{:S(2)}) %all-to-all-start.1) | async-done | bytes 2621472 | tf_op jit(solution)/shard_map/all_to_all | solution.py:707
  100.0 4.8 %all-to-all-start = ((bf16[32,40,1024]{2,1,0:T(8,128)(2,1)}), bf16[32,40,1024]{2,1,0:T(8,128)(2,1)}, u32[]{:S(2)}, u32[]{:S(2)}) async-start(bf16[32,40,1024]{2,1,0:T(8,128)(2,1)} %bitcast.162), calls=%async_computation | async-start | bytes 5242880 | tf_op jit(solution)/shard_map/all_to_all | solution.py:707
  106.4 3.4 %collective-permute-done.1 = bf16[768,1024]{1,0:T(8,128)(2,1)S(1)} collective-permute-done((bf16[768,1024]{1,0:T(8,128)(2,1)S(1)}, bf16[768,1024]{1,0:T(8,128)(2,1)S(1)}, u32[]{:S(2)}, u32[]{:S(2)}) %collective-permute-start.1) | collective-permute-done | bytes 1572896 | tf_op jit(solution)/shard_map/ppermute | solution.py:738
  112.9 29.9 %all-to-all-done = bf16[32,40,1024]{2,1,0:T(8,128)(2,1)} async-done(((bf16[32,40,1024]{2,1,0:T(8,128)(2,1)}), bf16[32,40,1024]{2,1,0:T(8,128)(2,1)}, u32[]{:S(2)}, u32[]{:S(2)}) %all-to-all-start) | async-done | bytes 2621472 | tf_op jit(solution)/shard_map/all_to_all | solution.py:707
  142.9 11.9 %experts_first.1 = (bf16[1280,512]{1,0:T(8,128)(2,1)}, bf16[1280,1024]{1,0:T(8,128)(2,1)}, bf16[1280,1024]{1,0:T(8,128)(2,1)}) custom-call(bf16[1280,1024]{1,0:T(8,128)(2,1)} %bitcast.30.x_ref, bf16[1280,1024]{1,0:T(8,128)(2,1)} %bitcast.32.g_ref, bf16[1024,1024]{1,0:T(8,128)(2,1)} %pad_maximum_fusion.pre_w_ref, bf16[512,1024]{1,0:T(8,128)(2,1)} %pad_maximum_fusion.2.down_w_ref), custom_call_target="tpu_custom_call" | custom-call | flops 6710886400 | bytes 13107200 | tf_op jit(solution)/shard_map/experts_first/pallas_call | solution.py:137
  154.8 5.1 %all-to-all-start.2 = ((bf16[32,40,1024]{2,1,0:T(8,128)(2,1)}), bf16[32,40,1024]{2,1,0:T(8,128)(2,1)}, u32[]{:S(2)}, u32[]{:S(2)}) async-start(bf16[32,40,1024]{2,1,0:T(8,128)(2,1)} %bitcast.171), calls=%async_computation.2 | async-start | bytes 5242880 | tf_op jit(solution)/shard_map/all_to_all | solution.py:707
  165.7 50.5 %experts_second.1 = (bf16[1280,1024]{1,0:T(8,128)(2,1)}, f32[2,256,1024]{2,1,0:T(8,128)}, bf16[256,1024]{1,0:T(8,128)(2,1)}) custom-call(bf16[1280,1024]{1,0:T(8,128)(2,1)} %bitcast.30.x_ref, bf16[1280,1024]{1,0:T(8,128)(2,1)} %bitcast.32.g_ref, bf16[1280,512]{1,0:T(8,128)(2,1)} %get-tuple-element.26.hidden_ref, ...), custom_call_target="tpu_custom_call" | custom-call | flops 5368709120 | bytes 52428800 | tf_op jit(solution)/shard_map/experts_second/pallas_call | solution.py:263
  216.2 3.1 slice_bitcast_fusion
  219.3 3.0 multiply_reduce_fusion
  223.8 3.1 fusion.37
  232.9 14.6 %all-to-all-start.3 = ((bf16[32,40,1024]{2,1,0:T(8,128)(2,1)}), bf16[32,40,1024]{2,1,0:T(8,128)(2,1)}, u32[]{:S(2)}, u32[]{:S(2)}) async-start(bf16[32,40,1024]{2,1,0:T(8,128)(2,1)} %bitcast.170), calls=%async_computation.3 | async-start | bytes 5242880 | tf_op jit(solution)/shard_map/all_to_all | solution.py:707
  249.2 2.4 fusion.17
  251.8 2.4 fusion.33
  254.3 2.5 fusion.71
  258.3 6.3 %projection_grads.1 = (f32[512,3200]{1,0:T(8,128)}, bf16[512,3200]{1,0:T(8,128)(2,1)}) custom-call(bf16[384,512]{1,0:T(8,128)(2,1)} %get-tuple-element.48.mine_ref, bf16[384,512]{1,0:T(8,128)(2,1)} %get-tuple-element.47.sent_ref, bf16[128,1024]{1,0:T(8,128)(2,1)} %copy.88.gq_ref, bf16[256,1024]{1,0:T(8,128)(2,1)} %maximum_maximum_fusion.gkv_ref, ...), custom_call_target="tpu_custom_call" | custom-call | tf_op jit(solution)/shard_map/projection_grads/pallas_call | solution.py:429
  264.6 48.1 %reduce_grads.1 = (f32[16,3200]{1,0:T(8,128)}, f32[256,1024]{1,0:T(8,128)}) custom-call(f32[4,4,2,16,3200]{4,3,2,1,0:T(8,128)} %bitcast.163, bf16[4,4,2,16,3200]{4,3,2,1,0:T(8,128)(2,1)} %bitcast.169, bf16[256,1024]{1,0:T(8,128)(2,1)} %get-tuple-element.33.low), custom_call_target="tpu_custom_call" | custom-call | flops 13107200 | bytes 98304000 | tf_op jit(solution)/shard_map/reduce_grads/pallas_call | solution.py:653
  317.5 3.0 fusion.43
  (228 shorter events, 44.8 us)
Async XLA Ops:
  0.6 72.8 %collective-permute-start = (bf16[128,1024]{1,0:T(8,128)(2,1)}, bf16[128,1024]{1,0:T(8,128)(2,1)S(1)}, u32[]{:S(2)}, u32[]{:S(2)}) collective-permute-start(bf16[128,1024]{1,0:T(8,128)(2,1)} %bitcast.166), channel_id=1, source_target_pairs={{0,64},{64,0},{1,65},{65,1},{2,66},{66,2},{3,67},{67,3},{4,68},{68... | collective-permute-start | bytes 786440 | tf_op jit(solution)/shard_map/ppermute | solution.py:732
  5.4 43.7 %copy-start.49 = (s32[1,128,8]{1,2,0:T(8,128)S(1)}, s32[1,128,8]{1,2,0:T(8,128)}, u32[]{:S(2)}) copy-start(s32[1,128,8]{1,2,0:T(8,128)} %param.20) | copy-start | bytes 12292
  5.4 44.0 %copy-start.55 = (f32[1,128,8]{1,2,0:T(8,128)S(1)}, f32[1,128,8]{1,2,0:T(8,128)}, u32[]{:S(2)}) copy-start(f32[1,128,8]{1,2,0:T(8,128)} %param.21) | copy-start | bytes 12292
  5.4 44.4 %copy-start.3 = (bf16[1,128,1024]{2,1,0:T(8,128)(2,1)S(1)}, bf16[1,128,1024]{2,1,0:T(8,128)(2,1)}, u32[]{:S(2)}) copy-start(bf16[1,128,1024]{2,1,0:T(8,128)(2,1)} %param.23) | copy-start | bytes 786436
  49.2 22.5 %copy-start.20 = (s32[32,128]{1,0:T(8,128)}, s32[32,128]{1,0:T(8,128)S(1)}, u32[]{:S(2)}) copy-start(s32[32,128]{1,0:T(8,128)S(1)} %fusion.42) | copy-start | bytes 49156
  52.2 7.4 %copy-start = (bf16[1,128,1024]{2,1,0:T(8,128)(2,1)S(1)}, bf16[1,128,1024]{2,1,0:T(8,128)(2,1)}, u32[]{:S(2)}) copy-start(bf16[1,128,1024]{2,1,0:T(8,128)(2,1)} %param.12) | copy-start | bytes 786436
  52.2 47.8 %all-to-all-start.1 = ((bf16[32,40,1024]{2,1,0:T(8,128)(2,1)}), bf16[32,40,1024]{2,1,0:T(8,128)(2,1)}, u32[]{:S(2)}, u32[]{:S(2)}) async-start(bf16[32,40,1024]{2,1,0:T(8,128)(2,1)} %bitcast.31), calls=%async_computation.1 | async-start | bytes 5242880 | tf_op jit(solution)/shard_map/all_to_all | solution.py:707
  59.8 11.0 %copy-start.62 = (s32[1,256]{1,0:T(1,128)S(1)}, s32[1,256]{1,0:T(1,128)}, u32[]{:S(2)}) copy-start(s32[1,256]{1,0:T(1,128)} %param.22) | copy-start | bytes 3076
  70.8 6.2 %copy-start.47 = (f32[1024,1]{0,1:T(1,128)}, f32[1024,1]{0,1:T(1,128)S(1)}, u32[]{:S(2)}) copy-start(f32[1024,1]{0,1:T(1,128)S(1)} %get-tuple-element.44) | copy-start | bytes 12292
  70.8 6.2 %copy-start.56 = (f32[128]{0:T(128)}, f32[128]{0:T(128)S(1)}, u32[]{:S(2)}) copy-start(f32[128]{0:T(128)S(1)} %add_rsqrt_fusion.2) | copy-start | bytes 1540
  84.3 78.1 %copy-start.2 = (bf16[8,64,2,128]{3,1,2,0:T(8,128)(2,1)}, bf16[8,64,2,128]{3,1,2,0:T(8,128)(2,1)S(1)}, u32[]{:S(2)}) copy-start(bf16[8,64,2,128]{3,1,2,0:T(8,128)(2,1)S(1)} %convolution_convert_fusion.1) | copy-start | bytes 786436
  86.6 13.3 %copy-start.51 = (f32[128]{0:T(128)}, f32[128]{0:T(128)S(1)}, u32[]{:S(2)}) copy-start(f32[128]{0:T(128)S(1)} %add_rsqrt_fusion) | copy-start | bytes 1540
  100.0 42.9 %all-to-all-start = ((bf16[32,40,1024]{2,1,0:T(8,128)(2,1)}), bf16[32,40,1024]{2,1,0:T(8,128)(2,1)}, u32[]{:S(2)}, u32[]{:S(2)}) async-start(bf16[32,40,1024]{2,1,0:T(8,128)(2,1)} %bitcast.162), calls=%async_computation | async-start | bytes 5242880 | tf_op jit(solution)/shard_map/all_to_all | solution.py:707
  106.3 3.6 %copy-start.7 = (bf16[256,1024]{1,0:T(8,128)(2,1)S(1)}, bf16[256,1024]{1,0:T(8,128)(2,1)}, u32[]{:S(2)}) copy-start(bf16[256,1024]{1,0:T(8,128)(2,1)} %param.19) | copy-start | bytes 1572868
  106.3 3.5 %collective-permute-start.1 = (bf16[768,1024]{1,0:T(8,128)(2,1)S(1)}, bf16[768,1024]{1,0:T(8,128)(2,1)S(1)}, u32[]{:S(2)}, u32[]{:S(2)}) collective-permute-start(bf16[768,1024]{1,0:T(8,128)(2,1)S(1)} %pad_maximum_fusion.1), channel_id=1, source_target_pairs={{0,1},{1,0},{2,3},{3,2},{4,5},{5,4},{6,7},{7,6},{8,9},{9,8},{10,11... | collective-permute-start | bytes 4718600 | tf_op jit(solution)/shard_map/ppermute | solution.py:738
  154.8 5.2 %copy-start.21 = (s32[32,128]{1,0:T(8,128)S(1)}, s32[32,128]{1,0:T(8,128)}, u32[]{:S(2)}) copy-start(s32[32,128]{1,0:T(8,128)} %copy-done.20) | copy-start | bytes 49156
  154.8 5.2 %copy-start.33 = (f32[128,32]{0,1:T(8,128)S(1)}, f32[128,32]{0,1:T(8,128)}, u32[]{:S(2)}) copy-start(f32[128,32]{0,1:T(8,128)} %copy-done.32) | copy-start | bytes 49156
  154.8 5.2 %copy-start.44 = (s32[1280]{0:T(1024)S(1)}, s32[1280]{0:T(1024)}, u32[]{:S(2)}) copy-start(s32[1280]{0:T(1024)} %copy-done.43) | copy-start | bytes 15364
  154.8 64.5 %all-to-all-start.2 = ((bf16[32,40,1024]{2,1,0:T(8,128)(2,1)}), bf16[32,40,1024]{2,1,0:T(8,128)(2,1)}, u32[]{:S(2)}, u32[]{:S(2)}) async-start(bf16[32,40,1024]{2,1,0:T(8,128)(2,1)} %bitcast.171), calls=%async_computation.2 | async-start | bytes 5242880 | tf_op jit(solution)/shard_map/all_to_all | solution.py:707
  232.8 21.4 %collective-permute-start.2 = (bf16[128,1024]{1,0:T(8,128)(2,1)S(1)}, bf16[128,1024]{1,0:T(8,128)(2,1)S(1)}, u32[]{:S(2)}, u32[]{:S(2)}) collective-permute-start(bf16[128,1024]{1,0:T(8,128)(2,1)S(1)} %pad_maximum_fusion.5), channel_id=1, source_target_pairs={{0,64},{64,0},{1,65},{65,1},{2,66},{66,2},{3,67},{67,3},{4,68},{68... | collective-permute-start | bytes 786440 | tf_op jit(solution)/shard_map/ppermute | solution.py:807
  232.9 84.5 %all-to-all-start.3 = ((bf16[32,40,1024]{2,1,0:T(8,128)(2,1)}), bf16[32,40,1024]{2,1,0:T(8,128)(2,1)}, u32[]{:S(2)}, u32[]{:S(2)}) async-start(bf16[32,40,1024]{2,1,0:T(8,128)(2,1)} %bitcast.170), calls=%async_computation.3 | async-start | bytes 5242880 | tf_op jit(solution)/shard_map/all_to_all | solution.py:707
  264.6 52.8 %copy-start.17 = (bf16[1280,128]{1,0:T(8,128)(2,1)S(1)}, bf16[1280,128]{1,0:T(8,128)(2,1)}, u32[]{:S(2)}) copy-start(bf16[1280,128]{1,0:T(8,128)(2,1)} %get-tuple-element.67) | copy-start | bytes 983044
  264.6 52.8 %copy-start.18 = (bf16[1280,128]{1,0:T(8,128)(2,1)S(1)}, bf16[1280,128]{1,0:T(8,128)(2,1)}, u32[]{:S(2)}) copy-start(bf16[1280,128]{1,0:T(8,128)(2,1)} %get-tuple-element.68) | copy-start | bytes 983044
  264.6 52.8 %copy-start.19 = (bf16[1280,128]{1,0:T(8,128)(2,1)S(1)}, bf16[1280,128]{1,0:T(8,128)(2,1)}, u32[]{:S(2)}) copy-start(bf16[1280,128]{1,0:T(8,128)(2,1)} %get-tuple-element.69) | copy-start | bytes 983044
  (47 other events, 99.4 us)

commit v4 on v3

--- a/solution.py
+++ b/solution.py
@@ -170,7 +170,7 @@
     down_w_ref,
     out_ref,
     total_ref,
-    third_ref,
+    rest_ref,
     theirs,
     came,
     last,
@@ -212,9 +212,9 @@
             target[:, columns] = dot(left[:, at : at + BLOCK], right[:, columns], TN)
 
     away = [send(k, theirs.at[k], came.at[k], partner) for k in range(3)]
-    across = [send(3 + k, low.at[k], low_came.at[k], mirror) for k in range(2)]
-    mine = [total_ref.at[0], total_ref.at[1], last]
-    lows = [low.at[0], low.at[1], third_ref]
+    across = [send(3 + k, low.at[k], low_came.at[k], mirror) for k in range(1)]
+    mine = [total_ref, last.at[0], last.at[1]]
+    lows = [low.at[0], rest_ref.at[0], rest_ref.at[1]]
     for k in range(3):
         unit_grads(1, k, theirs.at[k])
         if k:
@@ -234,6 +234,7 @@
         join(k)
         if k < 2:
             unit_grads(0, k + 1, mine[k + 1])
+        if k < len(across):
             across[k].start()
 
     @pl.loop(0, x_ref.shape[0] // ROW_BLOCK)
@@ -246,13 +247,13 @@
             out = part if out is None else out + part
         out_ref[rows, :] = out.astype(bf16)
 
-    for k in range(2):
+    for k in range(len(across)):
         across[k].wait_recv()
 
         @pl.loop(0, BLOCK // 32)
         def _(r):
             rows = pl.ds(pl.multiple_of(r * 32, 32), 32)
-            total_ref[k, rows, :] = low[k, rows, :].astype(f32) + low_came[k, rows, :].astype(f32)
+            mine[k][rows, :] = low[k, rows, :].astype(f32) + low_came[k, rows, :].astype(f32)
 
     for copy in away + across:
         copy.wait_send()
@@ -266,17 +267,17 @@
         out_specs=[pl.BlockSpec(memory_space=pltpu.VMEM)] * 3,
         out_shape=[
             jax.ShapeDtypeStruct((rows, width), bf16),
-            jax.ShapeDtypeStruct((2, BLOCK, width), f32),
-            jax.ShapeDtypeStruct((BLOCK, width), bf16),
+            jax.ShapeDtypeStruct((BLOCK, width), f32),
+            jax.ShapeDtypeStruct((2, BLOCK, width), bf16),
         ],
         scratch_shapes=[
             pltpu.VMEM((3, BLOCK, width), f32),
             pltpu.VMEM((3, BLOCK, width), f32),
-            pltpu.VMEM((BLOCK, width), f32),
-            pltpu.VMEM((2, BLOCK, width), bf16),
-            pltpu.VMEM((2, BLOCK, width), bf16),
-            pltpu.SemaphoreType.DMA((5,)),
-            pltpu.SemaphoreType.DMA((5,)),
+            pltpu.VMEM((2, BLOCK, width), f32),
+            pltpu.VMEM((1, BLOCK, width), bf16),
+            pltpu.VMEM((1, BLOCK, width), bf16),
+            pltpu.SemaphoreType.DMA((4,)),
+            pltpu.SemaphoreType.DMA((4,)),
         ],
         compiler_params=pltpu.CompilerParams(collective_id=1, has_side_effects=True),
         cost_estimate=pl.CostEstimate(
@@ -302,7 +303,7 @@
         return device((y + (1 - core) * step) % RING, (z + core * step) % RING, half, core)
 
     partner = device(y, z, half, 1 - core)
-    across = device(y, z, 1 - half, core)
+    across = (1 - seq, chip + 1 - 2 * half, core)
     ahead, behind = (1, RING - 1)
     barrier = pltpu.get_barrier_semaphore()
     for other in (partner, across, first(ahead), first(behind), last(ahead), last(behind)):
@@ -319,17 +320,10 @@
             device_id_type=MESH_ID,
         )
 
-    def line(c, step, part=None):
-        cut = slice(None) if part is None else pl.ds(part * (RING // 2), RING // 2)
-        if c == 0:
-            return out_ref.at[(y + step) % RING, cut, :, 0]
-        return out_ref.at[cut, (z + step) % RING, :, 1]
-
-    def pair(c, step, part=None):
+    def pair(c, f, l, part=None):
         cut = slice(None) if part is None else part
-        if c == 0:
-            return out_ref.at[y, (z + step) % RING, cut, 0]
-        return out_ref.at[(y + step) % RING, z, cut, 1]
+        to_y, to_z = (l, f) if c == 0 else (f, l)
+        return out_ref.at[(y + to_y) % RING, (z + to_z) % RING, cut, c]
 
     def run(c):
         sent = []
@@ -341,6 +335,19 @@
 
         def arrive(i, region):
             send(i, region, region, partner).wait_recv()
+
+        def spread(f):
+            go(5 + 2 * f, pair(c, f, 0), last(ahead))
+            go(6 + 2 * f, pair(c, f, 0), last(behind))
+            go(21 + 5 * f, pair(c, f, 0), partner)
+
+        def relay(f):
+            arrive(5 + 2 * f, pair(c, f, behind))
+            go(13 + 2 * f, pair(c, f, behind, 0), last(ahead))
+            go(22 + 5 * f, pair(c, f, behind), partner)
+            arrive(6 + 2 * f, pair(c, f, ahead))
+            go(14 + 2 * f, pair(c, f, ahead, 1), last(behind))
+            go(23 + 5 * f, pair(c, f, ahead), partner)
 
         own = out_ref.at[y, z, half, c]
         copy = send(0, shard_ref, own, across)
@@ -350,32 +357,31 @@
         local.start()
         local.wait()
         arrive(0, out_ref.at[y, z, 1 - half, c])
-        go(1, pair(c, 0), first(ahead))
-        go(2, pair(c, 0), first(behind))
-        arrive(1, pair(c, behind))
-        go(3, pair(c, behind, 0), first(ahead))
-        arrive(2, pair(c, ahead))
-        go(4, pair(c, ahead, 1), first(behind))
-        arrive(3, pair(c, 2, 0))
-        arrive(4, pair(c, 2, 1))
-        go(5, line(c, 0), last(ahead))
-        go(6, line(c, 0), last(behind))
-        go(9, line(c, 0), partner)
-        arrive(5, line(c, behind))
-        go(7, line(c, behind, 0), last(ahead))
-        go(10, line(c, behind), partner)
-        arrive(6, line(c, ahead))
-        go(8, line(c, ahead, 1), last(behind))
-        go(11, line(c, ahead), partner)
-        arrive(7, line(c, 2, 0))
-        go(12, line(c, 2, 0), partner)
-        arrive(8, line(c, 2, 1))
-        go(13, line(c, 2, 1), partner)
-        arrive(9, line(1 - c, 0))
-        arrive(10, line(1 - c, behind))
-        arrive(11, line(1 - c, ahead))
-        arrive(12, line(1 - c, 2, 0))
-        arrive(13, line(1 - c, 2, 1))
+        go(1, pair(c, 0, 0), first(ahead))
+        go(2, pair(c, 0, 0), first(behind))
+        spread(0)
+        arrive(1, pair(c, behind, 0))
+        go(3, pair(c, behind, 0, 0), first(ahead))
+        spread(behind)
+        arrive(2, pair(c, ahead, 0))
+        go(4, pair(c, ahead, 0, 1), first(behind))
+        spread(ahead)
+        relay(0)
+        arrive(3, pair(c, 2, 0, 0))
+        arrive(4, pair(c, 2, 0, 1))
+        spread(2)
+        for f in (behind, ahead, 2):
+            relay(f)
+        for f in (0, behind, ahead, 2):
+            for part in range(2):
+                arrive(13 + 2 * f + part, pair(c, f, 2, part))
+                go(24 + 5 * f + part, pair(c, f, 2, part), partner)
+        for f in (0, behind, ahead, 2):
+            arrive(21 + 5 * f, pair(1 - c, f, 0))
+            arrive(22 + 5 * f, pair(1 - c, f, behind))
+            arrive(23 + 5 * f, pair(1 - c, f, ahead))
+            for part in range(2):
+                arrive(24 + 5 * f + part, pair(1 - c, f, 2, part))
         for copy in sent:
             copy.wait_send()
 
@@ -391,8 +397,8 @@
         in_specs=[pl.BlockSpec(memory_space=pltpu.VMEM)],
         out_specs=pl.BlockSpec(memory_space=pl.ANY),
         scratch_shapes=[
-            pltpu.SemaphoreType.DMA((14,)),
-            pltpu.SemaphoreType.DMA((14,)),
+            pltpu.SemaphoreType.DMA((41,)),
+            pltpu.SemaphoreType.DMA((41,)),
             pltpu.SemaphoreType.DMA,
         ],
         compiler_params=pltpu.CompilerParams(collective_id=0, has_side_effects=True),
@@ -463,8 +469,11 @@
     mine,
     sent,
     low,
-    total_ref,
-    unit_ref,
+    in_ref,
+    out_ref,
+    gain_ref,
+    up_ref,
+    down_ref,
     came,
     acc,
     stage,
@@ -627,13 +636,19 @@
     ring[11].start()
     units.wait_recv()
 
-    @pl.loop(0, low.shape[0] // 32)
+    @pl.loop(0, low.shape[1] // 32)
     def _(r):
         rows = pl.ds(pl.multiple_of(r * 32, 32), 32)
-        unit_ref[rows, :] = low[rows, :].astype(f32) + low_came[rows, :].astype(f32)
+        up_ref[rows, :] = low[0, rows, :].astype(f32) + low_came[0, rows, :].astype(f32)
+        down_ref[rows, :] = low[1, rows, :].astype(f32) + low_came[1, rows, :].astype(f32)
 
     ring[11].wait_recv()
-    total_ref[...] = own[...] + in_own[...]
+    total = own[...] + in_own[...]
+    cut = in_ref.shape[1]
+    wide = cut + out_ref.shape[1]
+    in_ref[...] = total[:, :cut]
+    out_ref[...] = total[:, cut:wide]
+    gain_ref[...] = total[:, wide:]
     units.wait_send()
     for copy in ring:
         copy.wait_send()
@@ -644,7 +659,7 @@
             on_chip(s, j, flip)[2].wait_send()
 
 
-def reduce_grads(mine, sent, low):
+def reduce_grads(mine, sent, low, cut):
     width = mine.shape[1]
     share = mine.shape[0] // (2 * RING * RING)
     shape = (RING, RING, 2, share, width)
@@ -653,10 +668,13 @@
     return pl.pallas_call(
         reduce_body,
         in_specs=[pl.BlockSpec(memory_space=pltpu.VMEM)] * 3,
-        out_specs=[pl.BlockSpec(memory_space=pltpu.VMEM)] * 2,
+        out_specs=[pl.BlockSpec(memory_space=pltpu.VMEM)] * 5,
         out_shape=[
-            jax.ShapeDtypeStruct((share, width), f32),
-            jax.ShapeDtypeStruct(low.shape, f32),
+            jax.ShapeDtypeStruct((share, cut), f32),
+            jax.ShapeDtypeStruct((share, width - cut - 128), f32),
+            jax.ShapeDtypeStruct((share, 128), f32),
+            jax.ShapeDtypeStruct(low.shape[1:], f32),
+            jax.ShapeDtypeStruct(low.shape[1:], f32),
         ],
         scratch_shapes=[
             pltpu.VMEM(shape, bf16),
@@ -786,7 +804,7 @@
     arrived = exchange(dot(placed, normed_two).astype(bf16))
     hidden, grads, back = experts_first(arrived, grad_arrived, pre_w, down_w)
     grad_back = exchange(back)
-    out_rows, grad_units, third_low = experts_second(arrived, grad_arrived, hidden, grads, down_w)
+    out_rows, gate_total, rest_low = experts_second(arrived, grad_arrived, hidden, grads, down_w)
     grad_back, out_rows = lax.optimization_barrier((grad_back, out_rows))
     returned = exchange(out_rows)
 
@@ -836,10 +854,13 @@
         grad_res_low,
         gain_parts,
     )
-    totals, third_total = reduce_grads(grads_mine, grads_sent, third_low)
-    gain_totals = totals[:, wide : wide + 2] + totals[:, wide + 2 : wide + 4]
-    gain_totals = gain_totals + totals[:, wide + 4 : wide + 6]
-
+    in_width = query_width + 2 * kv_width
+    in_total, out_total, gain_total, up_total, down_total = reduce_grads(
+        grads_mine, grads_sent, rest_low, in_width
+    )
+    gain_total = gain_total[:, :2] + gain_total[:, 2:4] + gain_total[:, 4:6]
+
+    came, gain_total = lax.optimization_barrier((came, gain_total))
     grad_normed_one = from_own + dot(came, kv_w, NT)
     grad_norm_one, _ = norm_backward(row_values, inverse_one, gain_one, grad_normed_one)
     grad_inputs = (grad_residual + grad_norm_one).astype(bf16)
@@ -847,17 +868,16 @@
     mix = jnp.concatenate(mixers, axis=1)
     chosen = dot(mix, returned, TN).reshape(3, token_count, model_width)
     output = (residual + (chosen[2] + chosen[1] + chosen[0])).astype(bf16)
-    in_width = query_width + 2 * kv_width
     return (
         output.reshape(1, token_count, model_width),
         grad_inputs.reshape(1, token_count, model_width),
-        totals[:, :in_width],
-        totals[:, in_width:wide],
-        gain_totals[:, 0],
-        gain_totals[:, 1],
-        grad_units[0],
-        grad_units[1],
-        third_total,
+        in_total,
+        out_total,
+        gain_total[:, 0],
+        gain_total[:, 1],
+        gate_total,
+        up_total,
+        down_total,
     )
 
 

time: 325 us -> 306 us (0.942)
  Pallas kernels: 161 us -> 145 us
    pallas_call x1, Pallas kernels: 43.7 us -> 34 us  [gather_weights(): pl.pallas_call(gather_body, out_shape=jax.ShapeDtypeStruct((RING, RING, 2...]
    pallas_call x1, Pallas kernels: 50.5 us -> 41.2 us  [experts_second(): pl.pallas_call(experts_second_body, in_specs=[pl.BlockSpec(memory_space=p...]
    pallas_call x1, Pallas kernels: 48.1 us -> 51.7 us  [reduce_grads(): pl.pallas_call(reduce_body, in_specs=[pl.BlockSpec(memory_space=pltpu.VME...]
    unnamed x129 -> x135, local copies, waits for them, and re-layouts: 3.76 us -> 6.96 us
  transfers between devices with their start and end apart: 7 -> 7, of which waited for: 3 -> 3; matrix products, arithmetic and copies ran while one was open for 19% -> 18% of each run, Pallas kernels for 46% -> 44%
where the time goes in v4:
time: 306 us; the launch traced here: 305 us
  Pallas kernels  145 us (47%)
  waiting for transfers between devices  45.6 us (15%)
  matrix products  36.3 us (12%)
  starting transfers between devices  31.9 us (10%)
  local copies, waits for them, and re-layouts  26.3 us (9%)
  other arithmetic  17.4 us (6%)
    pallas_call x1, Pallas kernels, reduce_grads(): pl.pallas_call(reduce_body, in_specs=[pl.BlockSpec(memory_space=pltpu.VME...  51.7 us
    all_to_all x4, waiting for transfers between devices, exchange(): lax.all_to_all(blocks, 'chip', split_axis=0, concat_axis=0, tiled=True)  42.2 us
    pallas_call x1, Pallas kernels, experts_second(): pl.pallas_call(experts_second_body, in_specs=[pl.BlockSpec(memory_space=p...  41.2 us
    pallas_call x1, Pallas kernels, gather_weights(): pl.pallas_call(gather_body, out_shape=jax.ShapeDtypeStruct((RING, RING, 2...  34 us
    dot_general x14, matrix products, dot(): return lax.dot_general(a, b, dims, preferred_element_type=f32)  31.8 us
    all_to_all x4, starting transfers between devices, exchange(): lax.all_to_all(blocks, 'chip', split_axis=0, concat_axis=0, tiled=True)  30.1 us
    pallas_call x1, Pallas kernels, experts_first(): pl.pallas_call(experts_first_body, grid=(rows // ROW_BLOCK,), in_specs=[p...  11.9 us
    optimization_barrier x1, local copies, waits for them, and re-layouts, on_device(): gathered, grad_rows = lax.optimization_barrier((gathered, grad_rows))  9.6 us
  transfers between devices with their start and end apart: 7, of which 3 were waited for; matrix products, arithmetic and copies ran while one was open for 18% of the time, Pallas kernels for 44%

profile of v4, /device:TPU:0, one launch (start us, length us, event | category | flops | bytes accessed | tf_op | source)
XLA Modules:
  0.0 304.6 jit_solution(18439760452072975682)
XLA Ops:
  5.4 34.0 %gather_weights.1 = bf16[4,4,2,2,16,3200]{5,4,3,2,1,0:T(8,128)(2,1)} custom-call(bf16[16,3200]{1,0:T(8,128)(2,1)} %concatenate.79.shard_ref), custom_call_target="tpu_custom_call" | custom-call | bytes 52428800 | tf_op jit(solution)/shard_map/gather_weights/pallas_call | solution.py:394
  40.1 2.3 multiply_convert_fusion
  42.4 6.1 %all-to-all-start.1 = ((bf16[32,40,1024]{2,1,0:T(8,128)(2,1)}), bf16[32,40,1024]{2,1,0:T(8,128)(2,1)}, u32[]{:S(2)}, u32[]{:S(2)}) async-start(bf16[32,40,1024]{2,1,0:T(8,128)(2,1)} %bitcast.31), calls=%async_computation.1 | async-start | bytes 5242880 | tf_op jit(solution)/shard_map/all_to_all | solution.py:725
  48.7 9.6 %copy.71 = bf16[1024,3200]{0,1:T(8,128)(2,1)} copy(bf16[1024,3200]{1,0:T(8,128)(2,1)} %bitcast.150) | data formatting | bytes 13107200 | tf_op jit(solution)/shard_map/optimization_barrier | solution.py:768
  62.7 3.1 %fusion.2 = f32[128,2048]{1,0:T(8,128)S(1)} fusion(bf16[128,1024]{1,0:T(8,128)(2,1)S(1)} %get-tuple-element.82, bf16[1024,3200]{1,0:T(8,128)(2,1)} %bitcast.151), kind=kOutput, calls=%fused_computation.4 | convolution fusion | flops 536870912 | bytes 5505024 | tf_op jit(solution)/shard_map/dot_general | solution.py:33
  71.8 2.3 multiply_reduce_fusion.3
  74.2 2.4 convolution_convert_fusion
  76.6 12.3 %all-to-all-done.1 = bf16[32,40,1024]{2,1,0:T(8,128)(2,1)} async-done(((bf16[32,40,1024]{2,1,0:T(8,128)(2,1)}), bf16[32,40,1024]{2,1,0:T(8,128)(2,1)}, u32[]{:S(2)}, u32[]{:S(2)}) %all-to-all-start.1) | async-done | bytes 2621472 | tf_op jit(solution)/shard_map/all_to_all | solution.py:725
  88.9 4.8 %all-to-all-start = ((bf16[32,40,1024]{2,1,0:T(8,128)(2,1)}), bf16[32,40,1024]{2,1,0:T(8,128)(2,1)}, u32[]{:S(2)}, u32[]{:S(2)}) async-start(bf16[32,40,1024]{2,1,0:T(8,128)(2,1)} %bitcast.158), calls=%async_computation | async-start | bytes 5242880 | tf_op jit(solution)/shard_map/all_to_all | solution.py:725
  95.4 3.4 %collective-permute-done.1 = bf16[768,1024]{1,0:T(8,128)(2,1)S(1)} collective-permute-done((bf16[768,1024]{1,0:T(8,128)(2,1)S(1)}, bf16[768,1024]{1,0:T(8,128)(2,1)S(1)}, u32[]{:S(2)}, u32[]{:S(2)}) %collective-permute-start.1) | collective-permute-done | bytes 1572896 | tf_op jit(solution)/shard_map/ppermute | solution.py:756
  101.9 29.9 %all-to-all-done = bf16[32,40,1024]{2,1,0:T(8,128)(2,1)} async-done(((bf16[32,40,1024]{2,1,0:T(8,128)(2,1)}), bf16[32,40,1024]{2,1,0:T(8,128)(2,1)}, u32[]{:S(2)}, u32[]{:S(2)}) %all-to-all-start) | async-done | bytes 2621472 | tf_op jit(solution)/shard_map/all_to_all | solution.py:725
  131.8 11.9 %experts_first.1 = (bf16[1280,512]{1,0:T(8,128)(2,1)}, bf16[1280,1024]{1,0:T(8,128)(2,1)}, bf16[1280,1024]{1,0:T(8,128)(2,1)}) custom-call(bf16[1280,1024]{1,0:T(8,128)(2,1)} %bitcast.30.x_ref, bf16[1280,1024]{1,0:T(8,128)(2,1)} %bitcast.32.g_ref, bf16[1024,1024]{1,0:T(8,128)(2,1)} %pad_maximum_fusion.pre_w_ref, bf16[512,1024]{1,0:T(8,128)(2,1)} %pad_maximum_fusion.2.down_w_ref), custom_call_target="tpu_custom_call" | custom-call | flops 6710886400 | bytes 13107200 | tf_op jit(solution)/shard_map/experts_first/pallas_call | solution.py:137
  143.7 5.1 %all-to-all-start.2 = ((bf16[32,40,1024]{2,1,0:T(8,128)(2,1)}), bf16[32,40,1024]{2,1,0:T(8,128)(2,1)}, u32[]{:S(2)}, u32[]{:S(2)}) async-start(bf16[32,40,1024]{2,1,0:T(8,128)(2,1)} %bitcast.167), calls=%async_computation.2 | async-start | bytes 5242880 | tf_op jit(solution)/shard_map/all_to_all | solution.py:725
  151.6 2.1 fusion.21
  154.7 41.2 %experts_second.1 = (bf16[1280,1024]{1,0:T(8,128)(2,1)}, f32[256,1024]{1,0:T(8,128)}, bf16[2,256,1024]{2,1,0:T(8,128)(2,1)}) custom-call(bf16[1280,1024]{1,0:T(8,128)(2,1)} %bitcast.30.x_ref, bf16[1280,1024]{1,0:T(8,128)(2,1)} %bitcast.32.g_ref, bf16[1280,512]{1,0:T(8,128)(2,1)} %get-tuple-element.31.hidden_ref, ...), custom_call_target="tpu_custom_call" | custom-call | flops 5368709120 | bytes 52428800 | tf_op jit(solution)/shard_map/experts_second/pallas_call | solution.py:264
  195.9 3.0 multiply_reduce_fusion
  201.3 3.1 %fusion.37 = bf16[128,1024]{1,0:T(8,128)(2,1)} fusion(bf16[128,1024]{1,0:T(8,128)(2,1)S(1)} %fusion.111.gr_ref, bf16[1024,3200]{1,0:T(8,128)(2,1)} %bitcast.154), kind=kOutput, calls=%fused_computation.41 | convolution fusion | flops 268566528 | bytes 2621440 | tf_op jit(solution)/shard_map/dot_general | solution.py:33
  211.5 14.0 %all-to-all-start.3 = ((bf16[32,40,1024]{2,1,0:T(8,128)(2,1)}), bf16[32,40,1024]{2,1,0:T(8,128)(2,1)}, u32[]{:S(2)}, u32[]{:S(2)}) async-start(bf16[32,40,1024]{2,1,0:T(8,128)(2,1)} %bitcast.166), calls=%async_computation.3 | async-start | bytes 5242880 | tf_op jit(solution)/shard_map/all_to_all | solution.py:725
  225.6 2.4 fusion.17
  228.2 2.5 fusion.70
  233.8 6.3 %projection_grads.1 = (f32[512,3200]{1,0:T(8,128)}, bf16[512,3200]{1,0:T(8,128)(2,1)}) custom-call(bf16[384,512]{1,0:T(8,128)(2,1)} %get-tuple-element.54.mine_ref, bf16[384,512]{1,0:T(8,128)(2,1)} %get-tuple-element.53.sent_ref, bf16[128,1024]{1,0:T(8,128)(2,1)} %copy.88.gq_ref, bf16[256,1024]{1,0:T(8,128)(2,1)} %maximum_maximum_fusion.gkv_ref, ...), custom_call_target="tpu_custom_call" | custom-call | tf_op jit(solution)/shard_map/projection_grads/pallas_call | solution.py:435
  240.1 51.7 %reduce_grads.1 = (f32[16,2048]{1,0:T(8,128)}, f32[16,1024]{1,0:T(8,128)}, f32[16,128]{1,0:T(8,128)}, f32[256,1024]{1,0:T(8,128)}, f32[256,1024]{1,0:T(8,128)}) custom-call(f32[4,4,2,16,3200]{4,3,2,1,0:T(8,128)} %bitcast.160, bf16[4,4,2,16,3200]{4,3,2,1,0:T(8,128)(2,1)} %bitcast.165, bf16[2,256,1024]{2,1,0:T(8,128)(2,1)} %get-tuple-element.38.low), custom_call_target="tpu_custom_call" | custom-call | flops 13107200 | bytes 98304000 | tf_op jit(solution)/shard_map/reduce_grads/pallas_call | solution.py:668
  293.4 2.6 fusion.71
  296.2 3.0 fusion.43
  (231 shorter events, 43.5 us)
Async XLA Ops:
  0.6 61.7 %collective-permute-start = (bf16[128,1024]{1,0:T(8,128)(2,1)}, bf16[128,1024]{1,0:T(8,128)(2,1)S(1)}, u32[]{:S(2)}, u32[]{:S(2)}) collective-permute-start(bf16[128,1024]{1,0:T(8,128)(2,1)} %bitcast.159), channel_id=1, source_target_pairs={{0,64},{64,0},{1,65},{65,1},{2,66},{66,2},{3,67},{67,3},{4,68},{68... | collective-permute-start | bytes 786440 | tf_op jit(solution)/shard_map/ppermute | solution.py:750
  5.4 34.1 %copy-start.51 = (s32[1,128,8]{1,2,0:T(8,128)S(1)}, s32[1,128,8]{1,2,0:T(8,128)}, u32[]{:S(2)}) copy-start(s32[1,128,8]{1,2,0:T(8,128)} %param.20) | copy-start | bytes 12292
  5.4 34.4 %copy-start.56 = (f32[1,128,8]{1,2,0:T(8,128)S(1)}, f32[1,128,8]{1,2,0:T(8,128)}, u32[]{:S(2)}) copy-start(f32[1,128,8]{1,2,0:T(8,128)} %param.21) | copy-start | bytes 12292
  5.4 34.8 %copy-start.3 = (bf16[1,128,1024]{2,1,0:T(8,128)(2,1)S(1)}, bf16[1,128,1024]{2,1,0:T(8,128)(2,1)}, u32[]{:S(2)}) copy-start(bf16[1,128,1024]{2,1,0:T(8,128)(2,1)} %param.23) | copy-start | bytes 786436
  39.6 21.0 %copy-start.22 = (s32[32,128]{1,0:T(8,128)}, s32[32,128]{1,0:T(8,128)S(1)}, u32[]{:S(2)}) copy-start(s32[32,128]{1,0:T(8,128)S(1)} %fusion.42) | copy-start | bytes 49156
  42.4 6.1 %copy-start = (bf16[1,128,1024]{2,1,0:T(8,128)(2,1)S(1)}, bf16[1,128,1024]{2,1,0:T(8,128)(2,1)}, u32[]{:S(2)}) copy-start(bf16[1,128,1024]{2,1,0:T(8,128)(2,1)} %param.12) | copy-start | bytes 786436
  42.4 46.5 %all-to-all-start.1 = ((bf16[32,40,1024]{2,1,0:T(8,128)(2,1)}), bf16[32,40,1024]{2,1,0:T(8,128)(2,1)}, u32[]{:S(2)}, u32[]{:S(2)}) async-start(bf16[32,40,1024]{2,1,0:T(8,128)(2,1)} %bitcast.31), calls=%async_computation.1 | async-start | bytes 5242880 | tf_op jit(solution)/shard_map/all_to_all | solution.py:725
  48.7 11.0 %copy-start.63 = (s32[1,256]{1,0:T(1,128)S(1)}, s32[1,256]{1,0:T(1,128)}, u32[]{:S(2)}) copy-start(s32[1,256]{1,0:T(1,128)} %param.22) | copy-start | bytes 3076
  59.7 6.1 %copy-start.49 = (f32[1024,1]{0,1:T(1,128)}, f32[1024,1]{0,1:T(1,128)S(1)}, u32[]{:S(2)}) copy-start(f32[1024,1]{0,1:T(1,128)S(1)} %get-tuple-element.52) | copy-start | bytes 12292
  59.7 6.1 %copy-start.57 = (f32[128]{0:T(128)}, f32[128]{0:T(128)S(1)}, u32[]{:S(2)}) copy-start(f32[128]{0:T(128)S(1)} %add_rsqrt_fusion.2) | copy-start | bytes 1540
  62.3 6.7 %copy-start.38 = (f32[128,32]{0,1:T(8,128)}, f32[128,32]{0,1:T(8,128)S(1)}, u32[]{:S(2)}) copy-start(f32[128,32]{0,1:T(8,128)S(1)} %get-tuple-element.84) | copy-start | bytes 49156
  71.8 79.7 %copy-start.2 = (bf16[8,64,2,128]{3,1,2,0:T(8,128)(2,1)}, bf16[8,64,2,128]{3,1,2,0:T(8,128)(2,1)S(1)}, u32[]{:S(2)}) copy-start(bf16[8,64,2,128]{3,1,2,0:T(8,128)(2,1)S(1)} %convolution_convert_fusion.1) | copy-start | bytes 786436
  74.1 14.8 %copy-start.53 = (f32[128]{0:T(128)}, f32[128]{0:T(128)S(1)}, u32[]{:S(2)}) copy-start(f32[128]{0:T(128)S(1)} %add_rsqrt_fusion) | copy-start | bytes 1540
  88.9 42.9 %all-to-all-start = ((bf16[32,40,1024]{2,1,0:T(8,128)(2,1)}), bf16[32,40,1024]{2,1,0:T(8,128)(2,1)}, u32[]{:S(2)}, u32[]{:S(2)}) async-start(bf16[32,40,1024]{2,1,0:T(8,128)(2,1)} %bitcast.158), calls=%async_computation | async-start | bytes 5242880 | tf_op jit(solution)/shard_map/all_to_all | solution.py:725
  95.3 3.5 %collective-permute-start.1 = (bf16[768,1024]{1,0:T(8,128)(2,1)S(1)}, bf16[768,1024]{1,0:T(8,128)(2,1)S(1)}, u32[]{:S(2)}, u32[]{:S(2)}) collective-permute-start(bf16[768,1024]{1,0:T(8,128)(2,1)S(1)} %pad_maximum_fusion.1), channel_id=1, source_target_pairs={{0,1},{1,0},{2,3},{3,2},{4,5},{5,4},{6,7},{7,6},{8,9},{9,8},{10,11... | collective-permute-start | bytes 4718600 | tf_op jit(solution)/shard_map/ppermute | solution.py:756
  143.7 5.2 %copy-start.23 = (s32[32,128]{1,0:T(8,128)S(1)}, s32[32,128]{1,0:T(8,128)}, u32[]{:S(2)}) copy-start(s32[32,128]{1,0:T(8,128)} %copy-done.22) | copy-start | bytes 49156
  143.7 5.2 %copy-start.36 = (f32[128,32]{0,1:T(8,128)S(1)}, f32[128,32]{0,1:T(8,128)}, u32[]{:S(2)}) copy-start(f32[128,32]{0,1:T(8,128)} %copy-done.35) | copy-start | bytes 49156
  143.7 5.2 %copy-start.46 = (s32[1280]{0:T(1024)S(1)}, s32[1280]{0:T(1024)}, u32[]{:S(2)}) copy-start(s32[1280]{0:T(1024)} %copy-done.45) | copy-start | bytes 15364
  143.7 52.1 %all-to-all-start.2 = ((bf16[32,40,1024]{2,1,0:T(8,128)(2,1)}), bf16[32,40,1024]{2,1,0:T(8,128)(2,1)}, u32[]{:S(2)}, u32[]{:S(2)}) async-start(bf16[32,40,1024]{2,1,0:T(8,128)(2,1)} %bitcast.167), calls=%async_computation.2 | async-start | bytes 5242880 | tf_op jit(solution)/shard_map/all_to_all | solution.py:725
  211.4 81.3 %collective-permute-start.2 = (bf16[128,1024]{1,0:T(8,128)(2,1)S(1)}, bf16[128,1024]{1,0:T(8,128)(2,1)S(1)}, u32[]{:S(2)}, u32[]{:S(2)}) collective-permute-start(bf16[128,1024]{1,0:T(8,128)(2,1)S(1)} %pad_maximum_fusion.5), channel_id=1, source_target_pairs={{0,64},{64,0},{1,65},{65,1},{2,66},{66,2},{3,67},{67,3},{4,68},{68... | collective-permute-start | bytes 786440 | tf_op jit(solution)/shard_map/ppermute | solution.py:825
  211.5 84.6 %all-to-all-start.3 = ((bf16[32,40,1024]{2,1,0:T(8,128)(2,1)}), bf16[32,40,1024]{2,1,0:T(8,128)(2,1)}, u32[]{:S(2)}, u32[]{:S(2)}) async-start(bf16[32,40,1024]{2,1,0:T(8,128)(2,1)} %bitcast.166), calls=%async_computation.3 | async-start | bytes 5242880 | tf_op jit(solution)/shard_map/all_to_all | solution.py:725
  240.1 53.3 %copy-start.50 = (f32[1024,1]{0,1:T(1,128)S(1)}, f32[1024,1]{0,1:T(1,128)}, u32[]{:S(2)}) copy-start(f32[1024,1]{0,1:T(1,128)} %copy-done.49) | copy-start | bytes 12292
  291.8 4.3 %copy-start.19 = (bf16[1280,128]{1,0:T(8,128)(2,1)S(1)}, bf16[1280,128]{1,0:T(8,128)(2,1)}, u32[]{:S(2)}) copy-start(bf16[1280,128]{1,0:T(8,128)(2,1)} %get-tuple-element.73) | copy-start | bytes 983044
  291.8 4.3 %copy-start.20 = (bf16[1280,128]{1,0:T(8,128)(2,1)S(1)}, bf16[1280,128]{1,0:T(8,128)(2,1)}, u32[]{:S(2)}) copy-start(bf16[1280,128]{1,0:T(8,128)(2,1)} %get-tuple-element.74) | copy-start | bytes 983044
  (48 other events, 101.9 us)

commit v5 on v4

--- a/solution.py
+++ b/solution.py
@@ -169,8 +169,9 @@
     grads_ref,
     down_w_ref,
     out_ref,
-    total_ref,
-    rest_ref,
+    gate_ref,
+    up_ref,
+    third_ref,
     theirs,
     came,
     last,
@@ -212,9 +213,9 @@
             target[:, columns] = dot(left[:, at : at + BLOCK], right[:, columns], TN)
 
     away = [send(k, theirs.at[k], came.at[k], partner) for k in range(3)]
-    across = [send(3 + k, low.at[k], low_came.at[k], mirror) for k in range(1)]
-    mine = [total_ref, last.at[0], last.at[1]]
-    lows = [low.at[0], rest_ref.at[0], rest_ref.at[1]]
+    across = [send(3 + k, low.at[k], low_came.at[k], mirror) for k in range(2)]
+    mine = [gate_ref, up_ref, last]
+    lows = [low.at[0], low.at[1], third_ref]
     for k in range(3):
         unit_grads(1, k, theirs.at[k])
         if k:
@@ -234,7 +235,6 @@
         join(k)
         if k < 2:
             unit_grads(0, k + 1, mine[k + 1])
-        if k < len(across):
             across[k].start()
 
     @pl.loop(0, x_ref.shape[0] // ROW_BLOCK)
@@ -247,7 +247,7 @@
             out = part if out is None else out + part
         out_ref[rows, :] = out.astype(bf16)
 
-    for k in range(len(across)):
+    for k in range(2):
         across[k].wait_recv()
 
         @pl.loop(0, BLOCK // 32)
@@ -264,20 +264,21 @@
     return pl.pallas_call(
         experts_second_body,
         in_specs=[pl.BlockSpec(memory_space=pltpu.VMEM)] * 5,
-        out_specs=[pl.BlockSpec(memory_space=pltpu.VMEM)] * 3,
+        out_specs=[pl.BlockSpec(memory_space=pltpu.VMEM)] * 4,
         out_shape=[
             jax.ShapeDtypeStruct((rows, width), bf16),
             jax.ShapeDtypeStruct((BLOCK, width), f32),
-            jax.ShapeDtypeStruct((2, BLOCK, width), bf16),
+            jax.ShapeDtypeStruct((BLOCK, width), f32),
+            jax.ShapeDtypeStruct((BLOCK, width), bf16),
         ],
         scratch_shapes=[
             pltpu.VMEM((3, BLOCK, width), f32),
             pltpu.VMEM((3, BLOCK, width), f32),
-            pltpu.VMEM((2, BLOCK, width), f32),
-            pltpu.VMEM((1, BLOCK, width), bf16),
-            pltpu.VMEM((1, BLOCK, width), bf16),
-            pltpu.SemaphoreType.DMA((4,)),
-            pltpu.SemaphoreType.DMA((4,)),
+            pltpu.VMEM((BLOCK, width), f32),
+            pltpu.VMEM((2, BLOCK, width), bf16),
+            pltpu.VMEM((2, BLOCK, width), bf16),
+            pltpu.SemaphoreType.DMA((5,)),
+            pltpu.SemaphoreType.DMA((5,)),
         ],
         compiler_params=pltpu.CompilerParams(collective_id=1, has_side_effects=True),
         cost_estimate=pl.CostEstimate(
@@ -472,8 +473,7 @@
     in_ref,
     out_ref,
     gain_ref,
-    up_ref,
-    down_ref,
+    unit_ref,
     came,
     acc,
     stage,
@@ -508,7 +508,7 @@
         return device((y + flip * step) % RING, (z + core * step) % RING, half, core)
 
     partner = device(y, z, half, flip)
-    across = device(y, z, 1 - half, core)
+    across = (1 - seq, chip + 1 - 2 * half, core)
     mirror = (1 - seq, chip, core)
     ahead, behind = (1, RING - 1)
     barrier = pltpu.get_barrier_semaphore()
@@ -636,11 +636,10 @@
     ring[11].start()
     units.wait_recv()
 
-    @pl.loop(0, low.shape[1] // 32)
+    @pl.loop(0, low.shape[0] // 32)
     def _(r):
         rows = pl.ds(pl.multiple_of(r * 32, 32), 32)
-        up_ref[rows, :] = low[0, rows, :].astype(f32) + low_came[0, rows, :].astype(f32)
-        down_ref[rows, :] = low[1, rows, :].astype(f32) + low_came[1, rows, :].astype(f32)
+        unit_ref[rows, :] = low[rows, :].astype(f32) + low_came[rows, :].astype(f32)
 
     ring[11].wait_recv()
     total = own[...] + in_own[...]
@@ -668,13 +667,12 @@
     return pl.pallas_call(
         reduce_body,
         in_specs=[pl.BlockSpec(memory_space=pltpu.VMEM)] * 3,
-        out_specs=[pl.BlockSpec(memory_space=pltpu.VMEM)] * 5,
+        out_specs=[pl.BlockSpec(memory_space=pltpu.VMEM)] * 4,
         out_shape=[
             jax.ShapeDtypeStruct((share, cut), f32),
             jax.ShapeDtypeStruct((share, width - cut - 128), f32),
             jax.ShapeDtypeStruct((share, 128), f32),
-            jax.ShapeDtypeStruct(low.shape[1:], f32),
-            jax.ShapeDtypeStruct(low.shape[1:], f32),
+            jax.ShapeDtypeStruct(low.shape, f32),
         ],
         scratch_shapes=[
             pltpu.VMEM(shape, bf16),
@@ -722,7 +720,16 @@
 def exchange(rows):
     width = rows.shape[-1]
     blocks = rows.reshape(EXPERTS, -1, width)
-    return lax.all_to_all(blocks, "chip", split_axis=0, concat_axis=0, tiled=True).reshape(-1, width)
+    groups = [[(g ^ (c % 2)) * EXPERTS + c for c in range(EXPERTS)] for g in range(2)]
+    landed = lax.all_to_all(
+        blocks,
+        ("seq", "chip"),
+        split_axis=0,
+        concat_axis=0,
+        axis_index_groups=groups,
+        tiled=True,
+    )
+    return landed.reshape(-1, width)
 
 
 def on_device(
@@ -804,7 +811,7 @@
     arrived = exchange(dot(placed, normed_two).astype(bf16))
     hidden, grads, back = experts_first(arrived, grad_arrived, pre_w, down_w)
     grad_back = exchange(back)
-    out_rows, gate_total, rest_low = experts_second(arrived, grad_arrived, hidden, grads, down_w)
+    out_rows, gate_total, up_total, down_low = experts_second(arrived, grad_arrived, hidden, grads, down_w)
     grad_back, out_rows = lax.optimization_barrier((grad_back, out_rows))
     returned = exchange(out_rows)
 
@@ -855,8 +862,8 @@
         gain_parts,
     )
     in_width = query_width + 2 * kv_width
-    in_total, out_total, gain_total, up_total, down_total = reduce_grads(
-        grads_mine, grads_sent, rest_low, in_width
+    in_total, out_total, gain_total, down_total = reduce_grads(
+        grads_mine, grads_sent, down_low, in_width
     )
     gain_total = gain_total[:, :2] + gain_total[:, 2:4] + gain_total[:, 4:6]
 

time: 306 us -> 306 us (level); the launches traced: 305 us -> 301 us
  starting transfers between devices: 31.9 us -> 28.3 us
    all_to_all x4, starting transfers between devices: 30.1 us -> 25.7 us  [exchange(): lax.all_to_all(blocks, ('seq', 'chip'), split_axis=0, concat_axis=0, axis...]
where the time goes in v5:
time: 306 us; the launch traced here: 301 us
  Pallas kernels  146 us (48%)
  waiting for transfers between devices  45.5 us (15%)
  matrix products  36.3 us (12%)
  starting transfers between devices  28.3 us (9%)
  local copies, waits for them, and re-layouts  26.3 us (9%)
  other arithmetic  17.3 us (6%)
    pallas_call x1, Pallas kernels, reduce_grads(): pl.pallas_call(reduce_body, in_specs=[pl.BlockSpec(memory_space=pltpu.VME...  51.3 us
    all_to_all x4, waiting for transfers between devices, exchange(): lax.all_to_all(blocks, ('seq', 'chip'), split_axis=0, concat_axis=0, axis...  42.1 us
    pallas_call x1, Pallas kernels, experts_second(): pl.pallas_call(experts_second_body, in_specs=[pl.BlockSpec(memory_space=p...  41.9 us
    pallas_call x1, Pallas kernels, gather_weights(): pl.pallas_call(gather_body, out_shape=jax.ShapeDtypeStruct((RING, RING, 2...  34 us
    dot_general x14, matrix products, dot(): return lax.dot_general(a, b, dims, preferred_element_type=f32)  31.8 us
    all_to_all x4, starting transfers between devices, exchange(): lax.all_to_all(blocks, ('seq', 'chip'), split_axis=0, concat_axis=0, axis...  25.7 us
    pallas_call x1, Pallas kernels, experts_first(): pl.pallas_call(experts_first_body, grid=(rows // ROW_BLOCK,), in_specs=[p...  11.9 us
    optimization_barrier x1, local copies, waits for them, and re-layouts, on_device(): gathered, grad_rows = lax.optimization_barrier((gathered, grad_rows))  9.58 us
  transfers between devices with their start and end apart: 7, of which 3 were waited for; matrix products, arithmetic and copies ran while one was open for 18% of the time, Pallas kernels for 44%

profile of v5, /device:TPU:0, one launch (start us, length us, event | category | flops | bytes accessed | tf_op | source)
XLA Modules:
  0.0 301.2 jit_solution(4086706253107752057)
XLA Ops:
  5.4 34.0 %gather_weights.1 = bf16[4,4,2,2,16,3200]{5,4,3,2,1,0:T(8,128)(2,1)} custom-call(bf16[16,3200]{1,0:T(8,128)(2,1)} %concatenate.79.shard_ref), custom_call_target="tpu_custom_call" | custom-call | bytes 52428800 | tf_op jit(solution)/shard_map/gather_weights/pallas_call | solution.py:395
  40.1 2.3 multiply_convert_fusion
  42.5 6.6 %all-to-all-start.1 = ((bf16[32,40,1024]{2,1,0:T(8,128)(2,1)}), bf16[32,40,1024]{2,1,0:T(8,128)(2,1)}, u32[]{:S(2)}, u32[]{:S(2)}) async-start(bf16[32,40,1024]{2,1,0:T(8,128)(2,1)} %bitcast.31), calls=%async_computation.1 | async-start | bytes 5242880 | tf_op jit(solution)/shard_map/all_to_all | solution.py:724
  49.3 9.6 %copy.71 = bf16[1024,3200]{0,1:T(8,128)(2,1)} copy(bf16[1024,3200]{1,0:T(8,128)(2,1)} %bitcast.150) | data formatting | bytes 13107200 | tf_op jit(solution)/shard_map/optimization_barrier | solution.py:775
  63.3 3.1 %fusion.2 = f32[128,2048]{1,0:T(8,128)S(1)} fusion(bf16[128,1024]{1,0:T(8,128)(2,1)S(1)} %get-tuple-element.82, bf16[1024,3200]{1,0:T(8,128)(2,1)} %bitcast.151), kind=kOutput, calls=%fused_computation.4 | convolution fusion | flops 536870912 | bytes 5505024 | tf_op jit(solution)/shard_map/dot_general | solution.py:33
  72.4 2.3 multiply_reduce_fusion.3
  74.7 2.4 convolution_convert_fusion
  77.1 12.4 %all-to-all-done.1 = bf16[32,40,1024]{2,1,0:T(8,128)(2,1)} async-done(((bf16[32,40,1024]{2,1,0:T(8,128)(2,1)}), bf16[32,40,1024]{2,1,0:T(8,128)(2,1)}, u32[]{:S(2)}, u32[]{:S(2)}) %all-to-all-start.1) | async-done | bytes 2621472 | tf_op jit(solution)/shard_map/all_to_all | solution.py:724
  89.6 4.8 %all-to-all-start = ((bf16[32,40,1024]{2,1,0:T(8,128)(2,1)}), bf16[32,40,1024]{2,1,0:T(8,128)(2,1)}, u32[]{:S(2)}, u32[]{:S(2)}) async-start(bf16[32,40,1024]{2,1,0:T(8,128)(2,1)} %bitcast.158), calls=%async_computation | async-start | bytes 5242880 | tf_op jit(solution)/shard_map/all_to_all | solution.py:724
  96.0 3.4 %collective-permute-done.1 = bf16[768,1024]{1,0:T(8,128)(2,1)S(1)} collective-permute-done((bf16[768,1024]{1,0:T(8,128)(2,1)S(1)}, bf16[768,1024]{1,0:T(8,128)(2,1)S(1)}, u32[]{:S(2)}, u32[]{:S(2)}) %collective-permute-start.1) | collective-permute-done | bytes 1572896 | tf_op jit(solution)/shard_map/ppermute | solution.py:763
  102.5 29.7 %all-to-all-done = bf16[32,40,1024]{2,1,0:T(8,128)(2,1)} async-done(((bf16[32,40,1024]{2,1,0:T(8,128)(2,1)}), bf16[32,40,1024]{2,1,0:T(8,128)(2,1)}, u32[]{:S(2)}, u32[]{:S(2)}) %all-to-all-start) | async-done | bytes 2621472 | tf_op jit(solution)/shard_map/all_to_all | solution.py:724
  132.2 11.9 %experts_first.1 = (bf16[1280,512]{1,0:T(8,128)(2,1)}, bf16[1280,1024]{1,0:T(8,128)(2,1)}, bf16[1280,1024]{1,0:T(8,128)(2,1)}) custom-call(bf16[1280,1024]{1,0:T(8,128)(2,1)} %bitcast.30.x_ref, bf16[1280,1024]{1,0:T(8,128)(2,1)} %bitcast.32.g_ref, bf16[1024,1024]{1,0:T(8,128)(2,1)} %pad_maximum_fusion.pre_w_ref, bf16[512,1024]{1,0:T(8,128)(2,1)} %pad_maximum_fusion.2.down_w_ref), custom_call_target="tpu_custom_call" | custom-call | flops 6710886400 | bytes 13107200 | tf_op jit(solution)/shard_map/experts_first/pallas_call | solution.py:137
  144.1 5.1 %all-to-all-start.2 = ((bf16[32,40,1024]{2,1,0:T(8,128)(2,1)}), bf16[32,40,1024]{2,1,0:T(8,128)(2,1)}, u32[]{:S(2)}, u32[]{:S(2)}) async-start(bf16[32,40,1024]{2,1,0:T(8,128)(2,1)} %bitcast.167), calls=%async_computation.2 | async-start | bytes 5242880 | tf_op jit(solution)/shard_map/all_to_all | solution.py:724
  151.9 2.1 fusion.21
  155.0 41.9 %experts_second.1 = (bf16[1280,1024]{1,0:T(8,128)(2,1)}, f32[256,1024]{1,0:T(8,128)}, f32[256,1024]{1,0:T(8,128)}, bf16[256,1024]{1,0:T(8,128)(2,1)}) custom-call(bf16[1280,1024]{1,0:T(8,128)(2,1)} %bitcast.30.x_ref, bf16[1280,1024]{1,0:T(8,128)(2,1)} %bitcast.32.g_ref, bf16[1280,512]{1,0:T(8,128)(2,1)} %get-tuple-element.31.hidden_ref, ...), custom_call_target="tpu_custom_call" | custom-call | flops 5368709120 | bytes 52428800 | tf_op jit(solution)/shard_map/experts_second/pallas_call | solution.py:264
  196.9 3.0 %multiply_reduce_fusion = (f32[1024]{0:T(1024)}, f32[128]{0:T(128)S(1)}, f32[128,1024]{1,0:T(8,128)S(1)}) fusion(f32[128,1024]{1,0:T(8,128)S(1)} %get-tuple-element.97, f32[128]{0:T(128)} %copy-done.53, f32[1024]{0:T(1024)} %bitcast.190, pred[1280,128]{1,0:T(32,128)(4,1)} %bitcast_compare_fusion, bf16[1280,1024]{1,0:T(8,128)(2,1)} %bitcast.34), kind=kOutput, calls=%fused_computation.97 | convolution fusion | flops 336329600 | bytes 3843072 | tf_op jit(solution)/shard_map/dot_general | solution.py:33
  202.4 3.1 %fusion.37 = bf16[128,1024]{1,0:T(8,128)(2,1)} fusion(bf16[128,1024]{1,0:T(8,128)(2,1)S(1)} %fusion.111.gr_ref, bf16[1024,3200]{1,0:T(8,128)(2,1)} %bitcast.154), kind=kOutput, calls=%fused_computation.41 | convolution fusion | flops 268566528 | bytes 2621440 | tf_op jit(solution)/shard_map/dot_general | solution.py:33
  213.3 9.2 %all-to-all-start.3 = ((bf16[32,40,1024]{2,1,0:T(8,128)(2,1)}), bf16[32,40,1024]{2,1,0:T(8,128)(2,1)}, u32[]{:S(2)}, u32[]{:S(2)}) async-start(bf16[32,40,1024]{2,1,0:T(8,128)(2,1)} %bitcast.166), calls=%async_computation.3 | async-start | bytes 5242880 | tf_op jit(solution)/shard_map/all_to_all | solution.py:724
  222.5 2.4 fusion.17
  225.1 2.5 fusion.70
  230.7 6.3 %projection_grads.1 = (f32[512,3200]{1,0:T(8,128)}, bf16[512,3200]{1,0:T(8,128)(2,1)}) custom-call(bf16[384,512]{1,0:T(8,128)(2,1)} %get-tuple-element.54.mine_ref, bf16[384,512]{1,0:T(8,128)(2,1)} %get-tuple-element.53.sent_ref, bf16[128,1024]{1,0:T(8,128)(2,1)} %copy.88.gq_ref, bf16[256,1024]{1,0:T(8,128)(2,1)} %maximum_maximum_fusion.gkv_ref, ...), custom_call_target="tpu_custom_call" | custom-call | tf_op jit(solution)/shard_map/projection_grads/pallas_call | solution.py:436
  237.1 51.3 %reduce_grads.1 = (f32[16,2048]{1,0:T(8,128)}, f32[16,1024]{1,0:T(8,128)}, f32[16,128]{1,0:T(8,128)}, f32[256,1024]{1,0:T(8,128)}) custom-call(f32[4,4,2,16,3200]{4,3,2,1,0:T(8,128)} %bitcast.159, bf16[4,4,2,16,3200]{4,3,2,1,0:T(8,128)(2,1)} %bitcast.165, bf16[256,1024]{1,0:T(8,128)(2,1)} %get-tuple-element.38.low), custom_call_target="tpu_custom_call" | custom-call | flops 13107200 | bytes 98304000 | tf_op jit(solution)/shard_map/reduce_grads/pallas_call | solution.py:667
  290.0 2.6 fusion.71
  292.7 3.0 fusion.43
  (231 shorter events, 44.2 us)
Async XLA Ops:
  0.6 62.3 %collective-permute-start = (bf16[128,1024]{1,0:T(8,128)(2,1)}, bf16[128,1024]{1,0:T(8,128)(2,1)S(1)}, u32[]{:S(2)}, u32[]{:S(2)}) collective-permute-start(bf16[128,1024]{1,0:T(8,128)(2,1)} %bitcast.160), channel_id=1, source_target_pairs={{0,64},{64,0},{1,65},{65,1},{2,66},{66,2},{3,67},{67,3},{4,68},{68... | collective-permute-start | bytes 786440 | tf_op jit(solution)/shard_map/ppermute | solution.py:757
  5.4 34.1 %copy-start.51 = (s32[1,128,8]{1,2,0:T(8,128)S(1)}, s32[1,128,8]{1,2,0:T(8,128)}, u32[]{:S(2)}) copy-start(s32[1,128,8]{1,2,0:T(8,128)} %param.20) | copy-start | bytes 12292
  5.4 34.4 %copy-start.56 = (f32[1,128,8]{1,2,0:T(8,128)S(1)}, f32[1,128,8]{1,2,0:T(8,128)}, u32[]{:S(2)}) copy-start(f32[1,128,8]{1,2,0:T(8,128)} %param.21) | copy-start | bytes 12292
  5.4 34.8 %copy-start.3 = (bf16[1,128,1024]{2,1,0:T(8,128)(2,1)S(1)}, bf16[1,128,1024]{2,1,0:T(8,128)(2,1)}, u32[]{:S(2)}) copy-start(bf16[1,128,1024]{2,1,0:T(8,128)(2,1)} %param.23) | copy-start | bytes 786436
  39.6 21.6 %copy-start.22 = (s32[32,128]{1,0:T(8,128)}, s32[32,128]{1,0:T(8,128)S(1)}, u32[]{:S(2)}) copy-start(s32[32,128]{1,0:T(8,128)S(1)} %fusion.42) | copy-start | bytes 49156
  42.5 6.6 %copy-start = (bf16[1,128,1024]{2,1,0:T(8,128)(2,1)S(1)}, bf16[1,128,1024]{2,1,0:T(8,128)(2,1)}, u32[]{:S(2)}) copy-start(bf16[1,128,1024]{2,1,0:T(8,128)(2,1)} %param.12) | copy-start | bytes 786436
  42.5 47.1 %all-to-all-start.1 = ((bf16[32,40,1024]{2,1,0:T(8,128)(2,1)}), bf16[32,40,1024]{2,1,0:T(8,128)(2,1)}, u32[]{:S(2)}, u32[]{:S(2)}) async-start(bf16[32,40,1024]{2,1,0:T(8,128)(2,1)} %bitcast.31), calls=%async_computation.1 | async-start | bytes 5242880 | tf_op jit(solution)/shard_map/all_to_all | solution.py:724
  49.3 11.0 %copy-start.63 = (s32[1,256]{1,0:T(1,128)S(1)}, s32[1,256]{1,0:T(1,128)}, u32[]{:S(2)}) copy-start(s32[1,256]{1,0:T(1,128)} %param.22) | copy-start | bytes 3076
  60.3 6.1 %copy-start.49 = (f32[1024,1]{0,1:T(1,128)}, f32[1024,1]{0,1:T(1,128)S(1)}, u32[]{:S(2)}) copy-start(f32[1024,1]{0,1:T(1,128)S(1)} %get-tuple-element.52) | copy-start | bytes 12292
  60.3 6.1 %copy-start.57 = (f32[128]{0:T(128)}, f32[128]{0:T(128)S(1)}, u32[]{:S(2)}) copy-start(f32[128]{0:T(128)S(1)} %add_rsqrt_fusion.2) | copy-start | bytes 1540
  62.9 6.7 %copy-start.38 = (f32[128,32]{0,1:T(8,128)}, f32[128,32]{0,1:T(8,128)S(1)}, u32[]{:S(2)}) copy-start(f32[128,32]{0,1:T(8,128)S(1)} %get-tuple-element.84) | copy-start | bytes 49156
  72.4 79.4 %copy-start.2 = (bf16[8,64,2,128]{3,1,2,0:T(8,128)(2,1)}, bf16[8,64,2,128]{3,1,2,0:T(8,128)(2,1)S(1)}, u32[]{:S(2)}) copy-start(bf16[8,64,2,128]{3,1,2,0:T(8,128)(2,1)S(1)} %convolution_convert_fusion.1) | copy-start | bytes 786436
  74.7 14.9 %copy-start.53 = (f32[128]{0:T(128)}, f32[128]{0:T(128)S(1)}, u32[]{:S(2)}) copy-start(f32[128]{0:T(128)S(1)} %add_rsqrt_fusion) | copy-start | bytes 1540
  89.6 42.6 %all-to-all-start = ((bf16[32,40,1024]{2,1,0:T(8,128)(2,1)}), bf16[32,40,1024]{2,1,0:T(8,128)(2,1)}, u32[]{:S(2)}, u32[]{:S(2)}) async-start(bf16[32,40,1024]{2,1,0:T(8,128)(2,1)} %bitcast.158), calls=%async_computation | async-start | bytes 5242880 | tf_op jit(solution)/shard_map/all_to_all | solution.py:724
  95.9 3.5 %collective-permute-start.1 = (bf16[768,1024]{1,0:T(8,128)(2,1)S(1)}, bf16[768,1024]{1,0:T(8,128)(2,1)S(1)}, u32[]{:S(2)}, u32[]{:S(2)}) collective-permute-start(bf16[768,1024]{1,0:T(8,128)(2,1)S(1)} %pad_maximum_fusion.1), channel_id=1, source_target_pairs={{0,1},{1,0},{2,3},{3,2},{4,5},{5,4},{6,7},{7,6},{8,9},{9,8},{10,11... | collective-permute-start | bytes 4718600 | tf_op jit(solution)/shard_map/ppermute | solution.py:763
  144.1 5.2 %copy-start.23 = (s32[32,128]{1,0:T(8,128)S(1)}, s32[32,128]{1,0:T(8,128)}, u32[]{:S(2)}) copy-start(s32[32,128]{1,0:T(8,128)} %copy-done.22) | copy-start | bytes 49156
  144.1 5.2 %copy-start.36 = (f32[128,32]{0,1:T(8,128)S(1)}, f32[128,32]{0,1:T(8,128)}, u32[]{:S(2)}) copy-start(f32[128,32]{0,1:T(8,128)} %copy-done.35) | copy-start | bytes 49156
  144.1 5.2 %copy-start.46 = (s32[1280]{0:T(1024)S(1)}, s32[1280]{0:T(1024)}, u32[]{:S(2)}) copy-start(s32[1280]{0:T(1024)} %copy-done.45) | copy-start | bytes 15364
  144.1 52.8 %all-to-all-start.2 = ((bf16[32,40,1024]{2,1,0:T(8,128)(2,1)}), bf16[32,40,1024]{2,1,0:T(8,128)(2,1)}, u32[]{:S(2)}, u32[]{:S(2)}) async-start(bf16[32,40,1024]{2,1,0:T(8,128)(2,1)} %bitcast.167), calls=%async_computation.2 | async-start | bytes 5242880 | tf_op jit(solution)/shard_map/all_to_all | solution.py:724
  212.4 76.9 %collective-permute-start.2 = (bf16[128,1024]{1,0:T(8,128)(2,1)S(1)}, bf16[128,1024]{1,0:T(8,128)(2,1)S(1)}, u32[]{:S(2)}, u32[]{:S(2)}) collective-permute-start(bf16[128,1024]{1,0:T(8,128)(2,1)S(1)} %pad_maximum_fusion.5), channel_id=1, source_target_pairs={{0,64},{64,0},{1,65},{65,1},{2,66},{66,2},{3,67},{67,3},{4,68},{68... | collective-permute-start | bytes 786440 | tf_op jit(solution)/shard_map/ppermute | solution.py:832
  213.3 79.4 %all-to-all-start.3 = ((bf16[32,40,1024]{2,1,0:T(8,128)(2,1)}), bf16[32,40,1024]{2,1,0:T(8,128)(2,1)}, u32[]{:S(2)}, u32[]{:S(2)}) async-start(bf16[32,40,1024]{2,1,0:T(8,128)(2,1)} %bitcast.166), calls=%async_computation.3 | async-start | bytes 5242880 | tf_op jit(solution)/shard_map/all_to_all | solution.py:724
  237.1 52.9 %copy-start.50 = (f32[1024,1]{0,1:T(1,128)S(1)}, f32[1024,1]{0,1:T(1,128)}, u32[]{:S(2)}) copy-start(f32[1024,1]{0,1:T(1,128)} %copy-done.49) | copy-start | bytes 12292
  288.4 4.3 %copy-start.19 = (bf16[1280,128]{1,0:T(8,128)(2,1)S(1)}, bf16[1280,128]{1,0:T(8,128)(2,1)}, u32[]{:S(2)}) copy-start(bf16[1280,128]{1,0:T(8,128)(2,1)} %get-tuple-element.73) | copy-start | bytes 983044
  288.4 4.3 %copy-start.20 = (bf16[1280,128]{1,0:T(8,128)(2,1)S(1)}, bf16[1280,128]{1,0:T(8,128)(2,1)}, u32[]{:S(2)}) copy-start(bf16[1280,128]{1,0:T(8,128)(2,1)} %get-tuple-element.74) | copy-start | bytes 983044
  (48 other events, 102.0 us)

commit v6 on v5

--- a/solution.py
+++ b/solution.py
@@ -93,21 +93,6 @@
     weights = jnp.exp(scores - log_total).astype(bf16)
     mixed = jnp.einsum("kgqs,skd->qkgd", weights, values, preferred_element_type=f32)
     return (mixed.astype(bf16), log_total)
-
-
-def attend_backward(query, keys, values, allowed, attended, log_total, grad_attended):
-    scale_factor = HEAD_DIM ** (-0.5)
-    weights = jnp.exp(masked_scores(query, keys, allowed) - log_total)
-    grad_values = jnp.einsum(
-        "kgqs,qkgd->skd", weights.astype(bf16), grad_attended, preferred_element_type=f32
-    )
-    grad_weights = jnp.einsum("qkgd,skd->kgqs", grad_attended, values, preferred_element_type=f32)
-    row_delta = jnp.sum(grad_attended.astype(f32) * attended.astype(f32), axis=-1)
-    row_delta = jnp.transpose(row_delta, (1, 2, 0))
-    grad_scores = (weights * (grad_weights - row_delta[..., None])).astype(bf16)
-    grad_query = jnp.einsum("kgqs,skd->qkgd", grad_scores, keys, preferred_element_type=f32)
-    grad_keys = jnp.einsum("kgqs,qkgd->skd", grad_scores, query, preferred_element_type=f32)
-    return (grad_query * scale_factor, grad_keys * scale_factor, grad_values)
 
 
 def experts_first_body(x_ref, g_ref, pre_w_ref, down_w_ref, hidden_ref, grads_ref, back_ref):
@@ -695,10 +680,167 @@
         ],
         compiler_params=pltpu.CompilerParams(collective_id=2, has_side_effects=True),
         cost_estimate=pl.CostEstimate(
-            flops=mine.size * 8, bytes_accessed=mine.size * 60, transcendentals=0
+            flops=mine.size, bytes_accessed=mine.size, transcendentals=0
         ),
         name="reduce_grads",
     )(mine.reshape(shape), sent.reshape(shape), low)
+
+
+def rotated(block, cosine, sine, first_half):
+    partner = jnp.where(first_half, pltpu.roll(block, 96, 1), pltpu.roll(block, 32, 1))
+    return block * cosine + partner * sine
+
+
+def block_backward_body(
+    placed_ref,
+    back_ref,
+    residual_ref,
+    inverse_ref,
+    gain_ref,
+    cotangent_ref,
+    weights_hbm,
+    query_ref,
+    keys_ref,
+    values_ref,
+    allowed_ref,
+    attended_ref,
+    log_ref,
+    cosine_ref,
+    sine_ref,
+    own_ref,
+    other_ref,
+    residual_out,
+    low_out,
+    query_out,
+    kv_out,
+    from_out,
+    gains_out,
+    weights,
+    sems,
+):
+    tokens, width = residual_ref.shape
+    kv_width = keys_ref.shape[1]
+    in_width = width + 2 * kv_width
+    out_part = pltpu.make_async_copy(
+        weights_hbm.at[:, in_width : in_width + width],
+        weights.at[:, in_width : in_width + width],
+        sems.at[0],
+    )
+    in_part = pltpu.make_async_copy(
+        weights_hbm.at[:, :in_width], weights.at[:, :in_width], sems.at[1]
+    )
+    out_part.start()
+    in_part.start()
+    residual = residual_ref[...]
+    inverse = inverse_ref[...]
+    upstream = dot(placed_ref[...], back_ref[...], TN)
+    gains_out[1:2, :] = jnp.sum(upstream * residual * inverse, axis=0, keepdims=True)
+    scaled = upstream * gain_ref[...]
+    coupling = jnp.mean(scaled * residual, axis=-1, keepdims=True)
+    grad = inverse * scaled - residual * inverse * inverse * inverse * coupling
+    grad = cotangent_ref[...].astype(f32) + grad
+    residual_out[...] = grad
+    low = grad.astype(bf16)
+    low_out[...] = low
+    out_part.wait()
+    grad_mixed = dot(low, weights[:, in_width : in_width + width], NT).astype(bf16)
+
+    lane = lax.broadcasted_iota(jnp.int32, (1, 128), 1)
+    low_lanes = lane < HEAD_DIM
+    first_half = lane % HEAD_DIM < HEAD_DIM // 2
+    allowed = allowed_ref[...] != 0
+    cosine, sine = (cosine_ref[...], sine_ref[...])
+    scale = HEAD_DIM ** (-0.5)
+
+    def doubled(block, place):
+        wide = block.astype(f32)
+        turned = pltpu.roll(wide, HEAD_DIM, 1)
+        pair = (wide, turned) if place == 0 else (turned, wide)
+        return jnp.where(low_lanes, pair[0], pair[1]).astype(bf16)
+
+    for m in range(KV_HEADS // 2):
+        kv_lanes = slice(m * 128, (m + 1) * 128)
+        key_parts, value_parts = ([], [])
+        for place in range(2):
+            j = 2 * m + place
+            lanes = slice(j * 128, (j + 1) * 128)
+            keys = doubled(keys_ref[:, kv_lanes], place)
+            values = doubled(values_ref[:, kv_lanes], place)
+            grad_block = grad_mixed[:, lanes].astype(f32)
+            product = grad_block * attended_ref[:, lanes].astype(f32)
+            query_block = query_ref[:, lanes].astype(f32)
+            grad_query = []
+            grad_keys, grad_values = (None, None)
+            for part in range(2):
+                mine = low_lanes if part == 0 else jnp.logical_not(low_lanes)
+                query = jnp.where(mine, query_block, 0.0).astype(bf16)
+                upper = jnp.where(mine, grad_block, 0.0).astype(bf16)
+                scores = jnp.where(allowed, dot(query, keys, NT) * scale, -1e30)
+                exact = jnp.exp(scores - log_ref[:, 2 * j + part : 2 * j + part + 1])
+                delta = jnp.sum(jnp.where(mine, product, 0.0), axis=-1, keepdims=True)
+                grad_scores = (exact * (dot(upper, values, NT) - delta)).astype(bf16)
+                grad_query.append(dot(grad_scores, keys))
+                to_keys = dot(grad_scores, query, TN)
+                to_values = dot(exact.astype(bf16), upper, TN)
+                grad_keys = to_keys if part == 0 else grad_keys + to_keys
+                grad_values = to_values if part == 0 else grad_values + to_values
+            both = jnp.where(low_lanes, grad_query[0], grad_query[1]) * scale
+            both = rotated(both, cosine[:tokens], sine[:tokens], first_half)
+            query_out[:, lanes] = both.astype(bf16)
+            key_parts.append(grad_keys + pltpu.roll(grad_keys, HEAD_DIM, 1))
+            value_parts.append(grad_values + pltpu.roll(grad_values, HEAD_DIM, 1))
+        grad_keys = jnp.where(low_lanes, key_parts[0], key_parts[1]) * scale
+        kv_out[:, kv_lanes] = rotated(grad_keys, cosine, sine, first_half).astype(bf16)
+        value_lanes = slice(kv_width + m * 128, kv_width + (m + 1) * 128)
+        kv_out[:, value_lanes] = jnp.where(low_lanes, value_parts[0], value_parts[1]).astype(bf16)
+
+    in_part.wait()
+    from_kv = dot(kv_out[...], weights[:, width:in_width], NT)
+    from_own = dot(query_out[...], weights[:, :width], NT) + from_kv[:tokens]
+    from_out[...] = from_own
+    gain = jnp.sum(from_own * own_ref[...], axis=0, keepdims=True)
+    gain += jnp.sum(from_kv[tokens:] * other_ref[...], axis=0, keepdims=True)
+    gains_out[0:1, :] = gain
+
+
+def block_backward(
+    placed, back, residual, inverse, gain, cotangent, weights, heads, masks, tables, scaled_inputs
+):
+    tokens, width = residual.shape
+    query, keys, values = heads
+    vmem = pl.BlockSpec(memory_space=pltpu.VMEM)
+    return pl.pallas_call(
+        block_backward_body,
+        in_specs=[vmem] * 6 + [pl.BlockSpec(memory_space=pl.ANY)] + [vmem] * 10,
+        out_specs=[vmem] * 6,
+        out_shape=[
+            jax.ShapeDtypeStruct((tokens, width), f32),
+            jax.ShapeDtypeStruct((tokens, width), bf16),
+            jax.ShapeDtypeStruct((tokens, width), bf16),
+            jax.ShapeDtypeStruct((2 * tokens, 2 * keys.shape[1]), bf16),
+            jax.ShapeDtypeStruct((tokens, width), f32),
+            jax.ShapeDtypeStruct((2, width), f32),
+        ],
+        scratch_shapes=[pltpu.VMEM(weights.shape, bf16), pltpu.SemaphoreType.DMA((2,))],
+        cost_estimate=pl.CostEstimate(
+            flops=3_000_000_000, bytes_accessed=12_000_000, transcendentals=600_000
+        ),
+        name="block_backward",
+    )(
+        placed,
+        back,
+        residual,
+        inverse,
+        gain,
+        cotangent,
+        weights,
+        query,
+        keys,
+        values,
+        *masks,
+        *tables,
+        *scaled_inputs,
+    )
 
 
 def spread_plan(route_ids, mix_weights):
@@ -794,6 +936,7 @@
     other_keys = rotate_wide(projected_other[:, :kv_width], other_cos, other_sin, 1.0)
     keys = jnp.concatenate([own_keys, other_keys], axis=0).astype(bf16)
     values = jnp.concatenate([projected[:, key_cut:], projected_other[:, kv_width:]], axis=0)
+    flat_heads = (query, keys, values.astype(bf16))
     query = query.reshape(token_count, KV_HEADS, group, HEAD_DIM)
     keys = keys.reshape(2 * token_count, KV_HEADS, HEAD_DIM)
     values = values.astype(bf16).reshape(2 * token_count, KV_HEADS, HEAD_DIM)
@@ -815,30 +958,25 @@
     grad_back, out_rows = lax.optimization_barrier((grad_back, out_rows))
     returned = exchange(out_rows)
 
-    grad_out = cotangent[0].astype(f32)
-    grad_normed_two = dot(placed, grad_back, TN)
-    grad_norm_two, gain_two_grad = norm_backward(residual, inverse_two, gain_two, grad_normed_two)
-    grad_residual = grad_out + grad_norm_two
-    grad_res_low = grad_residual.astype(bf16)
-    grad_mixed = dot(grad_res_low, out_full, NT).astype(bf16)
-    grad_query, grad_keys, grad_values = attend_backward(
-        query, keys, values, allowed, attended, log_total, grad_mixed.reshape(attended.shape)
-    )
-    grad_query = grad_query.reshape(token_count, query_width)
-    grad_keys = grad_keys.reshape(2 * token_count, kv_width)
-    grad_values = grad_values.reshape(2 * token_count, kv_width)
-    away_keys = rotate_wide(grad_keys[token_count:], other_cos, other_sin, -1.0)
-    away = jnp.concatenate([away_keys, grad_values[token_count:]], axis=1).astype(bf16)
-    came = lax.ppermute(away, "seq", SWAP)
-    grad_query = rotate_wide(grad_query, own_cos, own_sin, -1.0).astype(bf16)
-    grad_keys = rotate_wide(grad_keys[:token_count], own_cos, own_sin, -1.0)
-    grad_kv = jnp.concatenate([grad_keys, grad_values[:token_count]], axis=1).astype(bf16)
-    from_query = dot(grad_query, in_full[:, :query_width], NT)
-    from_kv = dot(jnp.concatenate([grad_kv, away], axis=0), kv_w, NT)
-    from_own = from_query + from_kv[:token_count]
-    other_values = other_low.astype(f32)
-    gain_one_grad = jnp.sum(from_own * row_values * inverse_one, axis=0)
-    gain_one_grad += jnp.sum(from_kv[token_count:] * other_values * inverse_other, axis=0)
+    log_rows = log_total.reshape(HEADS, token_count).T
+    lanes = jnp.arange(128)
+    cosine = jnp.concatenate([own_cos, other_cos], axis=0)[:, lanes % (HEAD_DIM // 2)]
+    sine = jnp.concatenate([own_sin, other_sin], axis=0)[:, lanes % (HEAD_DIM // 2)]
+    sine = jnp.where(lanes % HEAD_DIM < HEAD_DIM // 2, sine, -sine)
+    grad_residual, grad_res_low, grad_query, grad_kv, from_own, gain_pair = block_backward(
+        placed,
+        grad_back,
+        residual,
+        inverse_two,
+        gain_two.astype(f32)[None, :],
+        cotangent[0],
+        gathered,
+        flat_heads,
+        (allowed.astype(jnp.int32), mixed, log_rows),
+        (cosine, sine),
+        (row_values * inverse_one, other_low.astype(f32) * inverse_other),
+    )
+    came = lax.ppermute(grad_kv[token_count:], "seq", SWAP)
 
     feature = jnp.arange(model_width)[:, None]
     slot = jnp.arange(model_width)[None, :]
@@ -849,7 +987,6 @@
     chosen_half = chosen_half.astype(bf16)
     features = jnp.concatenate([normed_one, normed_other, mixed], axis=0)
     features = dot(features, chosen_half).astype(bf16)
-    gain_pair = jnp.stack([gain_one_grad, gain_two_grad], axis=0)
     gain_parts = jnp.concatenate(three_parts(gain_pair) + (jnp.zeros_like(gain_pair, bf16),), axis=0)
     gain_parts = dot(gain_parts, chosen_half).astype(bf16)
     gain_parts = jnp.stack([gain_parts[:, :half_width], gain_parts[:, half_width:]], axis=0)
@@ -857,7 +994,7 @@
         features[:, :half_width],
         features[:, half_width:],
         grad_query,
-        jnp.concatenate([grad_kv, away], axis=0),
+        grad_kv,
         grad_res_low,
         gain_parts,
     )

time: 306 us -> 309 us (level); the launches traced: 301 us -> 308 us
  matrix products: 36.3 us -> 23.5 us
  local copies, waits for them, and re-layouts: 26.3 us -> 38 us
  other arithmetic: 17.3 us -> 28.2 us
  waiting for transfers between devices: 45.5 us -> 36.4 us
  Pallas kernels: 146 us -> 151 us
    pallas_call x0 -> x1, Pallas kernels: none -> 12.3 us  [block_backward(): pl.pallas_call(block_backward_body, in_specs=[vmem] * 6 + [pl.BlockSpec(m...]
    dot_general x14 -> x10, matrix products: 31.8 us -> 21.6 us  [dot(): return lax.dot_general(a, b, dims, preferred_element_type=f32)]
    optimization_barrier x1 -> x0, local copies, waits for them, and re-layouts: 9.58 us -> none  [on_device(): gathered, grad_rows = lax.optimization_barrier((gathered, grad_rows))]
    all_to_all x4, waiting for transfers between devices: 42.1 us -> 33 us  [exchange(): lax.all_to_all(blocks, ('seq', 'chip'), split_axis=0, concat_axis=0, axis...]
    gather x0 -> x4, local copies, waits for them, and re-layouts: none -> 6.11 us  [the longest x2 3.06 us: on_device(): jnp.concatenate([own_sin, other_sin], axis=0)[:, lanes % (HEAD_DIM // 2)]]
    pallas_call x1, Pallas kernels: 51.3 us -> 46.2 us  [reduce_grads(): pl.pallas_call(reduce_body, in_specs=[pl.BlockSpec(memory_space=pltpu.VME...]
    unnamed x135 -> x107, local copies, waits for them, and re-layouts: 6.98 us -> 10.3 us
  transfers between devices with their start and end apart: 7 -> 7, of which waited for: 3 -> 3; matrix products, arithmetic and copies ran while one was open for 18% -> 25% of each run, Pallas kernels for 44% -> 45%
where the time goes in v6:
time: 309 us; the launch traced here: 308 us
  Pallas kernels  151 us (49%)
  local copies, waits for them, and re-layouts  38 us (12%)
  waiting for transfers between devices  36.4 us (12%)
  starting transfers between devices  29.3 us (9%)
  other arithmetic  28.2 us (9%)
  matrix products  23.5 us (8%)
    pallas_call x1, Pallas kernels, reduce_grads(): pl.pallas_call(reduce_body, in_specs=[pl.BlockSpec(memory_space=pltpu.VME...  46.2 us
    pallas_call x1, Pallas kernels, experts_second(): pl.pallas_call(experts_second_body, in_specs=[pl.BlockSpec(memory_space=p...  40.2 us
    pallas_call x1, Pallas kernels, gather_weights(): pl.pallas_call(gather_body, out_shape=jax.ShapeDtypeStruct((RING, RING, 2...  34 us
    all_to_all x4, waiting for transfers between devices, exchange(): lax.all_to_all(blocks, ('seq', 'chip'), split_axis=0, concat_axis=0, axis...  33 us
    all_to_all x4, starting transfers between devices, exchange(): lax.all_to_all(blocks, ('seq', 'chip'), split_axis=0, concat_axis=0, axis...  26.6 us
    dot_general x10, matrix products, dot(): return lax.dot_general(a, b, dims, preferred_element_type=f32)  21.6 us
    pallas_call x1, Pallas kernels, block_backward(): pl.pallas_call(block_backward_body, in_specs=[vmem] * 6 + [pl.BlockSpec(m...  12.3 us
    pallas_call x1, Pallas kernels, experts_first(): pl.pallas_call(experts_first_body, grid=(rows // ROW_BLOCK,), in_specs=[p...  11.9 us
  transfers between devices with their start and end apart: 7, of which 3 were waited for; matrix products, arithmetic and copies ran while one was open for 25% of the time, Pallas kernels for 45%

profile of v6, /device:TPU:0, one launch (start us, length us, event | category | flops | bytes accessed | tf_op | source)
XLA Modules:
  0.0 307.8 jit_solution(11738410284156157546)
XLA Ops:
  5.4 34.0 %gather_weights.1 = bf16[4,4,2,2,16,3200]{5,4,3,2,1,0:T(8,128)(2,1)} custom-call(bf16[16,3200]{1,0:T(8,128)(2,1)} %concatenate.64.shard_ref), custom_call_target="tpu_custom_call" | custom-call | bytes 52428800 | tf_op jit(solution)/shard_map/gather_weights/pallas_call | solution.py:380
  40.1 2.4 multiply_convert_fusion
  42.5 6.5 %all-to-all-start.1 = ((bf16[32,40,1024]{2,1,0:T(8,128)(2,1)}), bf16[32,40,1024]{2,1,0:T(8,128)(2,1)S(1)}, u32[]{:S(2)}, u32[]{:S(2)}) async-start(bf16[32,40,1024]{2,1,0:T(8,128)(2,1)} %bitcast.29), calls=%async_computation.1 | async-start | bytes 5242880 | tf_op jit(solution)/shard_map/all_to_all | solution.py:866
  49.2 2.0 convert_reduce_fusion
  52.8 2.9 fusion.2
  69.3 1.9 convert_multiply_fusion.3
  71.2 2.1 fusion.10
  80.9 2.1 multiply_reduce_fusion
  83.6 2.4 convolution_convert_fusion
  86.0 3.4 %all-to-all-done.1 = bf16[32,40,1024]{2,1,0:T(8,128)(2,1)S(1)} async-done(((bf16[32,40,1024]{2,1,0:T(8,128)(2,1)}), bf16[32,40,1024]{2,1,0:T(8,128)(2,1)S(1)}, u32[]{:S(2)}, u32[]{:S(2)}) %all-to-all-start.1) | async-done | bytes 2621472 | tf_op jit(solution)/shard_map/all_to_all | solution.py:866
  90.9 6.2 %all-to-all-start = ((bf16[32,40,1024]{2,1,0:T(8,128)(2,1)}), bf16[32,40,1024]{2,1,0:T(8,128)(2,1)}, u32[]{:S(2)}, u32[]{:S(2)}) async-start(bf16[32,40,1024]{2,1,0:T(8,128)(2,1)} %bitcast.27), calls=%async_computation | async-start | bytes 5242880 | tf_op jit(solution)/shard_map/all_to_all | solution.py:866
  98.9 3.4 %collective-permute-done.1 = bf16[768,1024]{1,0:T(8,128)(2,1)S(1)} collective-permute-done((bf16[768,1024]{1,0:T(8,128)(2,1)S(1)}, bf16[768,1024]{1,0:T(8,128)(2,1)S(1)}, u32[]{:S(2)}, u32[]{:S(2)}) %collective-permute-start.1) | collective-permute-done | bytes 1572896 | tf_op jit(solution)/shard_map/ppermute | solution.py:905
  105.4 29.6 %all-to-all-done = bf16[32,40,1024]{2,1,0:T(8,128)(2,1)} async-done(((bf16[32,40,1024]{2,1,0:T(8,128)(2,1)}), bf16[32,40,1024]{2,1,0:T(8,128)(2,1)}, u32[]{:S(2)}, u32[]{:S(2)}) %all-to-all-start) | async-done | bytes 2621472 | tf_op jit(solution)/shard_map/all_to_all | solution.py:866
  135.0 11.9 %experts_first.1 = (bf16[1280,512]{1,0:T(8,128)(2,1)}, bf16[1280,1024]{1,0:T(8,128)(2,1)}, bf16[1280,1024]{1,0:T(8,128)(2,1)}) custom-call(bf16[1280,1024]{1,0:T(8,128)(2,1)} %bitcast.28.x_ref, bf16[1280,1024]{1,0:T(8,128)(2,1)} %bitcast.121, bf16[1024,1024]{1,0:T(8,128)(2,1)} %pad_maximum_fusion.pre_w_ref, bf16[512,1024]{1,0:T(8,128)(2,1)} %pad_maximum_fusion.2.down_w_ref), custom_call_target="tpu_custom_call" | custom-call | flops 6710886400 | bytes 13107200 | tf_op jit(solution)/shard_map/experts_first/pallas_call | solution.py:122
  147.0 4.7 %all-to-all-start.2 = ((bf16[32,40,1024]{2,1,0:T(8,128)(2,1)}), bf16[32,40,1024]{2,1,0:T(8,128)(2,1)S(1)}, u32[]{:S(2)}, u32[]{:S(2)}) async-start(bf16[32,40,1024]{2,1,0:T(8,128)(2,1)} %bitcast.124), calls=%async_computation.2 | async-start | bytes 5242880 | tf_op jit(solution)/shard_map/all_to_all | solution.py:866
  168.8 3.1 fusion.12
  171.9 40.2 %experts_second.1 = (bf16[1280,1024]{1,0:T(8,128)(2,1)}, f32[256,1024]{1,0:T(8,128)}, f32[256,1024]{1,0:T(8,128)}, bf16[256,1024]{1,0:T(8,128)(2,1)}) custom-call(bf16[1280,1024]{1,0:T(8,128)(2,1)} %bitcast.28.x_ref, bf16[1280,1024]{1,0:T(8,128)(2,1)} %bitcast.122, bf16[1280,512]{1,0:T(8,128)(2,1)} %get-tuple-element.37.hidden_ref, ...), custom_call_target="tpu_custom_call" | custom-call | flops 5368709120 | bytes 52428800 | tf_op jit(solution)/shard_map/experts_second/pallas_call | solution.py:249
  213.7 9.2 %all-to-all-start.3 = ((bf16[32,40,1024]{2,1,0:T(8,128)(2,1)}), bf16[32,40,1024]{2,1,0:T(8,128)(2,1)}, u32[]{:S(2)}, u32[]{:S(2)}) async-start(bf16[32,40,1024]{2,1,0:T(8,128)(2,1)} %bitcast.123), calls=%async_computation.3 | async-start | bytes 5242880 | tf_op jit(solution)/shard_map/all_to_all | solution.py:866
  223.6 2.1 fusion.78
  225.7 12.3 %block_backward.1 = (f32[128,1024]{1,0:T(8,128)}, bf16[128,1024]{1,0:T(8,128)(2,1)}, bf16[128,1024]{1,0:T(8,128)(2,1)}, bf16[256,1024]{1,0:T(8,128)(2,1)}, f32[128,1024]{1,0:T(8,128)}, /*index=5*/f32[2,1024]{1,0:T(2,128)}) custom-call(bf16[1280,128]{1,0:T(8,128)(2,1)} %get-tuple-element.78.placed_ref, bf16[1280,1024]{1,0:T(8,128)(2,1)} %bitcast.117, ...), custom_call_target="tpu_custom_call" | custom-call | flops 3000000000 | bytes 12000000 | tf_op jit(solution)/shard_map/block_backward/pallas_call | solution.py:812
  241.8 6.3 %projection_grads.1 = (f32[512,3200]{1,0:T(8,128)}, bf16[512,3200]{1,0:T(8,128)(2,1)}) custom-call(bf16[384,512]{1,0:T(8,128)(2,1)} %get-tuple-element.64.mine_ref, bf16[384,512]{1,0:T(8,128)(2,1)} %get-tuple-element.63.sent_ref, bf16[128,1024]{1,0:T(8,128)(2,1)} %get-tuple-element.45.gq_ref, bf16[256,1024]{1,0:T(8,128)(2,1)} %get-tuple-element.44.gkv_ref, ...), custom_call_target="tpu_custom_call" | custom-call | tf_op jit(solution)/shard_map/projection_grads/pallas_call | solution.py:421
  248.1 46.2 %reduce_grads.1 = (f32[16,2048]{1,0:T(8,128)}, f32[16,1024]{1,0:T(8,128)}, f32[16,128]{1,0:T(8,128)}, f32[256,1024]{1,0:T(8,128)}) custom-call(f32[4,4,2,16,3200]{4,3,2,1,0:T(8,128)} %bitcast.118, bf16[4,4,2,16,3200]{4,3,2,1,0:T(8,128)(2,1)} %bitcast.120, bf16[256,1024]{1,0:T(8,128)(2,1)} %get-tuple-element.50.low), custom_call_target="tpu_custom_call" | custom-call | flops 1638400 | bytes 1638400 | tf_op jit(solution)/shard_map/reduce_grads/pallas_call | solution.py:652
  296.0 2.6 fusion.34
  299.6 3.0 fusion.19
  (199 shorter events, 65.8 us)
Async XLA Ops:
  0.6 67.4 %collective-permute-start = (bf16[128,1024]{1,0:T(8,128)(2,1)}, bf16[128,1024]{1,0:T(8,128)(2,1)}, u32[]{:S(2)}, u32[]{:S(2)}) collective-permute-start(bf16[128,1024]{1,0:T(8,128)(2,1)} %bitcast.119), channel_id=1, source_target_pairs={{0,64},{64,0},{1,65},{65,1},{2,66},{66,2},{3,67},{67,3},{4,68},{68... | collective-permute-start | bytes 786440 | tf_op jit(solution)/shard_map/ppermute | solution.py:899
  5.4 34.1 %copy-start.45 = (s32[1,128,8]{1,2,0:T(8,128)S(1)}, s32[1,128,8]{1,2,0:T(8,128)}, u32[]{:S(2)}) copy-start(s32[1,128,8]{1,2,0:T(8,128)} %param.20) | copy-start | bytes 12292
  5.4 34.4 %copy-start.46 = (f32[1,128,8]{1,2,0:T(8,128)S(1)}, f32[1,128,8]{1,2,0:T(8,128)}, u32[]{:S(2)}) copy-start(f32[1,128,8]{1,2,0:T(8,128)} %param.21) | copy-start | bytes 12292
  5.4 34.8 %copy-start.16 = (bf16[1,128,1024]{2,1,0:T(8,128)(2,1)S(1)}, bf16[1,128,1024]{2,1,0:T(8,128)(2,1)}, u32[]{:S(2)}) copy-start(bf16[1,128,1024]{2,1,0:T(8,128)(2,1)} %param.23) | copy-start | bytes 786436
  42.5 6.5 %copy-start.3 = (bf16[1,128,1024]{2,1,0:T(8,128)(2,1)S(1)}, bf16[1,128,1024]{2,1,0:T(8,128)(2,1)}, u32[]{:S(2)}) copy-start(bf16[1,128,1024]{2,1,0:T(8,128)(2,1)} %param.12) | copy-start | bytes 786436
  42.5 46.9 %all-to-all-start.1 = ((bf16[32,40,1024]{2,1,0:T(8,128)(2,1)}), bf16[32,40,1024]{2,1,0:T(8,128)(2,1)S(1)}, u32[]{:S(2)}, u32[]{:S(2)}) async-start(bf16[32,40,1024]{2,1,0:T(8,128)(2,1)} %bitcast.29), calls=%async_computation.1 | async-start | bytes 5242880 | tf_op jit(solution)/shard_map/all_to_all | solution.py:866
  55.7 6.4 %copy-start.49 = (s32[1,256]{1,0:T(1,128)S(1)}, s32[1,256]{1,0:T(1,128)}, u32[]{:S(2)}) copy-start(s32[1,256]{1,0:T(1,128)} %param.22) | copy-start | bytes 3076
  68.1 9.6 %copy-start.7 = (bf16[128,16,64]{0,2,1:T(8,128)(2,1)}, bf16[128,16,64]{0,2,1:T(8,128)(2,1)S(1)}, u32[]{:S(2)}) copy-start(bf16[128,16,64]{0,2,1:T(8,128)(2,1)S(1)} %maximum_convert_fusion) | copy-start | bytes 786436
  74.0 5.5 %copy-start.13 = (bf16[128,512]{1,0:T(8,128)(2,1)}, bf16[128,512]{1,0:T(8,128)(2,1)S(1)}, u32[]{:S(2)}) copy-start(bf16[128,512]{1,0:T(8,128)(2,1)S(1)} %slice.202) | copy-start | bytes 393220
  83.0 6.4 %copy-start.1 = (f32[128,1024]{1,0:T(8,128)}, f32[128,1024]{1,0:T(8,128)S(1)}, u32[]{:S(2)}) copy-start(f32[128,1024]{1,0:T(8,128)S(1)} %get-tuple-element.100.residual_ref) | copy-start | bytes 1572868
  90.9 44.1 %all-to-all-start = ((bf16[32,40,1024]{2,1,0:T(8,128)(2,1)}), bf16[32,40,1024]{2,1,0:T(8,128)(2,1)}, u32[]{:S(2)}, u32[]{:S(2)}) async-start(bf16[32,40,1024]{2,1,0:T(8,128)(2,1)} %bitcast.27), calls=%async_computation | async-start | bytes 5242880 | tf_op jit(solution)/shard_map/all_to_all | solution.py:866
  98.6 3.7 %collective-permute-start.1 = (bf16[768,1024]{1,0:T(8,128)(2,1)S(1)}, bf16[768,1024]{1,0:T(8,128)(2,1)S(1)}, u32[]{:S(2)}, u32[]{:S(2)}) collective-permute-start(bf16[768,1024]{1,0:T(8,128)(2,1)S(1)} %pad_maximum_fusion.1), channel_id=1, source_target_pairs={{0,1},{1,0},{2,3},{3,2},{4,5},{5,4},{6,7},{7,6},{8,9},{9,8},{10,11... | collective-permute-start | bytes 4718600 | tf_op jit(solution)/shard_map/ppermute | solution.py:905
  146.9 6.0 %copy-start.8 = (bf16[128,16,64]{0,2,1:T(8,128)(2,1)S(1)}, bf16[128,16,64]{0,2,1:T(8,128)(2,1)}, u32[]{:S(2)}) copy-start(bf16[128,16,64]{0,2,1:T(8,128)(2,1)} %copy-done.7) | copy-start | bytes 786436
  147.0 65.2 %all-to-all-start.2 = ((bf16[32,40,1024]{2,1,0:T(8,128)(2,1)}), bf16[32,40,1024]{2,1,0:T(8,128)(2,1)S(1)}, u32[]{:S(2)}, u32[]{:S(2)}) async-start(bf16[32,40,1024]{2,1,0:T(8,128)(2,1)} %bitcast.124), calls=%async_computation.2 | async-start | bytes 5242880 | tf_op jit(solution)/shard_map/all_to_all | solution.py:866
  152.9 6.4 %copy-start.32 = (f32[128,32]{0,1:T(8,128)S(1)}, f32[128,32]{0,1:T(8,128)}, u32[]{:S(2)}) copy-start(f32[128,32]{0,1:T(8,128)} %copy-done.31) | copy-start | bytes 49156
  152.9 11.8 %copy-start.6 = (bf16[8,64,2,128]{3,1,2,0:T(8,128)(2,1)S(1)}, bf16[8,64,2,128]{3,1,2,0:T(8,128)(2,1)}, u32[]{:S(2)}) copy-start(bf16[8,64,2,128]{3,1,2,0:T(8,128)(2,1)} %copy-done.5) | copy-start | bytes 786436
  153.8 11.9 %copy-start.50 = (f32[128,1]{0,1:T(1,128)S(1)}, f32[128,1]{0,1:T(1,128)}, u32[]{:S(2)}) copy-start(f32[128,1]{0,1:T(1,128)} %get-tuple-element.93) | copy-start | bytes 1540
  155.5 11.9 %copy-start.42 = (f32[2,8,128]{2,1,0:T(8,128)S(1)}, f32[2,8,128]{2,1,0:T(8,128)}, u32[]{:S(2)}) copy-start(f32[2,8,128]{2,1,0:T(8,128)} %copy-done.41) | copy-start | bytes 24580
  155.5 12.6 %copy-start.14 = (bf16[128,512]{1,0:T(8,128)(2,1)S(1)}, bf16[128,512]{1,0:T(8,128)(2,1)}, u32[]{:S(2)}) copy-start(bf16[128,512]{1,0:T(8,128)(2,1)} %copy-done.13) | copy-start | bytes 393220
  212.2 10.8 %copy-start.24 = (bf16[128,512]{1,0:T(8,128)(2,1)S(1)}, bf16[128,512]{1,0:T(8,128)(2,1)}, u32[]{:S(2)}) copy-start(bf16[128,512]{1,0:T(8,128)(2,1)} %copy.73) | copy-start | bytes 393220
  213.7 85.9 %all-to-all-start.3 = ((bf16[32,40,1024]{2,1,0:T(8,128)(2,1)}), bf16[32,40,1024]{2,1,0:T(8,128)(2,1)}, u32[]{:S(2)}, u32[]{:S(2)}) async-start(bf16[32,40,1024]{2,1,0:T(8,128)(2,1)} %bitcast.123), calls=%async_computation.3 | async-start | bytes 5242880 | tf_op jit(solution)/shard_map/all_to_all | solution.py:866
  239.0 56.3 %collective-permute-start.2 = (bf16[128,1024]{1,0:T(8,128)(2,1)S(1)}, bf16[128,1024]{1,0:T(8,128)(2,1)S(1)}, u32[]{:S(2)}, u32[]{:S(2)}) collective-permute-start(bf16[128,1024]{1,0:T(8,128)(2,1)S(1)} %slice.120), channel_id=1, source_target_pairs={{0,64},{64,0},{1,65},{65,1},{2,66},{66,2},{3,67},{67,3},{4,68},{68... | collective-permute-start | bytes 786440 | tf_op jit(solution)/shard_map/ppermute | solution.py:979
  248.1 47.9 %copy-start.9 = (f32[128,1024]{1,0:T(8,128)S(1)}, f32[128,1024]{1,0:T(8,128)}, u32[]{:S(2)}) copy-start(f32[128,1024]{1,0:T(8,128)} %get-tuple-element.43) | copy-start | bytes 1572868
  248.1 47.9 %copy-start.38 = (f32[1024]{0:T(1024)S(1)}, f32[1024]{0:T(1024)}, u32[]{:S(2)}) copy-start(f32[1024]{0:T(1024)} %copy-done.37) | copy-start | bytes 12292
  (34 other events, 81.7 us)

commit v7 on v6

--- a/solution.py
+++ b/solution.py
@@ -39,6 +39,14 @@
     inverse_freq = ROPE_BASE ** (-powers)
     angles = positions.astype(f32)[:, None] * inverse_freq[None, :]
     return (jnp.cos(angles), jnp.sin(angles))
+
+
+def wide_tables(positions):
+    place = jnp.arange(128) % HEAD_DIM
+    powers = (place % (HEAD_DIM // 2)).astype(f32) * (2.0 / HEAD_DIM)
+    angles = positions.astype(f32)[:, None] * (ROPE_BASE ** (-powers))[None, :]
+    sine = jnp.sin(angles)
+    return (jnp.cos(angles), jnp.where(place < HEAD_DIM // 2, sine, -sine))
 
 
 def rotate(values, cosine_table, sine_table, turn_sign):
@@ -396,7 +404,18 @@
     return out.reshape(4 * RING * RING * rows, width)
 
 
-def projection_grads_body(mine_ref, sent_ref, gq_ref, gkv_ref, gr_ref, gains_ref, total_ref, away_ref):
+def projection_grads_body(
+    mine_ref,
+    sent_ref,
+    gq_ref,
+    gkv_ref,
+    gr_ref,
+    gains_ref,
+    chosen_mine_ref,
+    chosen_sent_ref,
+    total_ref,
+    away_ref,
+):
     query = gq_ref.shape[1]
     width = query + gkv_ref.shape[1]
     wide = width + gr_ref.shape[1]
@@ -404,14 +423,19 @@
     lane = lax.broadcasted_iota(jnp.int32, (8, 128), 1)
     apart = ((spread == lane) & (spread < 6)).astype(bf16)
     tokens = gq_ref.shape[0]
-    for ref, out_ref, which in ((mine_ref, total_ref, 0), (sent_ref, away_ref, 1)):
+    halves = (
+        (mine_ref, total_ref, chosen_mine_ref),
+        (sent_ref, away_ref, chosen_sent_ref),
+    )
+    for ref, out_ref, chosen_ref in halves:
         out_ref[:, :query] = dot(ref[:tokens, :], gq_ref[...], TN).astype(out_ref.dtype)
         out_ref[:, query:width] = dot(ref[: 2 * tokens, :], gkv_ref[...], TN).astype(out_ref.dtype)
         out_ref[:, width:wide] = dot(ref[2 * tokens :, :], gr_ref[...], TN).astype(out_ref.dtype)
-        out_ref[:, wide:] = dot(gains_ref[which], apart, TN).astype(out_ref.dtype)
-
-
-def projection_grads(rows_mine, rows_sent, grad_query, grad_kv, grad_res_low, gains):
+        picked = dot(gains_ref[...], chosen_ref[...]).astype(bf16)
+        out_ref[:, wide:] = dot(picked, apart, TN).astype(out_ref.dtype)
+
+
+def projection_grads(rows_mine, rows_sent, grad_query, grad_kv, grad_res_low, gains, chosen):
     count = rows_mine.shape[1]
     width = grad_query.shape[1] + grad_kv.shape[1] + grad_res_low.shape[1] + 128
     tile = 128
@@ -427,7 +451,9 @@
             pl.BlockSpec(grad_query.shape, whole),
             pl.BlockSpec(grad_kv.shape, whole),
             pl.BlockSpec(grad_res_low.shape, whole),
-            pl.BlockSpec((2, 8, tile), lambda i: (0, 0, i)),
+            pl.BlockSpec(gains.shape, whole),
+            pl.BlockSpec((chosen.shape[0], tile), by_column),
+            pl.BlockSpec((chosen.shape[0], tile), lambda i: (0, i + count // tile)),
         ],
         out_specs=[pl.BlockSpec((tile, width), by_row), pl.BlockSpec((tile, width), by_row)],
         out_shape=[
@@ -435,7 +461,7 @@
             jax.ShapeDtypeStruct((count, width), bf16),
         ],
         name="projection_grads",
-    )(rows_mine, rows_sent, grad_query, grad_kv, grad_res_low, gains)
+    )(rows_mine, rows_sent, grad_query, grad_kv, grad_res_low, gains, chosen, chosen)
 
 
 def packed(values):
@@ -734,7 +760,7 @@
     residual = residual_ref[...]
     inverse = inverse_ref[...]
     upstream = dot(placed_ref[...], back_ref[...], TN)
-    gains_out[1:2, :] = jnp.sum(upstream * residual * inverse, axis=0, keepdims=True)
+    gain_two = jnp.sum(upstream * residual * inverse, axis=0, keepdims=True)
     scaled = upstream * gain_ref[...]
     coupling = jnp.mean(scaled * residual, axis=-1, keepdims=True)
     grad = inverse * scaled - residual * inverse * inverse * inverse * coupling
@@ -800,7 +826,12 @@
     from_out[...] = from_own
     gain = jnp.sum(from_own * own_ref[...], axis=0, keepdims=True)
     gain += jnp.sum(from_kv[tokens:] * other_ref[...], axis=0, keepdims=True)
-    gains_out[0:1, :] = gain
+    gains = jnp.concatenate([gain, gain_two], axis=0)
+    one = gains.astype(bf16).astype(f32)
+    two = (gains - one).astype(bf16).astype(f32)
+    three = gains - one - two
+    parts = jnp.concatenate([one, two, three, jnp.zeros_like(gains)], axis=0)
+    gains_out[...] = parts.astype(bf16)
 
 
 def block_backward(
@@ -819,7 +850,7 @@
             jax.ShapeDtypeStruct((tokens, width), bf16),
             jax.ShapeDtypeStruct((2 * tokens, 2 * keys.shape[1]), bf16),
             jax.ShapeDtypeStruct((tokens, width), f32),
-            jax.ShapeDtypeStruct((2, width), f32),
+            jax.ShapeDtypeStruct((8, width), bf16),
         ],
         scratch_shapes=[pltpu.VMEM(weights.shape, bf16), pltpu.SemaphoreType.DMA((2,))],
         cost_estimate=pl.CostEstimate(
@@ -951,33 +982,12 @@
     residual = row_values + dot(mixed, out_full)
     normed_two, inverse_two = norm_forward(residual, gain_two)
 
-    arrived = exchange(dot(placed, normed_two).astype(bf16))
-    hidden, grads, back = experts_first(arrived, grad_arrived, pre_w, down_w)
-    grad_back = exchange(back)
-    out_rows, gate_total, up_total, down_low = experts_second(arrived, grad_arrived, hidden, grads, down_w)
-    grad_back, out_rows = lax.optimization_barrier((grad_back, out_rows))
-    returned = exchange(out_rows)
+    rows = dot(placed, normed_two).astype(bf16)
+    rows, grad_arrived = lax.optimization_barrier((rows, grad_arrived))
+    arrived = exchange(rows)
 
     log_rows = log_total.reshape(HEADS, token_count).T
-    lanes = jnp.arange(128)
-    cosine = jnp.concatenate([own_cos, other_cos], axis=0)[:, lanes % (HEAD_DIM // 2)]
-    sine = jnp.concatenate([own_sin, other_sin], axis=0)[:, lanes % (HEAD_DIM // 2)]
-    sine = jnp.where(lanes % HEAD_DIM < HEAD_DIM // 2, sine, -sine)
-    grad_residual, grad_res_low, grad_query, grad_kv, from_own, gain_pair = block_backward(
-        placed,
-        grad_back,
-        residual,
-        inverse_two,
-        gain_two.astype(f32)[None, :],
-        cotangent[0],
-        gathered,
-        flat_heads,
-        (allowed.astype(jnp.int32), mixed, log_rows),
-        (cosine, sine),
-        (row_values * inverse_one, other_low.astype(f32) * inverse_other),
-    )
-    came = lax.ppermute(grad_kv[token_count:], "seq", SWAP)
-
+    cosine, sine = wide_tables(key_at)
     feature = jnp.arange(model_width)[:, None]
     slot = jnp.arange(model_width)[None, :]
     half_width = model_width // 2
@@ -987,16 +997,41 @@
     chosen_half = chosen_half.astype(bf16)
     features = jnp.concatenate([normed_one, normed_other, mixed], axis=0)
     features = dot(features, chosen_half).astype(bf16)
-    gain_parts = jnp.concatenate(three_parts(gain_pair) + (jnp.zeros_like(gain_pair, bf16),), axis=0)
-    gain_parts = dot(gain_parts, chosen_half).astype(bf16)
-    gain_parts = jnp.stack([gain_parts[:, :half_width], gain_parts[:, half_width:]], axis=0)
-    grads_mine, grads_sent = projection_grads(
+    ready = (
         features[:, :half_width],
         features[:, half_width:],
-        grad_query,
-        grad_kv,
-        grad_res_low,
-        gain_parts,
+        chosen_half,
+        flat_heads,
+        (allowed.astype(jnp.int32), mixed, log_rows),
+        (cosine, sine),
+        (row_values * inverse_one, other_low.astype(f32) * inverse_other),
+    )
+    arrived, ready = lax.optimization_barrier((arrived, ready))
+    features_mine, features_sent, chosen_half, flat_heads, masks, tables, scaled_inputs = ready
+
+    hidden, grads, back = experts_first(arrived, grad_arrived, pre_w, down_w)
+    grad_back = exchange(back)
+    out_rows, gate_total, up_total, down_low = experts_second(arrived, grad_arrived, hidden, grads, down_w)
+    grad_back, out_rows = lax.optimization_barrier((grad_back, out_rows))
+    returned = exchange(out_rows)
+
+    grad_residual, grad_res_low, grad_query, grad_kv, from_own, gain_parts = block_backward(
+        placed,
+        grad_back,
+        residual,
+        inverse_two,
+        gain_two.astype(f32)[None, :],
+        cotangent[0],
+        gathered,
+        flat_heads,
+        masks,
+        tables,
+        scaled_inputs,
+    )
+    came = lax.ppermute(grad_kv[token_count:], "seq", SWAP)
+
+    grads_mine, grads_sent = projection_grads(
+        features_mine, features_sent, grad_query, grad_kv, grad_res_low, gain_parts, chosen_half
     )
     in_width = query_width + 2 * kv_width
     in_total, out_total, gain_total, down_total = reduce_grads(

time: 309 us -> 286 us (0.926)
  local copies, waits for them, and re-layouts: 38 us -> 18.5 us
  other arithmetic: 28.2 us -> 18.2 us
  waiting for transfers between devices: 36.4 us -> 44.5 us
  Pallas kernels: 151 us -> 155 us
    all_to_all x4, waiting for transfers between devices: 33 us -> 44.5 us  [exchange(): lax.all_to_all(blocks, ('seq', 'chip'), split_axis=0, concat_axis=0, axis...]
    gather x4 -> x0, local copies, waits for them, and re-layouts: 6.11 us -> none  [the longest x2 3.06 us: on_device(): jnp.concatenate([own_sin, other_sin], axis=0)[:, lanes % (HEAD_DIM // 2)]]
    unnamed x107 -> x51, local copies, waits for them, and re-layouts: 10.3 us -> 5.82 us
    ppermute x1, waiting for transfers between devices: 3.4 us -> 0.01 us  [on_device(): other_units = lax.ppermute(own_units, 'core', SWAP)]
    dot_general x10 -> x9, matrix products: 21.6 us -> 19.9 us  [dot(): return lax.dot_general(a, b, dims, preferred_element_type=f32)]
  transfers between devices with their start and end apart: 7 -> 7, of which waited for: 3 -> 2; matrix products, arithmetic and copies ran while one was open for 25% -> 17% of each run, Pallas kernels for 45% -> 50%
where the time goes in v7:
time: 286 us; the launch traced here: 285 us
  Pallas kernels  155 us (54%)
  waiting for transfers between devices  44.5 us (16%)
  starting transfers between devices  26.7 us (9%)
  matrix products  20.9 us (7%)
  local copies, waits for them, and re-layouts  18.5 us (6%)
  other arithmetic  18.2 us (6%)
    pallas_call x1, Pallas kernels, reduce_grads(): pl.pallas_call(reduce_body, in_specs=[pl.BlockSpec(memory_space=pltpu.VME...  46.7 us
    all_to_all x4, waiting for transfers between devices, exchange(): lax.all_to_all(blocks, ('seq', 'chip'), split_axis=0, concat_axis=0, axis...  44.5 us
    pallas_call x1, Pallas kernels, experts_second(): pl.pallas_call(experts_second_body, in_specs=[pl.BlockSpec(memory_space=p...  42.3 us
    pallas_call x1, Pallas kernels, gather_weights(): pl.pallas_call(gather_body, out_shape=jax.ShapeDtypeStruct((RING, RING, 2...  34 us
    all_to_all x4, starting transfers between devices, exchange(): lax.all_to_all(blocks, ('seq', 'chip'), split_axis=0, concat_axis=0, axis...  24.9 us
    dot_general x9, matrix products, dot(): return lax.dot_general(a, b, dims, preferred_element_type=f32)  19.9 us
    pallas_call x1, Pallas kernels, block_backward(): pl.pallas_call(block_backward_body, in_specs=[vmem] * 6 + [pl.BlockSpec(m...  12.3 us
    pallas_call x1, Pallas kernels, experts_first(): pl.pallas_call(experts_first_body, grid=(rows // ROW_BLOCK,), in_specs=[p...  11.9 us
  transfers between devices with their start and end apart: 7, of which 2 were waited for; matrix products, arithmetic and copies ran while one was open for 17% of the time, Pallas kernels for 50%

profile of v7, /device:TPU:0, one launch (start us, length us, event | category | flops | bytes accessed | tf_op | source)
XLA Modules:
  0.0 284.7 jit_solution(602680711671252792)
XLA Ops:
  0.6 1.7 collective-permute-start
  3.8 1.6 concatenate.59.shard_ref
  5.4 34.0 %gather_weights.1 = bf16[4,4,2,2,16,3200]{5,4,3,2,1,0:T(8,128)(2,1)} custom-call(bf16[16,3200]{1,0:T(8,128)(2,1)} %concatenate.59.shard_ref), custom_call_target="tpu_custom_call" | custom-call | bytes 52428800 | tf_op jit(solution)/shard_map/gather_weights/pallas_call | solution.py:388
  40.1 2.3 multiply_convert_fusion
  42.4 6.6 %all-to-all-start = ((bf16[32,40,1024]{2,1,0:T(8,128)(2,1)}), bf16[32,40,1024]{2,1,0:T(8,128)(2,1)}, u32[]{:S(2)}, u32[]{:S(2)}) async-start(bf16[32,40,1024]{2,1,0:T(8,128)(2,1)} %bitcast.27), calls=%async_computation | async-start | bytes 5242880 | tf_op jit(solution)/shard_map/all_to_all | solution.py:897
  51.5 3.0 %fusion.2 = f32[128,2048]{1,0:T(8,128)S(1)} fusion(bf16[128,1024]{1,0:T(8,128)(2,1)S(1)} %get-tuple-element.106, bf16[1024,3200]{1,0:T(8,128)(2,1)} %bitcast.103), kind=kOutput, calls=%fused_computation.4 | convolution fusion | flops 536870912 | bytes 5505024 | tf_op jit(solution)/shard_map/dot_general | solution.py:33
  58.6 2.1 fusion.9
  62.5 2.2 multiply_reduce_fusion
  64.8 2.5 convolution_convert_fusion
  67.2 22.2 %all-to-all-done = bf16[32,40,1024]{2,1,0:T(8,128)(2,1)} async-done(((bf16[32,40,1024]{2,1,0:T(8,128)(2,1)}), bf16[32,40,1024]{2,1,0:T(8,128)(2,1)}, u32[]{:S(2)}, u32[]{:S(2)}) %all-to-all-start) | async-done | bytes 2621472 | tf_op jit(solution)/shard_map/all_to_all | solution.py:897
  89.4 5.0 %all-to-all-start.1 = ((bf16[32,40,1024]{2,1,0:T(8,128)(2,1)}), bf16[32,40,1024]{2,1,0:T(8,128)(2,1)}, u32[]{:S(2)}, u32[]{:S(2)}) async-start(bf16[32,40,1024]{2,1,0:T(8,128)(2,1)} %bitcast.29), calls=%async_computation.1 | async-start | bytes 5242880 | tf_op jit(solution)/shard_map/all_to_all | solution.py:897
  97.2 2.2 fusion.chosen_mine_ref.chosen_sent_ref
  101.9 2.1 fusion.11
  108.3 1.6 pad_maximum_fusion.pre_w_ref
  109.9 22.2 %all-to-all-done.1 = bf16[32,40,1024]{2,1,0:T(8,128)(2,1)} async-done(((bf16[32,40,1024]{2,1,0:T(8,128)(2,1)}), bf16[32,40,1024]{2,1,0:T(8,128)(2,1)}, u32[]{:S(2)}, u32[]{:S(2)}) %all-to-all-start.1) | async-done | bytes 2621472 | tf_op jit(solution)/shard_map/all_to_all | solution.py:897
  132.2 11.9 %experts_first.1 = (bf16[1280,512]{1,0:T(8,128)(2,1)}, bf16[1280,1024]{1,0:T(8,128)(2,1)}, bf16[1280,1024]{1,0:T(8,128)(2,1)}) custom-call(bf16[1280,1024]{1,0:T(8,128)(2,1)} %bitcast.30.x_ref, bf16[1280,1024]{1,0:T(8,128)(2,1)} %bitcast.28.g_ref, bf16[1024,1024]{1,0:T(8,128)(2,1)} %pad_maximum_fusion.pre_w_ref, bf16[512,1024]{1,0:T(8,128)(2,1)} %pad_maximum_fusion.2.down_w_ref), custom_call_target="tpu_custom_call" | custom-call | flops 6710886400 | bytes 13107200 | tf_op jit(solution)/shard_map/experts_first/pallas_call | solution.py:130
  144.1 4.1 %all-to-all-start.2 = ((bf16[32,40,1024]{2,1,0:T(8,128)(2,1)}), bf16[32,40,1024]{2,1,0:T(8,128)(2,1)S(1)}, u32[]{:S(2)}, u32[]{:S(2)}) async-start(bf16[32,40,1024]{2,1,0:T(8,128)(2,1)} %bitcast.116), calls=%async_computation.2 | async-start | bytes 5242880 | tf_op jit(solution)/shard_map/all_to_all | solution.py:897
  148.2 42.3 %experts_second.1 = (bf16[1280,1024]{1,0:T(8,128)(2,1)}, f32[256,1024]{1,0:T(8,128)}, f32[256,1024]{1,0:T(8,128)}, bf16[256,1024]{1,0:T(8,128)(2,1)}) custom-call(bf16[1280,1024]{1,0:T(8,128)(2,1)} %bitcast.30.x_ref, bf16[1280,1024]{1,0:T(8,128)(2,1)} %bitcast.28.g_ref, bf16[1280,512]{1,0:T(8,128)(2,1)} %get-tuple-element.56.hidden_ref, ...), custom_call_target="tpu_custom_call" | custom-call | flops 5368709120 | bytes 52428800 | tf_op jit(solution)/shard_map/experts_second/pallas_call | solution.py:257
  192.0 9.2 %all-to-all-start.3 = ((bf16[32,40,1024]{2,1,0:T(8,128)(2,1)}), bf16[32,40,1024]{2,1,0:T(8,128)(2,1)}, u32[]{:S(2)}, u32[]{:S(2)}) async-start(bf16[32,40,1024]{2,1,0:T(8,128)(2,1)} %bitcast.115), calls=%async_computation.3 | async-start | bytes 5242880 | tf_op jit(solution)/shard_map/all_to_all | solution.py:897
  203.7 12.3 %block_backward.1 = (f32[128,1024]{1,0:T(8,128)}, bf16[128,1024]{1,0:T(8,128)(2,1)}, bf16[128,1024]{1,0:T(8,128)(2,1)}, bf16[256,1024]{1,0:T(8,128)(2,1)}, f32[128,1024]{1,0:T(8,128)}, /*index=5*/bf16[8,1024]{1,0:T(8,128)(2,1)}) custom-call(bf16[1280,128]{1,0:T(8,128)(2,1)} %get-tuple-element.110.placed_ref, bf16[1280,1024]{1,0:T(8,128)(2,1)} %bitcast.108, ...), custom_call_target="tpu_custom_call" | custom-call | flops 3000000000 | bytes 12000000 | tf_op jit(solution)/shard_map/block_backward/pallas_call | solution.py:843
  217.4 7.4 %projection_grads.1 = (f32[512,3200]{1,0:T(8,128)}, bf16[512,3200]{1,0:T(8,128)(2,1)}) custom-call(bf16[384,512]{1,0:T(8,128)(2,1)} %get-tuple-element.74.mine_ref, bf16[384,512]{1,0:T(8,128)(2,1)} %get-tuple-element.75.sent_ref, bf16[128,1024]{1,0:T(8,128)(2,1)} %get-tuple-element.76.gq_ref, bf16[256,1024]{1,0:T(8,128)(2,1)} %get-tuple-element.73.gkv_ref, ...), custom_call_target="tpu_custom_call" | custom-call | tf_op jit(solution)/shard_map/projection_grads/pallas_call | solution.py:445
  224.8 46.7 %reduce_grads.1 = (f32[16,2048]{1,0:T(8,128)}, f32[16,1024]{1,0:T(8,128)}, f32[16,128]{1,0:T(8,128)}, f32[256,1024]{1,0:T(8,128)}) custom-call(f32[4,4,2,16,3200]{4,3,2,1,0:T(8,128)} %bitcast.109, bf16[4,4,2,16,3200]{4,3,2,1,0:T(8,128)(2,1)} %bitcast.114, bf16[256,1024]{1,0:T(8,128)(2,1)} %get-tuple-element.82.low), custom_call_target="tpu_custom_call" | custom-call | flops 1638400 | bytes 1638400 | tf_op jit(solution)/shard_map/reduce_grads/pallas_call | solution.py:678
  273.1 2.5 fusion.38
  276.6 3.0 %fusion.23 = f32[384,1024]{1,0:T(8,128)S(1)} fusion(bf16[1280,1024]{1,0:T(8,128)(2,1)} %bitcast.40, bf16[1280,128]{1,0:T(8,128)(2,1)S(1)} %get-tuple-element.108, bf16[1280,128]{1,0:T(8,128)(2,1)S(1)} %get-tuple-element.109, bf16[1280,128]{1,0:T(8,128)(2,1)S(1)} %get-tuple-element.107), kind=kOutput, calls=%fused_computation.28 | convolution fusion | flops 1009582080 | bytes 5177344 | tf_op jit(solution)/shard_map/dot_general | solution.py:33
  (132 shorter events, 32.7 us)
Async XLA Ops:
  0.6 56.9 %collective-permute-start = (bf16[128,1024]{1,0:T(8,128)(2,1)}, bf16[128,1024]{1,0:T(8,128)(2,1)S(1)}, u32[]{:S(2)}, u32[]{:S(2)}) collective-permute-start(bf16[128,1024]{1,0:T(8,128)(2,1)} %bitcast.110), channel_id=1, source_target_pairs={{0,64},{64,0},{1,65},{65,1},{2,66},{66,2},{3,67},{67,3},{4,68},{68... | collective-permute-start | bytes 786440 | tf_op jit(solution)/shard_map/ppermute | solution.py:930
  5.4 34.1 %copy-start.20 = (s32[1,128,8]{1,2,0:T(8,128)S(1)}, s32[1,128,8]{1,2,0:T(8,128)}, u32[]{:S(2)}) copy-start(s32[1,128,8]{1,2,0:T(8,128)} %param.20) | copy-start | bytes 12292
  5.4 34.4 %copy-start.21 = (f32[1,128,8]{1,2,0:T(8,128)S(1)}, f32[1,128,8]{1,2,0:T(8,128)}, u32[]{:S(2)}) copy-start(f32[1,128,8]{1,2,0:T(8,128)} %param.21) | copy-start | bytes 12292
  5.4 34.8 %copy-start.9 = (bf16[1,128,1024]{2,1,0:T(8,128)(2,1)S(1)}, bf16[1,128,1024]{2,1,0:T(8,128)(2,1)}, u32[]{:S(2)}) copy-start(bf16[1,128,1024]{2,1,0:T(8,128)(2,1)} %param.23) | copy-start | bytes 786436
  42.4 6.6 %copy-start.3 = (bf16[1,128,1024]{2,1,0:T(8,128)(2,1)S(1)}, bf16[1,128,1024]{2,1,0:T(8,128)(2,1)}, u32[]{:S(2)}) copy-start(bf16[1,128,1024]{2,1,0:T(8,128)(2,1)} %param.12) | copy-start | bytes 786436
  42.4 47.0 %all-to-all-start = ((bf16[32,40,1024]{2,1,0:T(8,128)(2,1)}), bf16[32,40,1024]{2,1,0:T(8,128)(2,1)}, u32[]{:S(2)}, u32[]{:S(2)}) async-start(bf16[32,40,1024]{2,1,0:T(8,128)(2,1)} %bitcast.27), calls=%async_computation | async-start | bytes 5242880 | tf_op jit(solution)/shard_map/all_to_all | solution.py:897
  50.6 14.1 %copy-start.19 = (f32[1024]{0:T(1024)}, f32[1024]{0:T(1024)S(1)}, u32[]{:S(2)}) copy-start(f32[1024]{0:T(1024)S(1)} %get-tuple-element.91) | copy-start | bytes 12292
  51.5 3.0 %copy-start.15 = (bf16[128,1024]{1,0:T(8,128)(2,1)}, bf16[128,1024]{1,0:T(8,128)(2,1)S(1)}, u32[]{:S(2)}) copy-start(bf16[128,1024]{1,0:T(8,128)(2,1)S(1)} %get-tuple-element.106) | copy-start | bytes 786436
  62.5 36.9 %copy-start.4 = (bf16[8,64,2,128]{3,1,2,0:T(8,128)(2,1)}, bf16[8,64,2,128]{3,1,2,0:T(8,128)(2,1)S(1)}, u32[]{:S(2)}) copy-start(bf16[8,64,2,128]{3,1,2,0:T(8,128)(2,1)S(1)} %convolution_convert_fusion.1) | copy-start | bytes 786436
  64.7 24.7 %copy-start.1 = (f32[128,1024]{1,0:T(8,128)}, f32[128,1024]{1,0:T(8,128)S(1)}, u32[]{:S(2)}) copy-start(f32[128,1024]{1,0:T(8,128)S(1)} %get-tuple-element.131.residual_ref) | copy-start | bytes 1572868
  89.4 5.0 %copy-start.6 = (bf16[256,1024]{1,0:T(8,128)(2,1)S(1)}, bf16[256,1024]{1,0:T(8,128)(2,1)}, u32[]{:S(2)}) copy-start(bf16[256,1024]{1,0:T(8,128)(2,1)} %param.19) | copy-start | bytes 1572868
  89.4 5.0 %copy-start.7 = (bf16[256,1024]{1,0:T(8,128)(2,1)S(1)}, bf16[256,1024]{1,0:T(8,128)(2,1)}, u32[]{:S(2)}) copy-start(bf16[256,1024]{1,0:T(8,128)(2,1)} %param.18) | copy-start | bytes 1572868
  89.4 5.0 %copy-start.8 = (bf16[256,1024]{1,0:T(8,128)(2,1)S(1)}, bf16[256,1024]{1,0:T(8,128)(2,1)}, u32[]{:S(2)}) copy-start(bf16[256,1024]{1,0:T(8,128)(2,1)} %param.17) | copy-start | bytes 1572868
  89.4 42.7 %all-to-all-start.1 = ((bf16[32,40,1024]{2,1,0:T(8,128)(2,1)}), bf16[32,40,1024]{2,1,0:T(8,128)(2,1)}, u32[]{:S(2)}, u32[]{:S(2)}) async-start(bf16[32,40,1024]{2,1,0:T(8,128)(2,1)} %bitcast.29), calls=%async_computation.1 | async-start | bytes 5242880 | tf_op jit(solution)/shard_map/all_to_all | solution.py:897
  95.7 9.2 %collective-permute-start.1 = (bf16[768,1024]{1,0:T(8,128)(2,1)}, bf16[768,1024]{1,0:T(8,128)(2,1)}, u32[]{:S(2)}, u32[]{:S(2)}) collective-permute-start(bf16[768,1024]{1,0:T(8,128)(2,1)} %pad_maximum_fusion.1), channel_id=1, source_target_pairs={{0,1},{1,0},{2,3},{3,2},{4,5},{5,4},{6,7},{7,6},{8,9},{9,8},{10,11... | collective-permute-start | bytes 4718600 | tf_op jit(solution)/shard_map/ppermute | solution.py:936
  144.1 46.4 %all-to-all-start.2 = ((bf16[32,40,1024]{2,1,0:T(8,128)(2,1)}), bf16[32,40,1024]{2,1,0:T(8,128)(2,1)S(1)}, u32[]{:S(2)}, u32[]{:S(2)}) async-start(bf16[32,40,1024]{2,1,0:T(8,128)(2,1)} %bitcast.116), calls=%async_computation.2 | async-start | bytes 5242880 | tf_op jit(solution)/shard_map/all_to_all | solution.py:897
  190.5 12.3 %copy-start.5 = (bf16[8,64,2,128]{3,1,2,0:T(8,128)(2,1)S(1)}, bf16[8,64,2,128]{3,1,2,0:T(8,128)(2,1)}, u32[]{:S(2)}) copy-start(bf16[8,64,2,128]{3,1,2,0:T(8,128)(2,1)} %copy-done.4) | copy-start | bytes 786436
  192.0 84.6 %all-to-all-start.3 = ((bf16[32,40,1024]{2,1,0:T(8,128)(2,1)}), bf16[32,40,1024]{2,1,0:T(8,128)(2,1)}, u32[]{:S(2)}, u32[]{:S(2)}) async-start(bf16[32,40,1024]{2,1,0:T(8,128)(2,1)} %bitcast.115), calls=%async_computation.3 | async-start | bytes 5242880 | tf_op jit(solution)/shard_map/all_to_all | solution.py:897
  216.9 55.5 %collective-permute-start.2 = (bf16[128,1024]{1,0:T(8,128)(2,1)S(1)}, bf16[128,1024]{1,0:T(8,128)(2,1)S(1)}, u32[]{:S(2)}, u32[]{:S(2)}) collective-permute-start(bf16[128,1024]{1,0:T(8,128)(2,1)S(1)} %slice.116), channel_id=1, source_target_pairs={{0,64},{64,0},{1,65},{65,1},{2,66},{66,2},{3,67},{67,3},{4,68},{68... | collective-permute-start | bytes 786440 | tf_op jit(solution)/shard_map/ppermute | solution.py:1031
  224.8 48.3 %copy-start.13 = (f32[128,1024]{1,0:T(8,128)S(1)}, f32[128,1024]{1,0:T(8,128)}, u32[]{:S(2)}) copy-start(f32[128,1024]{1,0:T(8,128)} %get-tuple-element.72) | copy-start | bytes 1572868
  271.5 4.1 %copy-start.14 = (f32[128,1024]{1,0:T(8,128)S(1)}, f32[128,1024]{1,0:T(8,128)}, u32[]{:S(2)}) copy-start(f32[128,1024]{1,0:T(8,128)} %get-tuple-element.71) | copy-start | bytes 1572868
  276.6 3.0 %copy-start.2 = (f32[128,1024]{1,0:T(8,128)S(1)}, f32[128,1024]{1,0:T(8,128)}, u32[]{:S(2)}) copy-start(f32[128,1024]{1,0:T(8,128)} %copy-done.1) | copy-start | bytes 1572868
  279.6 2.2 copy-start.11
  279.6 3.1 %copy-start.10 = (f32[256,1024]{1,0:T(8,128)S(1)}, f32[256,1024]{1,0:T(8,128)}, u32[]{:S(2)}) copy-start(f32[256,1024]{1,0:T(8,128)} %get-tuple-element.154) | copy-start | bytes 3145732
  (6 other events, 8.9 us)

commit v8 on v7

--- a/solution.py
+++ b/solution.py
@@ -162,9 +162,8 @@
     grads_ref,
     down_w_ref,
     out_ref,
-    gate_ref,
-    up_ref,
-    third_ref,
+    total_ref,
+    rest_ref,
     theirs,
     came,
     last,
@@ -206,9 +205,9 @@
             target[:, columns] = dot(left[:, at : at + BLOCK], right[:, columns], TN)
 
     away = [send(k, theirs.at[k], came.at[k], partner) for k in range(3)]
-    across = [send(3 + k, low.at[k], low_came.at[k], mirror) for k in range(2)]
-    mine = [gate_ref, up_ref, last]
-    lows = [low.at[0], low.at[1], third_ref]
+    across = [send(3 + k, low.at[k], low_came.at[k], mirror) for k in range(1)]
+    mine = [total_ref, last.at[0], last.at[1]]
+    lows = [low.at[0], rest_ref.at[0], rest_ref.at[1]]
     for k in range(3):
         unit_grads(1, k, theirs.at[k])
         if k:
@@ -228,6 +227,7 @@
         join(k)
         if k < 2:
             unit_grads(0, k + 1, mine[k + 1])
+        if k < len(across):
             across[k].start()
 
     @pl.loop(0, x_ref.shape[0] // ROW_BLOCK)
@@ -240,7 +240,7 @@
             out = part if out is None else out + part
         out_ref[rows, :] = out.astype(bf16)
 
-    for k in range(2):
+    for k in range(len(across)):
         across[k].wait_recv()
 
         @pl.loop(0, BLOCK // 32)
@@ -257,21 +257,20 @@
     return pl.pallas_call(
         experts_second_body,
         in_specs=[pl.BlockSpec(memory_space=pltpu.VMEM)] * 5,
-        out_specs=[pl.BlockSpec(memory_space=pltpu.VMEM)] * 4,
+        out_specs=[pl.BlockSpec(memory_space=pltpu.VMEM)] * 3,
         out_shape=[
             jax.ShapeDtypeStruct((rows, width), bf16),
             jax.ShapeDtypeStruct((BLOCK, width), f32),
-            jax.ShapeDtypeStruct((BLOCK, width), f32),
-            jax.ShapeDtypeStruct((BLOCK, width), bf16),
+            jax.ShapeDtypeStruct((2, BLOCK, width), bf16),
         ],
         scratch_shapes=[
             pltpu.VMEM((3, BLOCK, width), f32),
             pltpu.VMEM((3, BLOCK, width), f32),
-            pltpu.VMEM((BLOCK, width), f32),
-            pltpu.VMEM((2, BLOCK, width), bf16),
-            pltpu.VMEM((2, BLOCK, width), bf16),
-            pltpu.SemaphoreType.DMA((5,)),
-            pltpu.SemaphoreType.DMA((5,)),
+            pltpu.VMEM((2, BLOCK, width), f32),
+            pltpu.VMEM((1, BLOCK, width), bf16),
+            pltpu.VMEM((1, BLOCK, width), bf16),
+            pltpu.SemaphoreType.DMA((4,)),
+            pltpu.SemaphoreType.DMA((4,)),
         ],
         compiler_params=pltpu.CompilerParams(collective_id=1, has_side_effects=True),
         cost_estimate=pl.CostEstimate(
@@ -283,7 +282,7 @@
     )(arrived, grad_arrived, hidden, grads, down_w)
 
 
-def gather_body(shard_ref, out_ref, send_sem, recv_sem, local_sem):
+def gather_body(in_ref, project_ref, gains_ref, out_ref, shard_ref, send_sem, recv_sem, local_sem):
     seq, chip, core = (lax.axis_index(name) for name in ("seq", "chip", "core"))
     y, z, half = (chip // (2 * RING), (chip // 2) % RING, chip % 2)
 
@@ -299,6 +298,11 @@
     partner = device(y, z, half, 1 - core)
     across = (1 - seq, chip + 1 - 2 * half, core)
     ahead, behind = (1, RING - 1)
+    cut = in_ref.shape[1]
+    wide = cut + project_ref.shape[1]
+    shard_ref[:, :cut] = in_ref[...]
+    shard_ref[:, cut:wide] = project_ref[...]
+    shard_ref[:, wide:] = gains_ref[...]
     barrier = pltpu.get_barrier_semaphore()
     for other in (partner, across, first(ahead), first(behind), last(ahead), last(behind)):
         pl.semaphore_signal(barrier, inc=1, device_id=other, device_id_type=MESH_ID)
@@ -383,14 +387,16 @@
         pl.when(core == c)(lambda c=c: run(c))
 
 
-def gather_weights(shard):
-    rows, width = shard.shape
+def gather_weights(project_in, project_out, gains):
+    parts = (project_in, project_out, gains)
+    rows, width = (gains.shape[0], sum(part.shape[1] for part in parts))
     out = pl.pallas_call(
         gather_body,
-        out_shape=jax.ShapeDtypeStruct((RING, RING, 2, 2, rows, width), shard.dtype),
-        in_specs=[pl.BlockSpec(memory_space=pltpu.VMEM)],
+        out_shape=jax.ShapeDtypeStruct((RING, RING, 2, 2, rows, width), bf16),
+        in_specs=[pl.BlockSpec(memory_space=pltpu.VMEM)] * 3,
         out_specs=pl.BlockSpec(memory_space=pl.ANY),
         scratch_shapes=[
+            pltpu.VMEM((rows, width), bf16),
             pltpu.SemaphoreType.DMA((41,)),
             pltpu.SemaphoreType.DMA((41,)),
             pltpu.SemaphoreType.DMA,
@@ -400,7 +406,7 @@
             flops=0, bytes_accessed=rows * width * 2 * 4 * RING * RING * 8, transcendentals=0
         ),
         name="gather_weights",
-    )(shard)
+    )(*parts)
     return out.reshape(4 * RING * RING * rows, width)
 
 
@@ -478,13 +484,14 @@
 
 
 def reduce_body(
-    mine,
+    mine_hbm,
     sent,
     low,
     in_ref,
     out_ref,
     gain_ref,
-    unit_ref,
+    up_ref,
+    down_ref,
     came,
     acc,
     stage,
@@ -498,6 +505,8 @@
     own,
     in_own,
     low_came,
+    mine,
+    mine_sem,
     chip_send,
     chip_recv,
     ring_send,
@@ -522,6 +531,8 @@
     across = (1 - seq, chip + 1 - 2 * half, core)
     mirror = (1 - seq, chip, core)
     ahead, behind = (1, RING - 1)
+    fetch = pltpu.make_async_copy(mine_hbm, mine, mine_sem)
+    fetch.start()
     barrier = pltpu.get_barrier_semaphore()
     others = (partner, across, mirror, first(ahead), first(behind), last(ahead), last(behind))
     for other in others:
@@ -592,6 +603,7 @@
                 if not to_stage or s != 2:
                     acc[s, j, h] = value
 
+    fetch.wait()
     merge(2, 0, RING, True)
     ring[0].start()
     ring[1].start()
@@ -647,10 +659,11 @@
     ring[11].start()
     units.wait_recv()
 
-    @pl.loop(0, low.shape[0] // 32)
+    @pl.loop(0, low.shape[1] // 32)
     def _(r):
         rows = pl.ds(pl.multiple_of(r * 32, 32), 32)
-        unit_ref[rows, :] = low[rows, :].astype(f32) + low_came[rows, :].astype(f32)
+        up_ref[rows, :] = low[0, rows, :].astype(f32) + low_came[0, rows, :].astype(f32)
+        down_ref[rows, :] = low[1, rows, :].astype(f32) + low_came[1, rows, :].astype(f32)
 
     ring[11].wait_recv()
     total = own[...] + in_own[...]
@@ -677,13 +690,14 @@
     pair = (2, share, width)
     return pl.pallas_call(
         reduce_body,
-        in_specs=[pl.BlockSpec(memory_space=pltpu.VMEM)] * 3,
-        out_specs=[pl.BlockSpec(memory_space=pltpu.VMEM)] * 4,
+        in_specs=[pl.BlockSpec(memory_space=pl.ANY)] * 2 + [pl.BlockSpec(memory_space=pltpu.VMEM)],
+        out_specs=[pl.BlockSpec(memory_space=pltpu.VMEM)] * 5,
         out_shape=[
             jax.ShapeDtypeStruct((share, cut), f32),
             jax.ShapeDtypeStruct((share, width - cut - 128), f32),
             jax.ShapeDtypeStruct((share, 128), f32),
-            jax.ShapeDtypeStruct(low.shape, f32),
+            jax.ShapeDtypeStruct(low.shape[1:], f32),
+            jax.ShapeDtypeStruct(low.shape[1:], f32),
         ],
         scratch_shapes=[
             pltpu.VMEM(shape, bf16),
@@ -699,6 +713,8 @@
             pltpu.VMEM((share, width), f32),
             pltpu.VMEM((share, width), f32),
             pltpu.VMEM(low.shape, bf16),
+            pltpu.VMEM(shape, f32),
+            pltpu.SemaphoreType.DMA,
             pltpu.SemaphoreType.DMA((RING, RING)),
             pltpu.SemaphoreType.DMA((RING, RING)),
             pltpu.SemaphoreType.DMA((13,)),
@@ -706,7 +722,7 @@
         ],
         compiler_params=pltpu.CompilerParams(collective_id=2, has_side_effects=True),
         cost_estimate=pl.CostEstimate(
-            flops=mine.size, bytes_accessed=mine.size, transcendentals=0
+            flops=mine.size * 8, bytes_accessed=mine.size * 60, transcendentals=0
         ),
         name="reduce_grads",
     )(mine.reshape(shape), sent.reshape(shape), low)
@@ -939,17 +955,15 @@
 
     share = gain_attend.shape[0]
     wide = query_width + 2 * kv_width + query_width
-    filler = jnp.zeros((share, 126), bf16)
-    gathered = gather_weights(
-        jnp.concatenate(
-            [project_in, project_out, gain_attend[:, None], gain_expert[:, None], filler], axis=1
-        )
-    )
+    gain_rows = jnp.stack([gain_attend, gain_expert], axis=0)
+    gain_rows = jnp.pad(gain_rows, ((0, share - 2), (0, 128 - share)))
+    gathered = gather_weights(project_in, project_out, gain_rows)
     gathered, grad_rows = lax.optimization_barrier((gathered, grad_rows))
     grad_arrived = exchange(grad_rows)
     in_full = gathered[:, : query_width + 2 * kv_width]
     out_full = gathered[:, query_width + 2 * kv_width : wide]
-    gain_one, gain_two = (gathered[:, wide], gathered[:, wide + 1])
+    gain_rows = gathered[:, wide : wide + share].reshape(-1, share, share)
+    gain_one, gain_two = (gain_rows[:, 0].reshape(-1), gain_rows[:, 1].reshape(-1))
 
     row_values = own_low.astype(f32)
     normed_one, inverse_one = norm_forward(row_values, gain_one)
@@ -1011,7 +1025,7 @@
 
     hidden, grads, back = experts_first(arrived, grad_arrived, pre_w, down_w)
     grad_back = exchange(back)
-    out_rows, gate_total, up_total, down_low = experts_second(arrived, grad_arrived, hidden, grads, down_w)
+    out_rows, gate_total, rest_low = experts_second(arrived, grad_arrived, hidden, grads, down_w)
     grad_back, out_rows = lax.optimization_barrier((grad_back, out_rows))
     returned = exchange(out_rows)
 
@@ -1034,8 +1048,8 @@
         features_mine, features_sent, grad_query, grad_kv, grad_res_low, gain_parts, chosen_half
     )
     in_width = query_width + 2 * kv_width
-    in_total, out_total, gain_total, down_total = reduce_grads(
-        grads_mine, grads_sent, down_low, in_width
+    in_total, out_total, gain_total, up_total, down_total = reduce_grads(
+        grads_mine, grads_sent, rest_low, in_width
     )
     gain_total = gain_total[:, :2] + gain_total[:, 2:4] + gain_total[:, 4:6]
 

time: 286 us -> 278 us (0.972)
  Pallas kernels: 155 us -> 139 us
  waiting for transfers between devices: 44.5 us -> 49 us
    pallas_call x1, Pallas kernels: 42.3 us -> 30.5 us  [experts_second(): pl.pallas_call(experts_second_body, in_specs=[pl.BlockSpec(memory_space=p...]
    ppermute x1, starting transfers between devices: 0.2 us -> 7.03 us  [on_device(): came = lax.ppermute(grad_kv[token_count:], 'seq', SWAP)]
    all_to_all x4, waiting for transfers between devices: 44.5 us -> 49 us  [exchange(): lax.all_to_all(blocks, ('seq', 'chip'), split_axis=0, concat_axis=0, axis...]
    all_to_all x4, starting transfers between devices: 24.9 us -> 20.7 us  [exchange(): lax.all_to_all(blocks, ('seq', 'chip'), split_axis=0, concat_axis=0, axis...]
    pallas_call x1, Pallas kernels: 46.7 us -> 43.1 us  [reduce_grads(): pl.pallas_call(reduce_body, in_specs=[pl.BlockSpec(memory_space=pl.ANY)]...]
    unnamed x51 -> x45, local copies, waits for them, and re-layouts: 5.82 us -> 5.85 us
  transfers between devices with their start and end apart: 7 -> 7, of which waited for: 2 -> 3; matrix products, arithmetic and copies ran while one was open for 17% -> 17% of each run, Pallas kernels for 50% -> 46%
where the time goes in v8:
time: 278 us; the launch traced here: 276 us
  Pallas kernels  139 us (50%)
  waiting for transfers between devices  49 us (18%)
  starting transfers between devices  29.3 us (11%)
  matrix products  20.8 us (7%)
  other arithmetic  19.6 us (7%)
  local copies, waits for them, and re-layouts  17.3 us (6%)
    all_to_all x4, waiting for transfers between devices, exchange(): lax.all_to_all(blocks, ('seq', 'chip'), split_axis=0, concat_axis=0, axis...  49 us
    pallas_call x1, Pallas kernels, reduce_grads(): pl.pallas_call(reduce_body, in_specs=[pl.BlockSpec(memory_space=pl.ANY)]...  43.1 us
    pallas_call x1, Pallas kernels, gather_weights(): pl.pallas_call(gather_body, out_shape=jax.ShapeDtypeStruct((RING, RING, 2...  34 us
    pallas_call x1, Pallas kernels, experts_second(): pl.pallas_call(experts_second_body, in_specs=[pl.BlockSpec(memory_space=p...  30.5 us
    all_to_all x4, starting transfers between devices, exchange(): lax.all_to_all(blocks, ('seq', 'chip'), split_axis=0, concat_axis=0, axis...  20.7 us
    dot_general x9, matrix products, dot(): return lax.dot_general(a, b, dims, preferred_element_type=f32)  19.8 us
    pallas_call x1, Pallas kernels, block_backward(): pl.pallas_call(block_backward_body, in_specs=[vmem] * 6 + [pl.BlockSpec(m...  12.2 us
    pallas_call x1, Pallas kernels, experts_first(): pl.pallas_call(experts_first_body, grid=(rows // ROW_BLOCK,), in_specs=[p...  11.9 us
  transfers between devices with their start and end apart: 7, of which 3 were waited for; matrix products, arithmetic and copies ran while one was open for 17% of the time, Pallas kernels for 46%

profile of v8, /device:TPU:0, one launch (start us, length us, event | category | flops | bytes accessed | tf_op | source)
XLA Modules:
  0.0 276.5 jit_solution(8309322411053175675)
XLA Ops:
  0.6 1.7 collective-permute-start
  5.6 34.0 %gather_weights.1 = bf16[4,4,2,2,16,3200]{5,4,3,2,1,0:T(8,128)(2,1)} custom-call(bf16[16,2048]{1,0:T(8,128)(2,1)} %in_ref.1, bf16[16,1024]{1,0:T(8,128)(2,1)} %project_ref.1, bf16[16,128]{1,0:T(8,128)(2,1)} %fusion.59.gains_ref), custom_call_target="tpu_custom_call" | custom-call | bytes 52428800 | tf_op jit(solution)/shard_map/gather_weights/pallas_call | solution.py:393
  39.7 2.3 multiply_convert_fusion
  42.0 6.6 %all-to-all-start = ((bf16[32,40,1024]{2,1,0:T(8,128)(2,1)}), bf16[32,40,1024]{2,1,0:T(8,128)(2,1)}, u32[]{:S(2)}, u32[]{:S(2)}) async-start(bf16[32,40,1024]{2,1,0:T(8,128)(2,1)} %bitcast.28), calls=%async_computation | async-start | bytes 5242880 | tf_op jit(solution)/shard_map/all_to_all | solution.py:913
  50.8 3.0 %fusion.2 = f32[128,2048]{1,0:T(8,128)S(1)} fusion(bf16[128,1024]{1,0:T(8,128)(2,1)S(1)} %get-tuple-element.104, bf16[1024,3200]{1,0:T(8,128)(2,1)} %bitcast.109), kind=kOutput, calls=%fused_computation.4 | convolution fusion | flops 536870912 | bytes 5505024 | tf_op jit(solution)/shard_map/dot_general | solution.py:33
  58.0 2.1 fusion.9
  61.9 2.2 multiply_reduce_fusion
  64.1 2.4 convolution_convert_fusion
  66.5 22.5 %all-to-all-done = bf16[32,40,1024]{2,1,0:T(8,128)(2,1)} async-done(((bf16[32,40,1024]{2,1,0:T(8,128)(2,1)}), bf16[32,40,1024]{2,1,0:T(8,128)(2,1)}, u32[]{:S(2)}, u32[]{:S(2)}) %all-to-all-start) | async-done | bytes 2621472 | tf_op jit(solution)/shard_map/all_to_all | solution.py:913
  89.1 4.9 %all-to-all-start.1 = ((bf16[32,40,1024]{2,1,0:T(8,128)(2,1)}), bf16[32,40,1024]{2,1,0:T(8,128)(2,1)}, u32[]{:S(2)}, u32[]{:S(2)}) async-start(bf16[32,40,1024]{2,1,0:T(8,128)(2,1)} %bitcast.30), calls=%async_computation.1 | async-start | bytes 5242880 | tf_op jit(solution)/shard_map/all_to_all | solution.py:913
  96.8 2.2 fusion.chosen_mine_ref.chosen_sent_ref
  101.5 2.1 fusion.11
  109.5 22.3 %all-to-all-done.1 = bf16[32,40,1024]{2,1,0:T(8,128)(2,1)} async-done(((bf16[32,40,1024]{2,1,0:T(8,128)(2,1)}), bf16[32,40,1024]{2,1,0:T(8,128)(2,1)}, u32[]{:S(2)}, u32[]{:S(2)}) %all-to-all-start.1) | async-done | bytes 2621472 | tf_op jit(solution)/shard_map/all_to_all | solution.py:913
  131.8 11.9 %experts_first.1 = (bf16[1280,512]{1,0:T(8,128)(2,1)}, bf16[1280,1024]{1,0:T(8,128)(2,1)}, bf16[1280,1024]{1,0:T(8,128)(2,1)}) custom-call(bf16[1280,1024]{1,0:T(8,128)(2,1)} %bitcast.31.x_ref, bf16[1280,1024]{1,0:T(8,128)(2,1)} %bitcast.29.g_ref, bf16[1024,1024]{1,0:T(8,128)(2,1)} %pad_maximum_fusion.pre_w_ref, bf16[512,1024]{1,0:T(8,128)(2,1)} %pad_maximum_fusion.2.down_w_ref), custom_call_target="tpu_custom_call" | custom-call | flops 6710886400 | bytes 13107200 | tf_op jit(solution)/shard_map/experts_first/pallas_call | solution.py:130
  143.8 4.1 %all-to-all-start.2 = ((bf16[32,40,1024]{2,1,0:T(8,128)(2,1)}), bf16[32,40,1024]{2,1,0:T(8,128)(2,1)S(1)}, u32[]{:S(2)}, u32[]{:S(2)}) async-start(bf16[32,40,1024]{2,1,0:T(8,128)(2,1)} %bitcast.122), calls=%async_computation.2 | async-start | bytes 5242880 | tf_op jit(solution)/shard_map/all_to_all | solution.py:913
  147.8 30.5 %experts_second.1 = (bf16[1280,1024]{1,0:T(8,128)(2,1)}, f32[256,1024]{1,0:T(8,128)}, bf16[2,256,1024]{2,1,0:T(8,128)(2,1)}) custom-call(bf16[1280,1024]{1,0:T(8,128)(2,1)} %bitcast.31.x_ref, bf16[1280,1024]{1,0:T(8,128)(2,1)} %bitcast.29.g_ref, bf16[1280,512]{1,0:T(8,128)(2,1)} %get-tuple-element.56.hidden_ref, ...), custom_call_target="tpu_custom_call" | custom-call | flops 5368709120 | bytes 52428800 | tf_op jit(solution)/shard_map/experts_second/pallas_call | solution.py:257
  178.3 4.2 %all-to-all-done.2 = bf16[32,40,1024]{2,1,0:T(8,128)(2,1)S(1)} async-done(((bf16[32,40,1024]{2,1,0:T(8,128)(2,1)}), bf16[32,40,1024]{2,1,0:T(8,128)(2,1)S(1)}, u32[]{:S(2)}, u32[]{:S(2)}) %all-to-all-start.2) | async-done | bytes 2621472 | tf_op jit(solution)/shard_map/all_to_all | solution.py:913
  184.1 5.1 %all-to-all-start.3 = ((bf16[32,40,1024]{2,1,0:T(8,128)(2,1)}), bf16[32,40,1024]{2,1,0:T(8,128)(2,1)}, u32[]{:S(2)}, u32[]{:S(2)}) async-start(bf16[32,40,1024]{2,1,0:T(8,128)(2,1)} %bitcast.121), calls=%async_computation.3 | async-start | bytes 5242880 | tf_op jit(solution)/shard_map/all_to_all | solution.py:913
  192.2 12.2 %block_backward.1 = (f32[128,1024]{1,0:T(8,128)}, bf16[128,1024]{1,0:T(8,128)(2,1)}, bf16[128,1024]{1,0:T(8,128)(2,1)}, bf16[256,1024]{1,0:T(8,128)(2,1)}, f32[128,1024]{1,0:T(8,128)}, /*index=5*/bf16[8,1024]{1,0:T(8,128)(2,1)}) custom-call(bf16[1280,128]{1,0:T(8,128)(2,1)} %get-tuple-element.110.placed_ref, bf16[1280,1024]{1,0:T(8,128)(2,1)} %bitcast.114, ...), custom_call_target="tpu_custom_call" | custom-call | flops 3000000000 | bytes 12000000 | tf_op jit(solution)/shard_map/block_backward/pallas_call | solution.py:859
  205.5 7.0 %collective-permute-start.2 = (bf16[128,1024]{1,0:T(8,128)(2,1)S(1)}, bf16[128,1024]{1,0:T(8,128)(2,1)S(1)}, u32[]{:S(2)}, u32[]{:S(2)}) collective-permute-start(bf16[128,1024]{1,0:T(8,128)(2,1)S(1)} %slice.120), channel_id=1, source_target_pairs={{0,64},{64,0},{1,65},{65,1},{2,66},{66,2},{3,67},{67,3},{4,68},{68... | collective-permute-start | bytes 786440 | tf_op jit(solution)/shard_map/ppermute | solution.py:1045
  212.8 7.4 %projection_grads.1 = (f32[512,3200]{1,0:T(8,128)}, bf16[512,3200]{1,0:T(8,128)(2,1)}) custom-call(bf16[384,512]{1,0:T(8,128)(2,1)} %get-tuple-element.74.mine_ref, bf16[384,512]{1,0:T(8,128)(2,1)} %get-tuple-element.75.sent_ref, bf16[128,1024]{1,0:T(8,128)(2,1)} %get-tuple-element.76.gq_ref, bf16[256,1024]{1,0:T(8,128)(2,1)} %get-tuple-element.73.gkv_ref, ...), custom_call_target="tpu_custom_call" | custom-call | tf_op jit(solution)/shard_map/projection_grads/pallas_call | solution.py:451
  220.2 43.1 %reduce_grads.1 = (f32[16,2048]{1,0:T(8,128)}, f32[16,1024]{1,0:T(8,128)}, f32[16,128]{1,0:T(8,128)}, f32[256,1024]{1,0:T(8,128)}, f32[256,1024]{1,0:T(8,128)}) custom-call(f32[4,4,2,16,3200]{4,3,2,1,0:T(8,128)} %bitcast.115, bf16[4,4,2,16,3200]{4,3,2,1,0:T(8,128)(2,1)} %bitcast.120, bf16[2,256,1024]{2,1,0:T(8,128)(2,1)} %get-tuple-element.82.low), custom_call_target="tpu_custom_call" | custom-call | flops 13107200 | bytes 98304000 | tf_op jit(solution)/shard_map/reduce_grads/pallas_call | solution.py:691
  264.9 2.5 fusion.38
  268.3 3.0 %fusion.23 = f32[384,1024]{1,0:T(8,128)S(1)} fusion(bf16[1280,1024]{1,0:T(8,128)(2,1)} %bitcast.41, bf16[1280,128]{1,0:T(8,128)(2,1)S(1)} %get-tuple-element.108, bf16[1280,128]{1,0:T(8,128)(2,1)S(1)} %get-tuple-element.109, bf16[1280,128]{1,0:T(8,128)(2,1)S(1)} %get-tuple-element.107), kind=kOutput, calls=%fused_computation.28 | convolution fusion | flops 1009582080 | bytes 5177344 | tf_op jit(solution)/shard_map/dot_general | solution.py:33
  (129 shorter events, 35.7 us)
Async XLA Ops:
  0.6 56.3 %collective-permute-start = (bf16[128,1024]{1,0:T(8,128)(2,1)}, bf16[128,1024]{1,0:T(8,128)(2,1)S(1)}, u32[]{:S(2)}, u32[]{:S(2)}) collective-permute-start(bf16[128,1024]{1,0:T(8,128)(2,1)} %bitcast.116), channel_id=1, source_target_pairs={{0,64},{64,0},{1,65},{65,1},{2,66},{66,2},{3,67},{67,3},{4,68},{68... | collective-permute-start | bytes 786440 | tf_op jit(solution)/shard_map/ppermute | solution.py:946
  5.6 34.1 %copy-start.9 = (bf16[1,128,1024]{2,1,0:T(8,128)(2,1)S(1)}, bf16[1,128,1024]{2,1,0:T(8,128)(2,1)}, u32[]{:S(2)}) copy-start(bf16[1,128,1024]{2,1,0:T(8,128)(2,1)} %param.23) | copy-start | bytes 786436
  42.0 6.6 %copy-start.3 = (bf16[1,128,1024]{2,1,0:T(8,128)(2,1)S(1)}, bf16[1,128,1024]{2,1,0:T(8,128)(2,1)}, u32[]{:S(2)}) copy-start(bf16[1,128,1024]{2,1,0:T(8,128)(2,1)} %param.12) | copy-start | bytes 786436
  42.0 47.0 %all-to-all-start = ((bf16[32,40,1024]{2,1,0:T(8,128)(2,1)}), bf16[32,40,1024]{2,1,0:T(8,128)(2,1)}, u32[]{:S(2)}, u32[]{:S(2)}) async-start(bf16[32,40,1024]{2,1,0:T(8,128)(2,1)} %bitcast.28), calls=%async_computation | async-start | bytes 5242880 | tf_op jit(solution)/shard_map/all_to_all | solution.py:913
  50.8 3.0 %copy-start.15 = (bf16[128,1024]{1,0:T(8,128)(2,1)}, bf16[128,1024]{1,0:T(8,128)(2,1)S(1)}, u32[]{:S(2)}) copy-start(bf16[128,1024]{1,0:T(8,128)(2,1)S(1)} %get-tuple-element.104) | copy-start | bytes 786436
  58.0 2.2 copy-start.16
  61.9 37.2 %copy-start.4 = (bf16[8,64,2,128]{3,1,2,0:T(8,128)(2,1)}, bf16[8,64,2,128]{3,1,2,0:T(8,128)(2,1)S(1)}, u32[]{:S(2)}) copy-start(bf16[8,64,2,128]{3,1,2,0:T(8,128)(2,1)S(1)} %convolution_convert_fusion.1) | copy-start | bytes 786436
  64.1 25.0 %copy-start.1 = (f32[128,1024]{1,0:T(8,128)}, f32[128,1024]{1,0:T(8,128)S(1)}, u32[]{:S(2)}) copy-start(f32[128,1024]{1,0:T(8,128)S(1)} %get-tuple-element.131.residual_ref) | copy-start | bytes 1572868
  89.0 5.0 %copy-start.6 = (bf16[256,1024]{1,0:T(8,128)(2,1)S(1)}, bf16[256,1024]{1,0:T(8,128)(2,1)}, u32[]{:S(2)}) copy-start(bf16[256,1024]{1,0:T(8,128)(2,1)} %param.19) | copy-start | bytes 1572868
  89.0 5.0 %copy-start.7 = (bf16[256,1024]{1,0:T(8,128)(2,1)S(1)}, bf16[256,1024]{1,0:T(8,128)(2,1)}, u32[]{:S(2)}) copy-start(bf16[256,1024]{1,0:T(8,128)(2,1)} %param.18) | copy-start | bytes 1572868
  89.0 5.0 %copy-start.8 = (bf16[256,1024]{1,0:T(8,128)(2,1)S(1)}, bf16[256,1024]{1,0:T(8,128)(2,1)}, u32[]{:S(2)}) copy-start(bf16[256,1024]{1,0:T(8,128)(2,1)} %param.17) | copy-start | bytes 1572868
  89.1 42.8 %all-to-all-start.1 = ((bf16[32,40,1024]{2,1,0:T(8,128)(2,1)}), bf16[32,40,1024]{2,1,0:T(8,128)(2,1)}, u32[]{:S(2)}, u32[]{:S(2)}) async-start(bf16[32,40,1024]{2,1,0:T(8,128)(2,1)} %bitcast.30), calls=%async_computation.1 | async-start | bytes 5242880 | tf_op jit(solution)/shard_map/all_to_all | solution.py:913
  95.3 9.2 %collective-permute-start.1 = (bf16[768,1024]{1,0:T(8,128)(2,1)}, bf16[768,1024]{1,0:T(8,128)(2,1)}, u32[]{:S(2)}, u32[]{:S(2)}) collective-permute-start(bf16[768,1024]{1,0:T(8,128)(2,1)} %pad_maximum_fusion.1), channel_id=1, source_target_pairs={{0,1},{1,0},{2,3},{3,2},{4,5},{5,4},{6,7},{7,6},{8,9},{9,8},{10,11... | collective-permute-start | bytes 4718600 | tf_op jit(solution)/shard_map/ppermute | solution.py:952
  143.8 38.7 %all-to-all-start.2 = ((bf16[32,40,1024]{2,1,0:T(8,128)(2,1)}), bf16[32,40,1024]{2,1,0:T(8,128)(2,1)S(1)}, u32[]{:S(2)}, u32[]{:S(2)}) async-start(bf16[32,40,1024]{2,1,0:T(8,128)(2,1)} %bitcast.122), calls=%async_computation.2 | async-start | bytes 5242880 | tf_op jit(solution)/shard_map/all_to_all | solution.py:913
  182.5 1.6 copy-start
  182.5 8.9 %copy-start.5 = (bf16[8,64,2,128]{3,1,2,0:T(8,128)(2,1)S(1)}, bf16[8,64,2,128]{3,1,2,0:T(8,128)(2,1)}, u32[]{:S(2)}) copy-start(bf16[8,64,2,128]{3,1,2,0:T(8,128)(2,1)} %copy-done.4) | copy-start | bytes 786436
  184.1 84.3 %all-to-all-start.3 = ((bf16[32,40,1024]{2,1,0:T(8,128)(2,1)}), bf16[32,40,1024]{2,1,0:T(8,128)(2,1)}, u32[]{:S(2)}, u32[]{:S(2)}) async-start(bf16[32,40,1024]{2,1,0:T(8,128)(2,1)} %bitcast.121), calls=%async_computation.3 | async-start | bytes 5242880 | tf_op jit(solution)/shard_map/all_to_all | solution.py:913
  205.5 58.7 %collective-permute-start.2 = (bf16[128,1024]{1,0:T(8,128)(2,1)S(1)}, bf16[128,1024]{1,0:T(8,128)(2,1)S(1)}, u32[]{:S(2)}, u32[]{:S(2)}) collective-permute-start(bf16[128,1024]{1,0:T(8,128)(2,1)S(1)} %slice.120), channel_id=1, source_target_pairs={{0,64},{64,0},{1,65},{65,1},{2,66},{66,2},{3,67},{67,3},{4,68},{68... | collective-permute-start | bytes 786440 | tf_op jit(solution)/shard_map/ppermute | solution.py:1045
  220.2 44.7 %copy-start.13 = (f32[128,1024]{1,0:T(8,128)S(1)}, f32[128,1024]{1,0:T(8,128)}, u32[]{:S(2)}) copy-start(f32[128,1024]{1,0:T(8,128)} %get-tuple-element.72) | copy-start | bytes 1572868
  263.3 4.1 %copy-start.14 = (f32[128,1024]{1,0:T(8,128)S(1)}, f32[128,1024]{1,0:T(8,128)}, u32[]{:S(2)}) copy-start(f32[128,1024]{1,0:T(8,128)} %get-tuple-element.71) | copy-start | bytes 1572868
  268.3 3.0 %copy-start.2 = (f32[128,1024]{1,0:T(8,128)S(1)}, f32[128,1024]{1,0:T(8,128)}, u32[]{:S(2)}) copy-start(f32[128,1024]{1,0:T(8,128)} %copy-done.1) | copy-start | bytes 1572868
  271.4 2.2 copy-start.10
  271.4 3.1 %copy-start.12 = (f32[256,1024]{1,0:T(8,128)S(1)}, f32[256,1024]{1,0:T(8,128)}, u32[]{:S(2)}) copy-start(f32[256,1024]{1,0:T(8,128)} %get-tuple-element.154) | copy-start | bytes 3145732
  273.5 1.9 copy-start.11
  (3 other events, 3.3 us)

commit v9 on v8

--- a/solution.py
+++ b/solution.py
@@ -69,13 +69,6 @@
 def norm_forward(values, gain_vector):
     inverse = lax.rsqrt(jnp.mean(values * values, axis=-1, keepdims=True) + EPSILON)
     return ((values * inverse * gain_vector.astype(f32)).astype(bf16), inverse)
-
-
-def norm_backward(values, inverse, gain_vector, upstream):
-    scaled = upstream * gain_vector.astype(f32)
-    grad_gain = jnp.sum(upstream * values * inverse, axis=0)
-    coupling = jnp.mean(scaled * values, axis=-1, keepdims=True)
-    return (inverse * scaled - values * inverse * inverse * inverse * coupling, grad_gain)
 
 
 def rounded(values):
@@ -487,11 +480,18 @@
     mine_hbm,
     sent,
     low,
+    kv_ref,
+    weights_hbm,
+    from_ref,
+    residual_ref,
+    inputs_ref,
+    gain_one_ref,
     in_ref,
     out_ref,
     gain_ref,
     up_ref,
     down_ref,
+    inputs_out,
     came,
     acc,
     stage,
@@ -506,7 +506,9 @@
     in_own,
     low_came,
     mine,
-    mine_sem,
+    kv_came,
+    kv_weights,
+    fetch_sems,
     chip_send,
     chip_recv,
     ring_send,
@@ -531,8 +533,13 @@
     across = (1 - seq, chip + 1 - 2 * half, core)
     mirror = (1 - seq, chip, core)
     ahead, behind = (1, RING - 1)
-    fetch = pltpu.make_async_copy(mine_hbm, mine, mine_sem)
+    fetch = pltpu.make_async_copy(mine_hbm, mine, fetch_sems.at[0])
     fetch.start()
+    tokens, width = from_ref.shape
+    fetch_weights = pltpu.make_async_copy(
+        weights_hbm.at[:, width : 2 * width], kv_weights, fetch_sems.at[1]
+    )
+    fetch_weights.start()
     barrier = pltpu.get_barrier_semaphore()
     others = (partner, across, mirror, first(ahead), first(behind), last(ahead), last(behind))
     for other in others:
@@ -568,6 +575,8 @@
 
     order = (2, ahead, behind, 0)
     two = RING // 2
+    kv_away = send(13, kv_ref.at[pl.ds(tokens, tokens)], kv_came, mirror)
+    kv_away.start()
     units = send(12, low, low_came, mirror)
     units.start()
     for s in order:
@@ -622,6 +631,16 @@
                 stage[s, first_j + k, h] = packed(value)
 
         ring[3 if i == 0 else 5].start()
+
+    kv_away.wait_recv()
+    fetch_weights.wait()
+    values = inputs_ref[...].astype(f32)
+    inverse = lax.rsqrt(jnp.mean(values * values, axis=-1, keepdims=True) + EPSILON)
+    upstream = from_ref[...] + dot(kv_came[...], kv_weights[...], NT)
+    scaled = upstream * gain_one_ref[...]
+    coupling = jnp.mean(scaled * values, axis=-1, keepdims=True)
+    grad = inverse * scaled - values * inverse * inverse * inverse * coupling
+    inputs_out[...] = (residual_ref[...] + grad).astype(bf16)
 
     for i, source, first_j in ((2, 0, two), (4, 1, 0), (3, 0, 0), (5, 1, two)):
         ring[i].wait_recv()
@@ -673,6 +692,7 @@
     out_ref[...] = total[:, cut:wide]
     gain_ref[...] = total[:, wide:]
     units.wait_send()
+    kv_away.wait_send()
     for copy in ring:
         copy.wait_send()
     for s in order:
@@ -682,22 +702,26 @@
             on_chip(s, j, flip)[2].wait_send()
 
 
-def reduce_grads(mine, sent, low, cut):
+def reduce_grads(mine, sent, low, cut, kv, weights, for_inputs):
     width = mine.shape[1]
     share = mine.shape[0] // (2 * RING * RING)
     shape = (RING, RING, 2, share, width)
     two = RING // 2
     pair = (2, share, width)
+    vmem = pl.BlockSpec(memory_space=pltpu.VMEM)
+    away = pl.BlockSpec(memory_space=pl.ANY)
+    tokens, kv_width = (kv.shape[0] // 2, kv.shape[1])
     return pl.pallas_call(
         reduce_body,
-        in_specs=[pl.BlockSpec(memory_space=pl.ANY)] * 2 + [pl.BlockSpec(memory_space=pltpu.VMEM)],
-        out_specs=[pl.BlockSpec(memory_space=pltpu.VMEM)] * 5,
+        in_specs=[away, away, vmem, vmem, away, vmem, vmem, vmem, vmem],
+        out_specs=[vmem] * 6,
         out_shape=[
             jax.ShapeDtypeStruct((share, cut), f32),
             jax.ShapeDtypeStruct((share, width - cut - 128), f32),
             jax.ShapeDtypeStruct((share, 128), f32),
             jax.ShapeDtypeStruct(low.shape[1:], f32),
             jax.ShapeDtypeStruct(low.shape[1:], f32),
+            jax.ShapeDtypeStruct((tokens, kv_width), bf16),
         ],
         scratch_shapes=[
             pltpu.VMEM(shape, bf16),
@@ -714,18 +738,20 @@
             pltpu.VMEM((share, width), f32),
             pltpu.VMEM(low.shape, bf16),
             pltpu.VMEM(shape, f32),
-            pltpu.SemaphoreType.DMA,
+            pltpu.VMEM((tokens, kv_width), bf16),
+            pltpu.VMEM((weights.shape[0], kv_width), bf16),
+            pltpu.SemaphoreType.DMA((2,)),
             pltpu.SemaphoreType.DMA((RING, RING)),
             pltpu.SemaphoreType.DMA((RING, RING)),
-            pltpu.SemaphoreType.DMA((13,)),
-            pltpu.SemaphoreType.DMA((13,)),
+            pltpu.SemaphoreType.DMA((14,)),
+            pltpu.SemaphoreType.DMA((14,)),
         ],
         compiler_params=pltpu.CompilerParams(collective_id=2, has_side_effects=True),
         cost_estimate=pl.CostEstimate(
             flops=mine.size * 8, bytes_accessed=mine.size * 60, transcendentals=0
         ),
         name="reduce_grads",
-    )(mine.reshape(shape), sent.reshape(shape), low)
+    )(mine.reshape(shape), sent.reshape(shape), low, kv, weights, *for_inputs)
 
 
 def rotated(block, cosine, sine, first_half):
@@ -737,7 +763,6 @@
     placed_ref,
     back_ref,
     residual_ref,
-    inverse_ref,
     gain_ref,
     cotangent_ref,
     weights_hbm,
@@ -774,7 +799,7 @@
     out_part.start()
     in_part.start()
     residual = residual_ref[...]
-    inverse = inverse_ref[...]
+    inverse = lax.rsqrt(jnp.mean(residual * residual, axis=-1, keepdims=True) + EPSILON)
     upstream = dot(placed_ref[...], back_ref[...], TN)
     gain_two = jnp.sum(upstream * residual * inverse, axis=0, keepdims=True)
     scaled = upstream * gain_ref[...]
@@ -851,14 +876,14 @@
 
 
 def block_backward(
-    placed, back, residual, inverse, gain, cotangent, weights, heads, masks, tables, scaled_inputs
+    placed, back, residual, gain, cotangent, weights, heads, masks, tables, scaled_inputs
 ):
     tokens, width = residual.shape
     query, keys, values = heads
     vmem = pl.BlockSpec(memory_space=pltpu.VMEM)
     return pl.pallas_call(
         block_backward_body,
-        in_specs=[vmem] * 6 + [pl.BlockSpec(memory_space=pl.ANY)] + [vmem] * 10,
+        in_specs=[vmem] * 5 + [pl.BlockSpec(memory_space=pl.ANY)] + [vmem] * 10,
         out_specs=[vmem] * 6,
         out_shape=[
             jax.ShapeDtypeStruct((tokens, width), f32),
@@ -877,7 +902,6 @@
         placed,
         back,
         residual,
-        inverse,
         gain,
         cotangent,
         weights,
@@ -994,7 +1018,7 @@
     attended, log_total = attend_forward(query, keys, values, allowed)
     mixed = attended.reshape(token_count, query_width)
     residual = row_values + dot(mixed, out_full)
-    normed_two, inverse_two = norm_forward(residual, gain_two)
+    normed_two, _ = norm_forward(residual, gain_two)
 
     rows = dot(placed, normed_two).astype(bf16)
     rows, grad_arrived = lax.optimization_barrier((rows, grad_arrived))
@@ -1019,9 +1043,10 @@
         (allowed.astype(jnp.int32), mixed, log_rows),
         (cosine, sine),
         (row_values * inverse_one, other_low.astype(f32) * inverse_other),
+        jnp.concatenate(mixers, axis=1),
     )
     arrived, ready = lax.optimization_barrier((arrived, ready))
-    features_mine, features_sent, chosen_half, flat_heads, masks, tables, scaled_inputs = ready
+    features_mine, features_sent, chosen_half, flat_heads, masks, tables, scaled_inputs, mix = ready
 
     hidden, grads, back = experts_first(arrived, grad_arrived, pre_w, down_w)
     grad_back = exchange(back)
@@ -1033,7 +1058,6 @@
         placed,
         grad_back,
         residual,
-        inverse_two,
         gain_two.astype(f32)[None, :],
         cotangent[0],
         gathered,
@@ -1042,23 +1066,22 @@
         tables,
         scaled_inputs,
     )
-    came = lax.ppermute(grad_kv[token_count:], "seq", SWAP)
 
     grads_mine, grads_sent = projection_grads(
         features_mine, features_sent, grad_query, grad_kv, grad_res_low, gain_parts, chosen_half
     )
     in_width = query_width + 2 * kv_width
-    in_total, out_total, gain_total, up_total, down_total = reduce_grads(
-        grads_mine, grads_sent, rest_low, in_width
+    in_total, out_total, gain_total, up_total, down_total, grad_inputs = reduce_grads(
+        grads_mine,
+        grads_sent,
+        rest_low,
+        in_width,
+        grad_kv,
+        gathered,
+        (from_own, grad_residual, own_low, gain_one.astype(f32)[None, :]),
     )
     gain_total = gain_total[:, :2] + gain_total[:, 2:4] + gain_total[:, 4:6]
 
-    came, gain_total = lax.optimization_barrier((came, gain_total))
-    grad_normed_one = from_own + dot(came, kv_w, NT)
-    grad_norm_one, _ = norm_backward(row_values, inverse_one, gain_one, grad_normed_one)
-    grad_inputs = (grad_residual + grad_norm_one).astype(bf16)
-
-    mix = jnp.concatenate(mixers, axis=1)
     chosen = dot(mix, returned, TN).reshape(3, token_count, model_width)
     output = (residual + (chosen[2] + chosen[1] + chosen[0])).astype(bf16)
     return (

time: 278 us -> 275 us (0.989)
  Pallas kernels: 139 us -> 147 us
  starting transfers between devices: 29.3 us -> 22.5 us
  waiting for transfers between devices: 49 us -> 44.2 us
  other arithmetic: 19.6 us -> 23.2 us
    pallas_call x2, Pallas kernels: 55.3 us -> 62.9 us  [the longest x1 50.6 us: reduce_grads(): pl.pallas_call(reduce_body, in_specs=[away, away, vmem, vmem, away, vmem,...]
    ppermute x1 -> x0, starting transfers between devices: 7.03 us -> none  [on_device(): came = lax.ppermute(grad_kv[token_count:], 'seq', SWAP)]
    all_to_all x4, waiting for transfers between devices: 49 us -> 44.2 us  [exchange(): lax.all_to_all(blocks, ('seq', 'chip'), split_axis=0, concat_axis=0, axis...]
    dot_general x9 -> x8, matrix products: 19.8 us -> 17.2 us  [dot(): return lax.dot_general(a, b, dims, preferred_element_type=f32)]
    unnamed x45 -> x68, local copies, waits for them, and re-layouts: 5.85 us -> 6.65 us
  transfers between devices with their start and end apart: 7 -> 6, of which waited for: 3 -> 3; matrix products, arithmetic and copies ran while one was open for 17% -> 18% of each run, Pallas kernels for 46% -> 49%
where the time goes in v9:
time: 275 us; the launch traced here: 274 us
  Pallas kernels  147 us (53%)
  waiting for transfers between devices  44.2 us (16%)
  other arithmetic  23.2 us (8%)
  starting transfers between devices  22.5 us (8%)
  matrix products  18.2 us (7%)
  local copies, waits for them, and re-layouts  17.7 us (6%)
    pallas_call x1, Pallas kernels, reduce_grads(): pl.pallas_call(reduce_body, in_specs=[away, away, vmem, vmem, away, vmem,...  50.6 us
    all_to_all x4, waiting for transfers between devices, exchange(): lax.all_to_all(blocks, ('seq', 'chip'), split_axis=0, concat_axis=0, axis...  44.2 us
    pallas_call x1, Pallas kernels, gather_weights(): pl.pallas_call(gather_body, out_shape=jax.ShapeDtypeStruct((RING, RING, 2...  34 us
    pallas_call x1, Pallas kernels, experts_second(): pl.pallas_call(experts_second_body, in_specs=[pl.BlockSpec(memory_space=p...  30.7 us
    all_to_all x4, starting transfers between devices, exchange(): lax.all_to_all(blocks, ('seq', 'chip'), split_axis=0, concat_axis=0, axis...  20.9 us
    dot_general x8, matrix products, dot(): return lax.dot_general(a, b, dims, preferred_element_type=f32)  17.2 us
    pallas_call x1, Pallas kernels, block_backward(): pl.pallas_call(block_backward_body, in_specs=[vmem] * 5 + [pl.BlockSpec(m...  12.3 us
    pallas_call x1, Pallas kernels, experts_first(): pl.pallas_call(experts_first_body, grid=(rows // ROW_BLOCK,), in_specs=[p...  11.9 us
  transfers between devices with their start and end apart: 6, of which 3 were waited for; matrix products, arithmetic and copies ran while one was open for 18% of the time, Pallas kernels for 49%

profile of v9, /device:TPU:0, one launch (start us, length us, event | category | flops | bytes accessed | tf_op | source)
XLA Modules:
  0.0 274.1 jit_solution(13508304259026202096)
XLA Ops:
  0.6 1.7 collective-permute-start
  5.7 3.2 %multiply_convert_fusion = bf16[1280,1024]{1,0:T(8,128)(2,1)} fusion(pred[1280,128]{1,0:T(8,128)(4,1)S(1)} %bitcast.128, f32[1280]{0:T(1024)S(1)} %mul.270, bf16[1,128,1024]{2,1,0:T(8,128)(2,1)} %param.23), kind=kOutput, calls=%fused_computation | convolution fusion | flops 338165760 | bytes 3052544 | tf_op jit(solution)/shard_map/dot_general | solution.py:33
  8.9 34.0 %gather_weights.1 = bf16[4,4,2,2,16,3200]{5,4,3,2,1,0:T(8,128)(2,1)} custom-call(bf16[16,2048]{1,0:T(8,128)(2,1)} %in_ref.1, bf16[16,1024]{1,0:T(8,128)(2,1)} %project_ref.1, bf16[16,128]{1,0:T(8,128)(2,1)} %fusion.43.gains_ref), custom_call_target="tpu_custom_call" | custom-call | bytes 52428800 | tf_op jit(solution)/shard_map/gather_weights/pallas_call | solution.py:386
  42.9 6.6 %all-to-all-start = ((bf16[32,40,1024]{2,1,0:T(8,128)(2,1)}), bf16[32,40,1024]{2,1,0:T(8,128)(2,1)}, u32[]{:S(2)}, u32[]{:S(2)}) async-start(bf16[32,40,1024]{2,1,0:T(8,128)(2,1)} %bitcast.27), calls=%async_computation | async-start | bytes 5242880 | tf_op jit(solution)/shard_map/all_to_all | solution.py:937
  51.8 3.0 %fusion.2 = f32[128,2048]{1,0:T(8,128)S(1)} fusion(bf16[128,1024]{1,0:T(8,128)(2,1)S(1)} %get-tuple-element.104, bf16[1024,3200]{1,0:T(8,128)(2,1)} %bitcast.105), kind=kOutput, calls=%fused_computation.4 | convolution fusion | flops 536870912 | bytes 5505024 | tf_op jit(solution)/shard_map/dot_general | solution.py:33
  59.6 2.1 fusion.7
  63.4 2.2 multiply_reduce_fusion
  65.7 2.5 convolution_convert_fusion
  68.2 21.8 %all-to-all-done = bf16[32,40,1024]{2,1,0:T(8,128)(2,1)} async-done(((bf16[32,40,1024]{2,1,0:T(8,128)(2,1)}), bf16[32,40,1024]{2,1,0:T(8,128)(2,1)}, u32[]{:S(2)}, u32[]{:S(2)}) %all-to-all-start) | async-done | bytes 2621472 | tf_op jit(solution)/shard_map/all_to_all | solution.py:937
  90.0 5.0 %all-to-all-start.1 = ((bf16[32,40,1024]{2,1,0:T(8,128)(2,1)}), bf16[32,40,1024]{2,1,0:T(8,128)(2,1)}, u32[]{:S(2)}, u32[]{:S(2)}) async-start(bf16[32,40,1024]{2,1,0:T(8,128)(2,1)} %bitcast.29), calls=%async_computation.1 | async-start | bytes 5242880 | tf_op jit(solution)/shard_map/all_to_all | solution.py:937
  99.7 1.9 negate_select_fusion
  102.7 2.2 fusion.chosen_mine_ref.chosen_sent_ref
  112.8 1.6 pad_maximum_fusion.pre_w_ref
  114.4 18.4 %all-to-all-done.1 = bf16[32,40,1024]{2,1,0:T(8,128)(2,1)} async-done(((bf16[32,40,1024]{2,1,0:T(8,128)(2,1)}), bf16[32,40,1024]{2,1,0:T(8,128)(2,1)}, u32[]{:S(2)}, u32[]{:S(2)}) %all-to-all-start.1) | async-done | bytes 2621472 | tf_op jit(solution)/shard_map/all_to_all | solution.py:937
  132.8 11.9 %experts_first.1 = (bf16[1280,512]{1,0:T(8,128)(2,1)}, bf16[1280,1024]{1,0:T(8,128)(2,1)}, bf16[1280,1024]{1,0:T(8,128)(2,1)}) custom-call(bf16[1280,1024]{1,0:T(8,128)(2,1)} %bitcast.30.x_ref, bf16[1280,1024]{1,0:T(8,128)(2,1)} %bitcast.28.g_ref, bf16[1024,1024]{1,0:T(8,128)(2,1)} %pad_maximum_fusion.pre_w_ref, bf16[512,1024]{1,0:T(8,128)(2,1)} %pad_maximum_fusion.2.down_w_ref), custom_call_target="tpu_custom_call" | custom-call | flops 6710886400 | bytes 13107200 | tf_op jit(solution)/shard_map/experts_first/pallas_call | solution.py:123
  144.7 4.1 %all-to-all-start.2 = ((bf16[32,40,1024]{2,1,0:T(8,128)(2,1)}), bf16[32,40,1024]{2,1,0:T(8,128)(2,1)S(1)}, u32[]{:S(2)}, u32[]{:S(2)}) async-start(bf16[32,40,1024]{2,1,0:T(8,128)(2,1)} %bitcast.119), calls=%async_computation.2 | async-start | bytes 5242880 | tf_op jit(solution)/shard_map/all_to_all | solution.py:937
  148.7 30.7 %experts_second.1 = (bf16[1280,1024]{1,0:T(8,128)(2,1)}, f32[256,1024]{1,0:T(8,128)}, bf16[2,256,1024]{2,1,0:T(8,128)(2,1)}) custom-call(bf16[1280,1024]{1,0:T(8,128)(2,1)} %bitcast.30.x_ref, bf16[1280,1024]{1,0:T(8,128)(2,1)} %bitcast.28.g_ref, bf16[1280,512]{1,0:T(8,128)(2,1)} %get-tuple-element.57.hidden_ref, ...), custom_call_target="tpu_custom_call" | custom-call | flops 5368709120 | bytes 52428800 | tf_op jit(solution)/shard_map/experts_second/pallas_call | solution.py:250
  179.4 4.0 %all-to-all-done.2 = bf16[32,40,1024]{2,1,0:T(8,128)(2,1)S(1)} async-done(((bf16[32,40,1024]{2,1,0:T(8,128)(2,1)}), bf16[32,40,1024]{2,1,0:T(8,128)(2,1)S(1)}, u32[]{:S(2)}, u32[]{:S(2)}) %all-to-all-start.2) | async-done | bytes 2621472 | tf_op jit(solution)/shard_map/all_to_all | solution.py:937
  183.4 1.5 copy-done
  185.0 5.2 %all-to-all-start.3 = ((bf16[32,40,1024]{2,1,0:T(8,128)(2,1)}), bf16[32,40,1024]{2,1,0:T(8,128)(2,1)}, u32[]{:S(2)}, u32[]{:S(2)}) async-start(bf16[32,40,1024]{2,1,0:T(8,128)(2,1)} %bitcast.118), calls=%async_computation.3 | async-start | bytes 5242880 | tf_op jit(solution)/shard_map/all_to_all | solution.py:937
  193.3 12.3 %block_backward.1 = (f32[128,1024]{1,0:T(8,128)}, bf16[128,1024]{1,0:T(8,128)(2,1)}, bf16[128,1024]{1,0:T(8,128)(2,1)}, bf16[256,1024]{1,0:T(8,128)(2,1)}, f32[128,1024]{1,0:T(8,128)}, /*index=5*/bf16[8,1024]{1,0:T(8,128)(2,1)}) custom-call(bf16[1280,128]{1,0:T(8,128)(2,1)} %get-tuple-element.110.placed_ref, bf16[1280,1024]{1,0:T(8,128)(2,1)} %bitcast.110, ...), custom_call_target="tpu_custom_call" | custom-call | flops 3000000000 | bytes 12000000 | tf_op jit(solution)/shard_map/block_backward/pallas_call | solution.py:884
  205.6 7.4 %projection_grads.1 = (f32[512,3200]{1,0:T(8,128)}, bf16[512,3200]{1,0:T(8,128)(2,1)}) custom-call(bf16[384,512]{1,0:T(8,128)(2,1)} %get-tuple-element.61.mine_ref, bf16[384,512]{1,0:T(8,128)(2,1)} %get-tuple-element.62.sent_ref, bf16[128,1024]{1,0:T(8,128)(2,1)} %get-tuple-element.74.gq_ref, bf16[256,1024]{1,0:T(8,128)(2,1)} %get-tuple-element.75.gkv_ref.kv_ref, ...), custom_call_target="tpu_custom_call" | custom-call | tf_op jit(solution)/shard_map/projection_grads/pallas_call | solution.py:444
  213.0 50.6 %reduce_grads.1 = (f32[16,2048]{1,0:T(8,128)}, f32[16,1024]{1,0:T(8,128)}, f32[16,128]{1,0:T(8,128)}, f32[256,1024]{1,0:T(8,128)}, f32[256,1024]{1,0:T(8,128)}, /*index=5*/bf16[128,1024]{1,0:T(8,128)(2,1)}) custom-call(f32[4,4,2,16,3200]{4,3,2,1,0:T(8,128)} %bitcast.111, bf16[4,4,2,16,3200]{4,3,2,1,0:T(8,128)(2,1)} %bitcast.117, ...), custom_call_target="tpu_custom_call" | custom-call | flops 13107200 | bytes 98304000 | tf_op jit(solution)/shard_map/reduce_grads/pallas_call | solution.py:714
  265.2 3.0 %fusion.68 = f32[384,1024]{1,0:T(8,128)S(1)} fusion(bf16[1280,384]{1,0:T(8,128)(2,1)S(1)} %copy-done.14, bf16[1280,1024]{1,0:T(8,128)(2,1)} %bitcast.41), kind=kOutput, calls=%fused_computation.154 | convolution fusion | flops 1006632960 | bytes 5177344 | tf_op jit(solution)/shard_map/dot_general | solution.py:33
  (147 shorter events, 35.9 us)
Async XLA Ops:
  0.6 57.8 %collective-permute-start = (bf16[128,1024]{1,0:T(8,128)(2,1)}, bf16[128,1024]{1,0:T(8,128)(2,1)S(1)}, u32[]{:S(2)}, u32[]{:S(2)}) collective-permute-start(bf16[128,1024]{1,0:T(8,128)(2,1)} %bitcast.112), channel_id=1, source_target_pairs={{0,64},{64,0},{1,65},{65,1},{2,66},{66,2},{3,67},{67,3},{4,68},{68... | collective-permute-start | bytes 786440 | tf_op jit(solution)/shard_map/ppermute | solution.py:970
  3.9 39.0 %copy-start.21 = (f32[128,32]{0,1:T(8,128)}, f32[128,32]{0,1:T(8,128)S(1)}, u32[]{:S(2)}) copy-start(f32[128,32]{0,1:T(8,128)S(1)} %select_reduce_fusion.1) | copy-start | bytes 49156
  42.9 6.6 %copy-start.3 = (bf16[1,128,1024]{2,1,0:T(8,128)(2,1)S(1)}, bf16[1,128,1024]{2,1,0:T(8,128)(2,1)}, u32[]{:S(2)}) copy-start(bf16[1,128,1024]{2,1,0:T(8,128)(2,1)} %param.12) | copy-start | bytes 786436
  42.9 47.0 %all-to-all-start = ((bf16[32,40,1024]{2,1,0:T(8,128)(2,1)}), bf16[32,40,1024]{2,1,0:T(8,128)(2,1)}, u32[]{:S(2)}, u32[]{:S(2)}) async-start(bf16[32,40,1024]{2,1,0:T(8,128)(2,1)} %bitcast.27), calls=%async_computation | async-start | bytes 5242880 | tf_op jit(solution)/shard_map/all_to_all | solution.py:937
  50.9 3.9 %copy-start.27 = (f32[1024]{0:T(1024)}, f32[1024]{0:T(1024)S(1)}, u32[]{:S(2)}) copy-start(f32[1024]{0:T(1024)S(1)} %reshape.533) | copy-start | bytes 12292
  55.1 3.5 %copy-start.28 = (f32[1024]{0:T(1024)S(1)}, f32[1024]{0:T(1024)}, u32[]{:S(2)}) copy-start(f32[1024]{0:T(1024)} %copy-done.27) | copy-start | bytes 12292
  63.4 41.5 %copy-start.4 = (bf16[8,64,2,128]{3,1,2,0:T(8,128)(2,1)}, bf16[8,64,2,128]{3,1,2,0:T(8,128)(2,1)S(1)}, u32[]{:S(2)}) copy-start(bf16[8,64,2,128]{3,1,2,0:T(8,128)(2,1)S(1)} %convolution_convert_fusion.1) | copy-start | bytes 786436
  65.7 24.3 %copy-start.1 = (f32[128,1024]{1,0:T(8,128)}, f32[128,1024]{1,0:T(8,128)S(1)}, u32[]{:S(2)}) copy-start(f32[128,1024]{1,0:T(8,128)S(1)} %get-tuple-element.129.residual_ref) | copy-start | bytes 1572868
  90.0 5.0 %copy-start.6 = (bf16[256,1024]{1,0:T(8,128)(2,1)S(1)}, bf16[256,1024]{1,0:T(8,128)(2,1)}, u32[]{:S(2)}) copy-start(bf16[256,1024]{1,0:T(8,128)(2,1)} %param.19) | copy-start | bytes 1572868
  90.0 5.0 %copy-start.7 = (bf16[256,1024]{1,0:T(8,128)(2,1)S(1)}, bf16[256,1024]{1,0:T(8,128)(2,1)}, u32[]{:S(2)}) copy-start(bf16[256,1024]{1,0:T(8,128)(2,1)} %param.18) | copy-start | bytes 1572868
  90.0 5.0 %copy-start.8 = (bf16[256,1024]{1,0:T(8,128)(2,1)S(1)}, bf16[256,1024]{1,0:T(8,128)(2,1)}, u32[]{:S(2)}) copy-start(bf16[256,1024]{1,0:T(8,128)(2,1)} %param.17) | copy-start | bytes 1572868
  90.0 42.8 %all-to-all-start.1 = ((bf16[32,40,1024]{2,1,0:T(8,128)(2,1)}), bf16[32,40,1024]{2,1,0:T(8,128)(2,1)}, u32[]{:S(2)}, u32[]{:S(2)}) async-start(bf16[32,40,1024]{2,1,0:T(8,128)(2,1)} %bitcast.29), calls=%async_computation.1 | async-start | bytes 5242880 | tf_op jit(solution)/shard_map/all_to_all | solution.py:937
  96.3 13.2 %collective-permute-start.1 = (bf16[768,1024]{1,0:T(8,128)(2,1)}, bf16[768,1024]{1,0:T(8,128)(2,1)}, u32[]{:S(2)}, u32[]{:S(2)}) collective-permute-start(bf16[768,1024]{1,0:T(8,128)(2,1)} %pad_maximum_fusion.1), channel_id=1, source_target_pairs={{0,1},{1,0},{2,3},{3,2},{4,5},{5,4},{6,7},{7,6},{8,9},{9,8},{10,11... | collective-permute-start | bytes 4718600 | tf_op jit(solution)/shard_map/ppermute | solution.py:976
  98.9 3.8 %copy-start.29 = (s32[1024]{0:T(1024)S(1)}, s32[1024]{0:T(1024)}, u32[]{:S(2)}) copy-start(s32[1024]{0:T(1024)} %fusion.42) | copy-start | bytes 12292
  101.6 3.5 %copy-start.10 = (bf16[128,8,64]{0,2,1:T(8,128)(2,1)S(1)}, bf16[128,8,64]{0,2,1:T(8,128)(2,1)}, u32[]{:S(2)}) copy-start(bf16[128,8,64]{0,2,1:T(8,128)(2,1)} %copy-done.9) | copy-start | bytes 393220
  101.6 3.6 %copy-start.25 = (f32[2,8,128]{2,1,0:T(8,128)S(1)}, f32[2,8,128]{2,1,0:T(8,128)}, u32[]{:S(2)}) copy-start(f32[2,8,128]{2,1,0:T(8,128)} %copy-done.24) | copy-start | bytes 24580
  102.7 4.0 %copy-start.15 = (bf16[128,512]{1,0:T(8,128)(2,1)S(1)}, bf16[128,512]{1,0:T(8,128)(2,1)}, u32[]{:S(2)}) copy-start(bf16[128,512]{1,0:T(8,128)(2,1)} %copy.67) | copy-start | bytes 393220
  102.7 4.7 %copy-start.18 = (bf16[128,1024]{1,0:T(8,128)(2,1)S(1)}, bf16[128,1024]{1,0:T(8,128)(2,1)}, u32[]{:S(2)}) copy-start(bf16[128,1024]{1,0:T(8,128)(2,1)} %copy-done.17) | copy-start | bytes 786436
  102.7 4.7 %copy-start.20 = (bf16[128,1024]{1,0:T(8,128)(2,1)S(1)}, bf16[128,1024]{1,0:T(8,128)(2,1)}, u32[]{:S(2)}) copy-start(bf16[128,1024]{1,0:T(8,128)(2,1)} %copy-done.19) | copy-start | bytes 786436
  144.7 38.7 %all-to-all-start.2 = ((bf16[32,40,1024]{2,1,0:T(8,128)(2,1)}), bf16[32,40,1024]{2,1,0:T(8,128)(2,1)S(1)}, u32[]{:S(2)}, u32[]{:S(2)}) async-start(bf16[32,40,1024]{2,1,0:T(8,128)(2,1)} %bitcast.119), calls=%async_computation.2 | async-start | bytes 5242880 | tf_op jit(solution)/shard_map/all_to_all | solution.py:937
  183.4 9.0 %copy-start.5 = (bf16[8,64,2,128]{3,1,2,0:T(8,128)(2,1)S(1)}, bf16[8,64,2,128]{3,1,2,0:T(8,128)(2,1)}, u32[]{:S(2)}) copy-start(bf16[8,64,2,128]{3,1,2,0:T(8,128)(2,1)} %copy-done.4) | copy-start | bytes 786436
  185.0 80.2 %all-to-all-start.3 = ((bf16[32,40,1024]{2,1,0:T(8,128)(2,1)}), bf16[32,40,1024]{2,1,0:T(8,128)(2,1)}, u32[]{:S(2)}, u32[]{:S(2)}) async-start(bf16[32,40,1024]{2,1,0:T(8,128)(2,1)} %bitcast.118), calls=%async_computation.3 | async-start | bytes 5242880 | tf_op jit(solution)/shard_map/all_to_all | solution.py:937
  213.0 52.2 %copy-start.14 = (bf16[1280,384]{1,0:T(8,128)(2,1)S(1)}, bf16[1280,384]{1,0:T(8,128)(2,1)}, u32[]{:S(2)}) copy-start(bf16[1280,384]{1,0:T(8,128)(2,1)} %pad_maximum_fusion.3) | copy-start | bytes 2949124
  269.1 3.0 %copy-start.13 = (f32[256,1024]{1,0:T(8,128)S(1)}, f32[256,1024]{1,0:T(8,128)}, u32[]{:S(2)}) copy-start(f32[256,1024]{1,0:T(8,128)} %get-tuple-element.150) | copy-start | bytes 3145732
  (13 other events, 24.9 us)

commit v10 on v9

--- a/solution.py
+++ b/solution.py
@@ -155,11 +155,13 @@
     grads_ref,
     down_w_ref,
     out_ref,
-    total_ref,
+    gate_ref,
+    gate_came_ref,
     rest_ref,
     theirs,
     came,
     last,
+    gate,
     low,
     low_came,
     send_sem,
@@ -199,7 +201,7 @@
 
     away = [send(k, theirs.at[k], came.at[k], partner) for k in range(3)]
     across = [send(3 + k, low.at[k], low_came.at[k], mirror) for k in range(1)]
-    mine = [total_ref, last.at[0], last.at[1]]
+    mine = [gate, last.at[0], last.at[1]]
     lows = [low.at[0], rest_ref.at[0], rest_ref.at[1]]
     for k in range(3):
         unit_grads(1, k, theirs.at[k])
@@ -233,14 +235,9 @@
             out = part if out is None else out + part
         out_ref[rows, :] = out.astype(bf16)
 
-    for k in range(len(across)):
-        across[k].wait_recv()
-
-        @pl.loop(0, BLOCK // 32)
-        def _(r):
-            rows = pl.ds(pl.multiple_of(r * 32, 32), 32)
-            mine[k][rows, :] = low[k, rows, :].astype(f32) + low_came[k, rows, :].astype(f32)
-
+    across[0].wait_recv()
+    gate_ref[...] = low[0]
+    gate_came_ref[...] = low_came[0]
     for copy in away + across:
         copy.wait_send()
 
@@ -250,16 +247,18 @@
     return pl.pallas_call(
         experts_second_body,
         in_specs=[pl.BlockSpec(memory_space=pltpu.VMEM)] * 5,
-        out_specs=[pl.BlockSpec(memory_space=pltpu.VMEM)] * 3,
+        out_specs=[pl.BlockSpec(memory_space=pltpu.VMEM)] * 4,
         out_shape=[
             jax.ShapeDtypeStruct((rows, width), bf16),
-            jax.ShapeDtypeStruct((BLOCK, width), f32),
+            jax.ShapeDtypeStruct((BLOCK, width), bf16),
+            jax.ShapeDtypeStruct((BLOCK, width), bf16),
             jax.ShapeDtypeStruct((2, BLOCK, width), bf16),
         ],
         scratch_shapes=[
             pltpu.VMEM((3, BLOCK, width), f32),
             pltpu.VMEM((3, BLOCK, width), f32),
             pltpu.VMEM((2, BLOCK, width), f32),
+            pltpu.VMEM((BLOCK, width), f32),
             pltpu.VMEM((1, BLOCK, width), bf16),
             pltpu.VMEM((1, BLOCK, width), bf16),
             pltpu.SemaphoreType.DMA((4,)),
@@ -437,7 +436,7 @@
 def projection_grads(rows_mine, rows_sent, grad_query, grad_kv, grad_res_low, gains, chosen):
     count = rows_mine.shape[1]
     width = grad_query.shape[1] + grad_kv.shape[1] + grad_res_low.shape[1] + 128
-    tile = 128
+    tile = 256
     whole = lambda i: (0, 0)
     by_column = lambda i: (0, i)
     by_row = lambda i: (i, 0)
@@ -690,7 +689,8 @@
     wide = cut + out_ref.shape[1]
     in_ref[...] = total[:, :cut]
     out_ref[...] = total[:, cut:wide]
-    gain_ref[...] = total[:, wide:]
+    tail = total[:, wide:]
+    gain_ref[...] = tail + pltpu.roll(tail, 126, 1) + pltpu.roll(tail, 124, 1)
     units.wait_send()
     kv_away.wait_send()
     for copy in ring:
@@ -1050,8 +1050,9 @@
 
     hidden, grads, back = experts_first(arrived, grad_arrived, pre_w, down_w)
     grad_back = exchange(back)
-    out_rows, gate_total, rest_low = experts_second(arrived, grad_arrived, hidden, grads, down_w)
-    grad_back, out_rows = lax.optimization_barrier((grad_back, out_rows))
+    out_rows, gate_own, gate_came, rest_low = experts_second(arrived, grad_arrived, hidden, grads, down_w)
+    gate_total = gate_own.astype(f32) + gate_came.astype(f32)
+    grad_back, out_rows, gate_total = lax.optimization_barrier((grad_back, out_rows, gate_total))
     returned = exchange(out_rows)
 
     grad_residual, grad_res_low, grad_query, grad_kv, from_own, gain_parts = block_backward(
@@ -1080,7 +1081,6 @@
         gathered,
         (from_own, grad_residual, own_low, gain_one.astype(f32)[None, :]),
     )
-    gain_total = gain_total[:, :2] + gain_total[:, 2:4] + gain_total[:, 4:6]
 
     chosen = dot(mix, returned, TN).reshape(3, token_count, model_width)
     output = (residual + (chosen[2] + chosen[1] + chosen[0])).astype(bf16)

time: 275 us -> 274 us (level)
  Pallas kernels: 147 us -> 144 us
    unnamed x68 -> x65, local copies, waits for them, and re-layouts: 6.65 us -> 5.66 us
  transfers between devices with their start and end apart: 6 -> 6, of which waited for: 3 -> 3; matrix products, arithmetic and copies ran while one was open for 18% -> 19% of each run, Pallas kernels for 49% -> 48%
where the time goes in v10:
time: 274 us; the launch traced here: 272 us
  Pallas kernels  144 us (53%)
  waiting for transfers between devices  41.7 us (15%)
  other arithmetic  24.9 us (9%)
  starting transfers between devices  24.8 us (9%)
  matrix products  18.2 us (7%)
  local copies, waits for them, and re-layouts  17.5 us (6%)
    pallas_call x1, Pallas kernels, reduce_grads(): pl.pallas_call(reduce_body, in_specs=[away, away, vmem, vmem, away, vmem,...  48.3 us
    all_to_all x4, waiting for transfers between devices, exchange(): lax.all_to_all(blocks, ('seq', 'chip'), split_axis=0, concat_axis=0, axis...  41.7 us
    pallas_call x1, Pallas kernels, gather_weights(): pl.pallas_call(gather_body, out_shape=jax.ShapeDtypeStruct((RING, RING, 2...  34 us
    pallas_call x1, Pallas kernels, experts_second(): pl.pallas_call(experts_second_body, in_specs=[pl.BlockSpec(memory_space=p...  30.7 us
    all_to_all x4, starting transfers between devices, exchange(): lax.all_to_all(blocks, ('seq', 'chip'), split_axis=0, concat_axis=0, axis...  23.2 us
    dot_general x8, matrix products, dot(): return lax.dot_general(a, b, dims, preferred_element_type=f32)  17.3 us
    pallas_call x1, Pallas kernels, block_backward(): pl.pallas_call(block_backward_body, in_specs=[vmem] * 5 + [pl.BlockSpec(m...  12.3 us
    pallas_call x1, Pallas kernels, experts_first(): pl.pallas_call(experts_first_body, grid=(rows // ROW_BLOCK,), in_specs=[p...  11.9 us
  transfers between devices with their start and end apart: 6, of which 3 were waited for; matrix products, arithmetic and copies ran while one was open for 19% of the time, Pallas kernels for 48%

profile of v10, /device:TPU:0, one launch (start us, length us, event | category | flops | bytes accessed | tf_op | source)
XLA Modules:
  0.0 272.1 jit_solution(15594131075049411757)
XLA Ops:
  0.6 1.7 collective-permute-start
  5.7 3.2 %multiply_convert_fusion = bf16[1280,1024]{1,0:T(8,128)(2,1)} fusion(pred[1280,128]{1,0:T(8,128)(4,1)S(1)} %bitcast.128, f32[1280]{0:T(1024)S(1)} %mul.270, bf16[1,128,1024]{2,1,0:T(8,128)(2,1)} %param.23), kind=kOutput, calls=%fused_computation | convolution fusion | flops 338165760 | bytes 3052544 | tf_op jit(solution)/shard_map/dot_general | solution.py:33
  8.9 34.0 %gather_weights.1 = bf16[4,4,2,2,16,3200]{5,4,3,2,1,0:T(8,128)(2,1)} custom-call(bf16[16,2048]{1,0:T(8,128)(2,1)} %in_ref.1, bf16[16,1024]{1,0:T(8,128)(2,1)} %project_ref.1, bf16[16,128]{1,0:T(8,128)(2,1)} %fusion.43.gains_ref), custom_call_target="tpu_custom_call" | custom-call | bytes 52428800 | tf_op jit(solution)/shard_map/gather_weights/pallas_call | solution.py:385
  42.9 6.6 %all-to-all-start = ((bf16[32,40,1024]{2,1,0:T(8,128)(2,1)}), bf16[32,40,1024]{2,1,0:T(8,128)(2,1)}, u32[]{:S(2)}, u32[]{:S(2)}) async-start(bf16[32,40,1024]{2,1,0:T(8,128)(2,1)} %bitcast.27), calls=%async_computation | async-start | bytes 5242880 | tf_op jit(solution)/shard_map/all_to_all | solution.py:937
  51.8 3.0 %fusion.2 = f32[128,2048]{1,0:T(8,128)S(1)} fusion(bf16[128,1024]{1,0:T(8,128)(2,1)S(1)} %get-tuple-element.108, bf16[1024,3200]{1,0:T(8,128)(2,1)} %bitcast.105), kind=kOutput, calls=%fused_computation.4 | convolution fusion | flops 536870912 | bytes 5505024 | tf_op jit(solution)/shard_map/dot_general | solution.py:33
  59.7 2.1 fusion.7
  63.5 2.2 multiply_reduce_fusion
  65.8 2.5 convolution_convert_fusion
  68.3 21.7 %all-to-all-done = bf16[32,40,1024]{2,1,0:T(8,128)(2,1)} async-done(((bf16[32,40,1024]{2,1,0:T(8,128)(2,1)}), bf16[32,40,1024]{2,1,0:T(8,128)(2,1)}, u32[]{:S(2)}, u32[]{:S(2)}) %all-to-all-start) | async-done | bytes 2621472 | tf_op jit(solution)/shard_map/all_to_all | solution.py:937
  90.0 4.9 %all-to-all-start.1 = ((bf16[32,40,1024]{2,1,0:T(8,128)(2,1)}), bf16[32,40,1024]{2,1,0:T(8,128)(2,1)}, u32[]{:S(2)}, u32[]{:S(2)}) async-start(bf16[32,40,1024]{2,1,0:T(8,128)(2,1)} %bitcast.29), calls=%async_computation.1 | async-start | bytes 5242880 | tf_op jit(solution)/shard_map/all_to_all | solution.py:937
  99.7 2.0 negate_select_fusion
  102.7 2.2 fusion.chosen_mine_ref.chosen_sent_ref
  112.9 1.6 pad_maximum_fusion.pre_w_ref
  114.5 18.3 %all-to-all-done.1 = bf16[32,40,1024]{2,1,0:T(8,128)(2,1)} async-done(((bf16[32,40,1024]{2,1,0:T(8,128)(2,1)}), bf16[32,40,1024]{2,1,0:T(8,128)(2,1)}, u32[]{:S(2)}, u32[]{:S(2)}) %all-to-all-start.1) | async-done | bytes 2621472 | tf_op jit(solution)/shard_map/all_to_all | solution.py:937
  132.8 11.9 %experts_first.1 = (bf16[1280,512]{1,0:T(8,128)(2,1)}, bf16[1280,1024]{1,0:T(8,128)(2,1)}, bf16[1280,1024]{1,0:T(8,128)(2,1)}) custom-call(bf16[1280,1024]{1,0:T(8,128)(2,1)} %bitcast.30.x_ref, bf16[1280,1024]{1,0:T(8,128)(2,1)} %bitcast.28.g_ref, bf16[1024,1024]{1,0:T(8,128)(2,1)} %pad_maximum_fusion.pre_w_ref, bf16[512,1024]{1,0:T(8,128)(2,1)} %pad_maximum_fusion.2.down_w_ref), custom_call_target="tpu_custom_call" | custom-call | flops 6710886400 | bytes 13107200 | tf_op jit(solution)/shard_map/experts_first/pallas_call | solution.py:123
  144.7 4.1 %all-to-all-start.2 = ((bf16[32,40,1024]{2,1,0:T(8,128)(2,1)}), bf16[32,40,1024]{2,1,0:T(8,128)(2,1)S(1)}, u32[]{:S(2)}, u32[]{:S(2)}) async-start(bf16[32,40,1024]{2,1,0:T(8,128)(2,1)} %bitcast.119), calls=%async_computation.2 | async-start | bytes 5242880 | tf_op jit(solution)/shard_map/all_to_all | solution.py:937
  148.8 30.7 %experts_second.1 = (bf16[1280,1024]{1,0:T(8,128)(2,1)}, bf16[256,1024]{1,0:T(8,128)(2,1)}, bf16[256,1024]{1,0:T(8,128)(2,1)}, bf16[2,256,1024]{2,1,0:T(8,128)(2,1)}) custom-call(bf16[1280,1024]{1,0:T(8,128)(2,1)} %bitcast.30.x_ref, bf16[1280,1024]{1,0:T(8,128)(2,1)} %bitcast.28.g_ref, bf16[1280,512]{1,0:T(8,128)(2,1)} %get-tuple-element.59.hidden_ref, ...), custom_call_target="tpu_custom_call" | custom-call | flops 5368709120 | bytes 52428800 | tf_op jit(solution)/shard_map/experts_second/pallas_call | solution.py:247
  179.4 2.3 convert_add_fusion
  181.8 1.7 all-to-all-done.2
  185.0 7.6 %all-to-all-start.3 = ((bf16[32,40,1024]{2,1,0:T(8,128)(2,1)}), bf16[32,40,1024]{2,1,0:T(8,128)(2,1)}, u32[]{:S(2)}, u32[]{:S(2)}) async-start(bf16[32,40,1024]{2,1,0:T(8,128)(2,1)} %bitcast.118), calls=%async_computation.3 | async-start | bytes 5242880 | tf_op jit(solution)/shard_map/all_to_all | solution.py:937
  195.6 12.3 %block_backward.1 = (f32[128,1024]{1,0:T(8,128)}, bf16[128,1024]{1,0:T(8,128)(2,1)}, bf16[128,1024]{1,0:T(8,128)(2,1)}, bf16[256,1024]{1,0:T(8,128)(2,1)}, f32[128,1024]{1,0:T(8,128)}, /*index=5*/bf16[8,1024]{1,0:T(8,128)(2,1)}) custom-call(bf16[1280,128]{1,0:T(8,128)(2,1)} %get-tuple-element.114.placed_ref, bf16[1280,1024]{1,0:T(8,128)(2,1)} %bitcast.110, ...), custom_call_target="tpu_custom_call" | custom-call | flops 3000000000 | bytes 12000000 | tf_op jit(solution)/shard_map/block_backward/pallas_call | solution.py:884
  207.9 6.5 %projection_grads.1 = (f32[512,3200]{1,0:T(8,128)}, bf16[512,3200]{1,0:T(8,128)(2,1)}) custom-call(bf16[384,512]{1,0:T(8,128)(2,1)} %get-tuple-element.65.mine_ref, bf16[384,512]{1,0:T(8,128)(2,1)} %get-tuple-element.66.sent_ref, bf16[128,1024]{1,0:T(8,128)(2,1)} %get-tuple-element.78.gq_ref, bf16[256,1024]{1,0:T(8,128)(2,1)} %get-tuple-element.79.gkv_ref.kv_ref, ...), custom_call_target="tpu_custom_call" | custom-call | tf_op jit(solution)/shard_map/projection_grads/pallas_call | solution.py:443
  214.4 48.3 %reduce_grads.1 = (f32[16,2048]{1,0:T(8,128)}, f32[16,1024]{1,0:T(8,128)}, f32[16,128]{1,0:T(8,128)}, f32[256,1024]{1,0:T(8,128)}, f32[256,1024]{1,0:T(8,128)}, /*index=5*/bf16[128,1024]{1,0:T(8,128)(2,1)}) custom-call(f32[4,4,2,16,3200]{4,3,2,1,0:T(8,128)} %bitcast.111, bf16[4,4,2,16,3200]{4,3,2,1,0:T(8,128)(2,1)} %bitcast.117, ...), custom_call_target="tpu_custom_call" | custom-call | flops 13107200 | bytes 98304000 | tf_op jit(solution)/shard_map/reduce_grads/pallas_call | solution.py:714
  264.2 3.0 %fusion.68 = f32[384,1024]{1,0:T(8,128)S(1)} fusion(bf16[1280,384]{1,0:T(8,128)(2,1)S(1)} %copy-done.13, bf16[1280,1024]{1,0:T(8,128)(2,1)} %bitcast.41), kind=kOutput, calls=%fused_computation.154 | convolution fusion | flops 1006632960 | bytes 5177344 | tf_op jit(solution)/shard_map/dot_general | solution.py:33
  (144 shorter events, 36.5 us)
Async XLA Ops:
  0.6 57.9 %collective-permute-start = (bf16[128,1024]{1,0:T(8,128)(2,1)}, bf16[128,1024]{1,0:T(8,128)(2,1)S(1)}, u32[]{:S(2)}, u32[]{:S(2)}) collective-permute-start(bf16[128,1024]{1,0:T(8,128)(2,1)} %bitcast.112), channel_id=1, source_target_pairs={{0,64},{64,0},{1,65},{65,1},{2,66},{66,2},{3,67},{67,3},{4,68},{68... | collective-permute-start | bytes 786440 | tf_op jit(solution)/shard_map/ppermute | solution.py:970
  3.9 39.0 %copy-start.20 = (f32[128,32]{0,1:T(8,128)}, f32[128,32]{0,1:T(8,128)S(1)}, u32[]{:S(2)}) copy-start(f32[128,32]{0,1:T(8,128)S(1)} %select_reduce_fusion.1) | copy-start | bytes 49156
  42.9 6.6 %copy-start.3 = (bf16[1,128,1024]{2,1,0:T(8,128)(2,1)S(1)}, bf16[1,128,1024]{2,1,0:T(8,128)(2,1)}, u32[]{:S(2)}) copy-start(bf16[1,128,1024]{2,1,0:T(8,128)(2,1)} %param.12) | copy-start | bytes 786436
  42.9 47.0 %all-to-all-start = ((bf16[32,40,1024]{2,1,0:T(8,128)(2,1)}), bf16[32,40,1024]{2,1,0:T(8,128)(2,1)}, u32[]{:S(2)}, u32[]{:S(2)}) async-start(bf16[32,40,1024]{2,1,0:T(8,128)(2,1)} %bitcast.27), calls=%async_computation | async-start | bytes 5242880 | tf_op jit(solution)/shard_map/all_to_all | solution.py:937
  50.9 4.0 %copy-start.26 = (f32[1024]{0:T(1024)}, f32[1024]{0:T(1024)S(1)}, u32[]{:S(2)}) copy-start(f32[1024]{0:T(1024)S(1)} %reshape.533) | copy-start | bytes 12292
  55.1 3.5 %copy-start.27 = (f32[1024]{0:T(1024)S(1)}, f32[1024]{0:T(1024)}, u32[]{:S(2)}) copy-start(f32[1024]{0:T(1024)} %copy-done.26) | copy-start | bytes 12292
  63.5 41.4 %copy-start.4 = (bf16[8,64,2,128]{3,1,2,0:T(8,128)(2,1)}, bf16[8,64,2,128]{3,1,2,0:T(8,128)(2,1)S(1)}, u32[]{:S(2)}) copy-start(bf16[8,64,2,128]{3,1,2,0:T(8,128)(2,1)S(1)} %convolution_convert_fusion.1) | copy-start | bytes 786436
  65.8 24.2 %copy-start.1 = (f32[128,1024]{1,0:T(8,128)}, f32[128,1024]{1,0:T(8,128)S(1)}, u32[]{:S(2)}) copy-start(f32[128,1024]{1,0:T(8,128)S(1)} %get-tuple-element.133.residual_ref) | copy-start | bytes 1572868
  90.0 5.0 %copy-start.6 = (bf16[256,1024]{1,0:T(8,128)(2,1)S(1)}, bf16[256,1024]{1,0:T(8,128)(2,1)}, u32[]{:S(2)}) copy-start(bf16[256,1024]{1,0:T(8,128)(2,1)} %param.19) | copy-start | bytes 1572868
  90.0 5.0 %copy-start.7 = (bf16[256,1024]{1,0:T(8,128)(2,1)S(1)}, bf16[256,1024]{1,0:T(8,128)(2,1)}, u32[]{:S(2)}) copy-start(bf16[256,1024]{1,0:T(8,128)(2,1)} %param.18) | copy-start | bytes 1572868
  90.0 5.0 %copy-start.8 = (bf16[256,1024]{1,0:T(8,128)(2,1)S(1)}, bf16[256,1024]{1,0:T(8,128)(2,1)}, u32[]{:S(2)}) copy-start(bf16[256,1024]{1,0:T(8,128)(2,1)} %param.17) | copy-start | bytes 1572868
  90.0 42.8 %all-to-all-start.1 = ((bf16[32,40,1024]{2,1,0:T(8,128)(2,1)}), bf16[32,40,1024]{2,1,0:T(8,128)(2,1)}, u32[]{:S(2)}, u32[]{:S(2)}) async-start(bf16[32,40,1024]{2,1,0:T(8,128)(2,1)} %bitcast.29), calls=%async_computation.1 | async-start | bytes 5242880 | tf_op jit(solution)/shard_map/all_to_all | solution.py:937
  96.3 13.2 %collective-permute-start.1 = (bf16[768,1024]{1,0:T(8,128)(2,1)}, bf16[768,1024]{1,0:T(8,128)(2,1)}, u32[]{:S(2)}, u32[]{:S(2)}) collective-permute-start(bf16[768,1024]{1,0:T(8,128)(2,1)} %pad_maximum_fusion.1), channel_id=1, source_target_pairs={{0,1},{1,0},{2,3},{3,2},{4,5},{5,4},{6,7},{7,6},{8,9},{9,8},{10,11... | collective-permute-start | bytes 4718600 | tf_op jit(solution)/shard_map/ppermute | solution.py:976
  98.9 3.8 %copy-start.28 = (s32[1024]{0:T(1024)S(1)}, s32[1024]{0:T(1024)}, u32[]{:S(2)}) copy-start(s32[1024]{0:T(1024)} %fusion.42) | copy-start | bytes 12292
  101.6 3.5 %copy-start.10 = (bf16[128,8,64]{0,2,1:T(8,128)(2,1)S(1)}, bf16[128,8,64]{0,2,1:T(8,128)(2,1)}, u32[]{:S(2)}) copy-start(bf16[128,8,64]{0,2,1:T(8,128)(2,1)} %copy-done.9) | copy-start | bytes 393220
  101.6 3.6 %copy-start.24 = (f32[2,8,128]{2,1,0:T(8,128)S(1)}, f32[2,8,128]{2,1,0:T(8,128)}, u32[]{:S(2)}) copy-start(f32[2,8,128]{2,1,0:T(8,128)} %copy-done.23) | copy-start | bytes 24580
  102.7 4.0 %copy-start.14 = (bf16[128,512]{1,0:T(8,128)(2,1)S(1)}, bf16[128,512]{1,0:T(8,128)(2,1)}, u32[]{:S(2)}) copy-start(bf16[128,512]{1,0:T(8,128)(2,1)} %copy.67) | copy-start | bytes 393220
  102.7 4.7 %copy-start.17 = (bf16[128,1024]{1,0:T(8,128)(2,1)S(1)}, bf16[128,1024]{1,0:T(8,128)(2,1)}, u32[]{:S(2)}) copy-start(bf16[128,1024]{1,0:T(8,128)(2,1)} %copy-done.16) | copy-start | bytes 786436
  102.7 4.7 %copy-start.19 = (bf16[128,1024]{1,0:T(8,128)(2,1)S(1)}, bf16[128,1024]{1,0:T(8,128)(2,1)}, u32[]{:S(2)}) copy-start(bf16[128,1024]{1,0:T(8,128)(2,1)} %copy-done.18) | copy-start | bytes 786436
  144.7 38.7 %all-to-all-start.2 = ((bf16[32,40,1024]{2,1,0:T(8,128)(2,1)}), bf16[32,40,1024]{2,1,0:T(8,128)(2,1)S(1)}, u32[]{:S(2)}, u32[]{:S(2)}) async-start(bf16[32,40,1024]{2,1,0:T(8,128)(2,1)} %bitcast.119), calls=%async_computation.2 | async-start | bytes 5242880 | tf_op jit(solution)/shard_map/all_to_all | solution.py:937
  183.4 11.3 %copy-start.5 = (bf16[8,64,2,128]{3,1,2,0:T(8,128)(2,1)S(1)}, bf16[8,64,2,128]{3,1,2,0:T(8,128)(2,1)}, u32[]{:S(2)}) copy-start(bf16[8,64,2,128]{3,1,2,0:T(8,128)(2,1)} %copy-done.4) | copy-start | bytes 786436
  185.0 79.3 %all-to-all-start.3 = ((bf16[32,40,1024]{2,1,0:T(8,128)(2,1)}), bf16[32,40,1024]{2,1,0:T(8,128)(2,1)}, u32[]{:S(2)}, u32[]{:S(2)}) async-start(bf16[32,40,1024]{2,1,0:T(8,128)(2,1)} %bitcast.118), calls=%async_computation.3 | async-start | bytes 5242880 | tf_op jit(solution)/shard_map/all_to_all | solution.py:937
  214.4 49.8 %copy-start.13 = (bf16[1280,384]{1,0:T(8,128)(2,1)S(1)}, bf16[1280,384]{1,0:T(8,128)(2,1)}, u32[]{:S(2)}) copy-start(bf16[1280,384]{1,0:T(8,128)(2,1)} %pad_maximum_fusion.3) | copy-start | bytes 2949124
  268.1 3.0 %copy-start.11 = (f32[256,1024]{1,0:T(8,128)S(1)}, f32[256,1024]{1,0:T(8,128)}, u32[]{:S(2)}) copy-start(f32[256,1024]{1,0:T(8,128)} %get-tuple-element.155) | copy-start | bytes 3145732
  (12 other events, 23.0 us)
